TPU v7x, 32 devices: a whole 2x2x4 slice. The times are simulated.
32 devices in a mesh: batch: 8 (over z, y), wide: 4 (over x, core).
Axes of the slice: x: 2, y: 2, z: 4, core: 2. Of those that a mesh axis runs over, the one named last changes fastest.
Arguments:
- tokens: bfloat16 [16384, 768], P(('batch', 'wide')), may hold values from -6 to 6
- block_row: int32 [128], P(('batch', 'wide')), may hold values from 0 to 3, as said below
- block_live: int32 [128], P(('batch', 'wide')), may hold values from 0 to 128, as said below
- query_weight: float32 [768, 768], P(('batch', 'wide')), may hold values from -0.21875 to 0.21875
- key_weight: float32 [768, 768], P(('batch', 'wide')), may hold values from -0.21875 to 0.21875
- value_weight: float32 [768, 768], P(('batch', 'wide')), may hold values from -0.21875 to 0.21875
- out_weight: float32 [768, 768], P(('batch', 'wide')), may hold values from -2.5 to 2.5
- position_bias: float32 [12, 1024], replicated, may hold values from -3 to 3
- features: float32 [64, 64], replicated, may hold values from -5 to 5
- up_weight: float32 [768, 3072], P('batch', 'wide'), may hold values from -0.21875 to 0.21875
- up_bias: float32 [3072], replicated, may hold values from -1.5 to 1.5
- down_weight: float32 [768, 3072], P('batch', 'wide'), may hold values from -0.109375 to 0.109375
- down_bias: float32 [768], replicated, may hold values from -1.5 to 1.5
- gain_one: float32 [768], replicated, may hold values from 0.5 to 1.5
- shift_one: float32 [768], replicated, may hold values from -1 to 1
- gain_two: float32 [768], replicated, may hold values from 0.5 to 1.5
- shift_two: float32 [768], replicated, may hold values from -1 to 1
- cotangent: bfloat16 [16384, 768], P(('batch', 'wide')), may hold values from -6 to 6
Outputs:
- out_tokens: bfloat16 [16384, 768], P(('batch', 'wide'))
- grad_tokens: float32 [16384, 768], P(('batch', 'wide'))
- grad_query_weight: float32 [768, 768], P(('batch', 'wide'))
- grad_key_weight: float32 [768, 768], P(('batch', 'wide'))
- grad_value_weight: float32 [768, 768], P(('batch', 'wide'))
- grad_out_weight: float32 [768, 768], P(('batch', 'wide'))
- grad_position_bias: float32 [12, 1024], replicated
- grad_up_weight: float32 [768, 3072], P('batch', 'wide')
- grad_up_bias: float32 [3072], replicated
- grad_down_weight: float32 [768, 3072], P('batch', 'wide')
- grad_down_bias: float32 [768], replicated
- grad_gain_one: float32 [768], replicated
- grad_shift_one: float32 [768], replicated
- grad_gain_two: float32 [768], replicated
- grad_shift_two: float32 [768], replicated
Inputs may be any that keep to these rules, and one draw needn't show every extreme that they name: `block_row`: in each device's 512 // 128 entries the row numbers start at 0 and rise by one at the first block of each row; a row covers an aligned run of a power of two blocks, from one block to all of a device's blocks. `block_live`: the live tokens of a row are its first ones and more than half of its blocks' slots; a one-block row is full.
All inputs are finite; a program needn't handle non-finite values.
Results may differ from a plain program's by a relative error of at most 0.018.
Values may be sent and summed in bfloat16 or wider, within the bound.
No kernel may reach another device: no remote copies, remote signals or barrier semaphores. Data moves between devices by JAX's collectives and lax.ppermute only.
A program may use at most 192 MiB of HBM per device.

v0:
```python
from functools import partial

import jax
import jax.numpy as jnp
from jax import lax
from jax.sharding import PartitionSpec as P

BLK = 128


eps = 1e-05
highest = lax.Precision.HIGHEST
rows_contract = (((0,), (0,)), ((), ()))
cols_contract = (((1,), (1,)), ((), ()))


def token_masks(block_row, block_live, width):
    blocks = block_row.shape[0]
    offsets = jnp.broadcast_to(jnp.arange(width, dtype=jnp.int32)[None, :], (blocks, width))
    row_ids = jnp.broadcast_to(block_row[:, None], (blocks, width)).reshape(-1)
    live_tok = (offsets < block_live[:, None]).astype(jnp.float32).reshape(-1)
    return (row_ids, live_tok)


def toeplitz_from(vector, length):
    flipped = vector[::-1]
    tiled_flat = jnp.broadcast_to(flipped[None, :], (length, 2 * length)).reshape(-1)
    return tiled_flat[: length * (2 * length - 1)].reshape(length, 2 * length - 1)[:, length - 1 :]


def diagonal_sums(matrix, length):
    padded = jnp.concatenate([jnp.zeros((length, length), jnp.float32), matrix], axis=1).reshape(-1)
    padded = jnp.concatenate([padded, jnp.zeros((length,), jnp.float32)])
    column_sums = jnp.sum(padded.reshape(length, 2 * length + 1), axis=0)
    return column_sums[::-1][: 2 * length]


def feature_map(head_part, features):
    scaled = head_part * head_part.shape[-1] ** (-0.25)
    projected = jnp.einsum("thd,df->thf", scaled, features, precision=highest)
    return jnp.exp(projected - 0.5 * jnp.sum(scaled * scaled, axis=-1, keepdims=True))


def layer_norm(residual, scale_row, shift_row):
    centered = residual - jnp.mean(residual, axis=-1, keepdims=True)
    variance = jnp.mean(centered * centered, axis=-1, keepdims=True)
    return centered * lax.rsqrt(variance + eps) * scale_row + shift_row


def exact_gelu(hidden):
    return jax.nn.gelu(hidden, approximate=False)


def attend_head(same_row, query_phi, key_phi, bias_row):
    length = query_phi.shape[0]
    scores = jnp.einsum("if,jf->ij", query_phi, key_phi, preferred_element_type=jnp.float32)
    coupling = toeplitz_from(jnp.exp(bias_row), length) * same_row
    weights = coupling * scores
    totals = jnp.sum(weights, axis=1, keepdims=True)
    return (weights, totals, coupling)


def mix_head(same_row, head_in):
    query_phi, key_phi, value_head, bias_row = head_in
    weights, totals, coupling = attend_head(same_row, query_phi, key_phi, bias_row)
    prob_low = (weights / totals).astype(jnp.bfloat16)
    return jnp.einsum("ij,jd->id", prob_low, value_head, preferred_element_type=jnp.float32)


def head_backward(same_row, head_in):
    query_phi, key_phi, value_head, bias_row, grad_mix = head_in
    length = query_phi.shape[0]
    weights, totals, coupling = attend_head(same_row, query_phi, key_phi, bias_row)
    shares = weights / totals
    prob_low = shares.astype(jnp.bfloat16)
    grad_probs = jnp.einsum("id,jd->ij", grad_mix, value_head, preferred_element_type=jnp.float32)
    grad_value = jnp.einsum("ij,id->jd", prob_low, grad_mix, preferred_element_type=jnp.float32)
    inner_sum = jnp.sum(grad_probs * shares, axis=1, keepdims=True)
    grad_weights = (grad_probs - inner_sum) / totals
    grad_bias = diagonal_sums(grad_weights * weights, length)
    grad_scores = (grad_weights * coupling).astype(jnp.bfloat16)
    grad_query_phi = jnp.einsum(
        "ij,jf->if", grad_scores, key_phi, preferred_element_type=jnp.float32
    )
    grad_key_phi = jnp.einsum(
        "ij,if->jf", grad_scores, query_phi, preferred_element_type=jnp.float32
    )
    return (grad_query_phi, grad_key_phi, grad_value, grad_bias)


def per_device(
    tokens,
    block_row,
    block_live,
    query_weight,
    key_weight,
    value_weight,
    out_weight,
    position_bias,
    features,
    up_weight,
    up_bias,
    down_weight,
    down_bias,
    gain_one,
    shift_one,
    gain_two,
    shift_two,
    cotangent,
):
    length = tokens.shape[0]
    head_count = position_bias.shape[0]
    head_size = features.shape[0]
    head_shape = (length, head_count, head_size)
    row_ids, live_tok = token_masks(block_row, block_live, BLK)
    same_row = (row_ids[:, None] == row_ids[None, :]).astype(jnp.float32) * live_tok[None, :]
    query_full, key_full, value_full, out_full = (
        lax.all_gather(query_weight.astype(jnp.bfloat16), ("batch", "wide"), axis=0, tiled=True),
        lax.all_gather(key_weight.astype(jnp.bfloat16), ("batch", "wide"), axis=0, tiled=True),
        lax.all_gather(value_weight.astype(jnp.bfloat16), ("batch", "wide"), axis=0, tiled=True),
        lax.all_gather(out_weight.astype(jnp.bfloat16), ("batch", "wide"), axis=0, tiled=True),
    )
    up_rows, down_rows = (
        lax.all_gather(up_weight.astype(jnp.bfloat16), "batch", axis=0, tiled=True),
        lax.all_gather(down_weight.astype(jnp.bfloat16), "batch", axis=0, tiled=True),
    )
    queries = jnp.dot(tokens, query_full, preferred_element_type=jnp.float32)
    key_rows = jnp.dot(tokens, key_full, preferred_element_type=jnp.float32)
    values = jnp.dot(tokens, value_full, preferred_element_type=jnp.float32).astype(jnp.bfloat16)
    map_features = partial(feature_map, features=features)
    query_map, query_back = jax.vjp(map_features, queries.reshape(head_shape))
    key_map, key_back = jax.vjp(map_features, key_rows.reshape(head_shape))
    query_phi = jnp.swapaxes(query_map.astype(jnp.bfloat16), 0, 1)
    key_phi = jnp.swapaxes(key_map.astype(jnp.bfloat16), 0, 1)
    value_heads = jnp.swapaxes(values.reshape(head_shape), 0, 1)
    mixed_heads = lax.map(
        partial(mix_head, same_row), (query_phi, key_phi, value_heads, position_bias)
    )
    mixed_low = jnp.swapaxes(mixed_heads, 0, 1).reshape(length, -1).astype(jnp.bfloat16)
    attention = jnp.dot(mixed_low, out_full, preferred_element_type=jnp.float32)
    residual_one = tokens.astype(jnp.float32) + attention
    normed_one, norm_one_back = jax.vjp(layer_norm, residual_one, gain_one, shift_one)
    normed_low = normed_one.astype(jnp.bfloat16)
    wide_index = lax.axis_index("wide")
    hidden_width = up_rows.shape[1]
    bias_part = lax.dynamic_slice_in_dim(up_bias, wide_index * hidden_width, hidden_width, 0)
    group_rows = lax.all_gather(normed_low, "wide", axis=0, tiled=True)
    hidden = jnp.dot(group_rows, up_rows, preferred_element_type=jnp.float32) + bias_part
    activation_full, gelu_back = jax.vjp(exact_gelu, hidden)
    activation = activation_full.astype(jnp.bfloat16)
    block_rows = activation
    branch = (
        lax.psum_scatter(
            lax.dot_general(
                block_rows, down_rows, cols_contract, preferred_element_type=jnp.float32
            ).astype(jnp.bfloat16),
            "wide",
            scatter_dimension=0,
            tiled=True,
        ).astype(jnp.float32)
        + down_bias
    )
    residual_two = normed_one + branch
    normed_two, norm_two_back = jax.vjp(layer_norm, residual_two, gain_two, shift_two)
    out_tokens = (normed_two * live_tok[:, None]).astype(jnp.bfloat16)
    grad_out = cotangent.astype(jnp.float32) * live_tok[:, None]
    grad_two, grad_gain_two, grad_shift_two = norm_two_back(grad_out)
    grad_branch = grad_two.astype(jnp.bfloat16)
    grad_down_bias = jnp.sum(grad_branch, axis=0, dtype=jnp.float32)
    group_grads = lax.all_gather(grad_branch, "wide", axis=0, tiled=True)
    grad_act = jnp.dot(group_grads, down_rows, preferred_element_type=jnp.float32)
    grad_hidden = gelu_back(grad_act)[0].astype(jnp.bfloat16)
    grad_up_part = lax.dot_general(
        group_rows, grad_hidden, rows_contract, preferred_element_type=jnp.float32
    )
    grad_down_part = lax.dot_general(
        group_grads, activation, rows_contract, preferred_element_type=jnp.float32
    )
    bias_sum = jnp.sum(grad_hidden, axis=0, dtype=jnp.float32)
    bias_grad = lax.dynamic_update_slice_in_dim(
        jnp.zeros(up_bias.shape, jnp.float32), bias_sum, wide_index * hidden_width, 0
    )
    block_rows = grad_hidden
    grad_back = lax.psum_scatter(
        lax.dot_general(
            block_rows, up_rows, cols_contract, preferred_element_type=jnp.float32
        ).astype(jnp.bfloat16),
        "wide",
        scatter_dimension=0,
        tiled=True,
    ).astype(jnp.float32)
    grad_back, grad_up_part, grad_down_part, grad_up_bias = (
        grad_back,
        grad_up_part,
        grad_down_part,
        bias_grad,
    )
    grad_up_weight, grad_down_weight = (
        lax.psum_scatter(
            grad_up_part.astype(jnp.bfloat16), "batch", scatter_dimension=0, tiled=True
        ).astype(jnp.float32),
        lax.psum_scatter(
            grad_down_part.astype(jnp.bfloat16), "batch", scatter_dimension=0, tiled=True
        ).astype(jnp.float32),
    )
    grad_one, grad_gain_one, grad_shift_one = norm_one_back(grad_two + grad_back)
    grad_attention = grad_one.astype(jnp.bfloat16)
    grad_out_local = lax.dot_general(
        mixed_low, grad_attention, rows_contract, preferred_element_type=jnp.float32
    )
    grad_mixed = lax.dot_general(
        grad_attention, out_full, cols_contract, preferred_element_type=jnp.float32
    ).astype(jnp.bfloat16)
    grad_mixed_heads = jnp.swapaxes(grad_mixed.reshape(head_shape), 0, 1)
    grad_query_phi, grad_key_phi, grad_value_heads, grad_bias_local = lax.map(
        partial(head_backward, same_row),
        (query_phi, key_phi, value_heads, position_bias, grad_mixed_heads),
    )
    grad_queries = (
        query_back(jnp.swapaxes(grad_query_phi, 0, 1))[0].reshape(length, -1).astype(jnp.bfloat16)
    )
    grad_keys = (
        key_back(jnp.swapaxes(grad_key_phi, 0, 1))[0].reshape(length, -1).astype(jnp.bfloat16)
    )
    grad_values = jnp.swapaxes(grad_value_heads, 0, 1).reshape(length, -1).astype(jnp.bfloat16)
    grad_query_local = lax.dot_general(
        tokens, grad_queries, rows_contract, preferred_element_type=jnp.float32
    )
    grad_key_local = lax.dot_general(
        tokens, grad_keys, rows_contract, preferred_element_type=jnp.float32
    )
    grad_value_local = lax.dot_general(
        tokens, grad_values, rows_contract, preferred_element_type=jnp.float32
    )
    grad_query_weight, grad_key_weight, grad_value_weight, grad_out_weight = (
        lax.psum_scatter(grad_query_local, ("batch", "wide"), scatter_dimension=0, tiled=True),
        lax.psum_scatter(grad_key_local, ("batch", "wide"), scatter_dimension=0, tiled=True),
        lax.psum_scatter(grad_value_local, ("batch", "wide"), scatter_dimension=0, tiled=True),
        lax.psum_scatter(grad_out_local, ("batch", "wide"), scatter_dimension=0, tiled=True),
    )
    grad_tokens = (
        grad_one
        + lax.dot_general(
            grad_queries, query_full, cols_contract, preferred_element_type=jnp.float32
        )
        + lax.dot_general(grad_keys, key_full, cols_contract, preferred_element_type=jnp.float32)
        + lax.dot_general(
            grad_values, value_full, cols_contract, preferred_element_type=jnp.float32
        )
    )
    (
        grad_up_bias,
        grad_down_bias,
        grad_gain_one,
        grad_shift_one,
        grad_gain_two,
        grad_shift_two,
        grad_position_bias,
    ) = lax.psum(
        (
            grad_up_bias,
            grad_down_bias,
            grad_gain_one,
            grad_shift_one,
            grad_gain_two,
            grad_shift_two,
            grad_bias_local,
        ),
        ("batch", "wide"),
    )
    return (
        out_tokens,
        grad_tokens,
        grad_query_weight,
        grad_key_weight,
        grad_value_weight,
        grad_out_weight,
        grad_position_bias,
        grad_up_weight,
        grad_up_bias,
        grad_down_weight,
        grad_down_bias,
        grad_gain_one,
        grad_shift_one,
        grad_gain_two,
        grad_shift_two,
    )


def solution(mesh):
    placed = (
        P(("batch", "wide"), None),
        P(("batch", "wide")),
        P(("batch", "wide")),
        P(("batch", "wide"), None),
        P(("batch", "wide"), None),
        P(("batch", "wide"), None),
        P(("batch", "wide"), None),
        P(),
        P(),
        P("batch", "wide"),
        P(),
        P("batch", "wide"),
        P(),
        P(),
        P(),
        P(),
        P(),
        P(("batch", "wide"), None),
    )
    return jax.shard_map(
        per_device,
        mesh=mesh,
        in_specs=placed,
        out_specs=(
            P(("batch", "wide"), None),
            P(("batch", "wide"), None),
            P(("batch", "wide"), None),
            P(("batch", "wide"), None),
            P(("batch", "wide"), None),
            P(("batch", "wide"), None),
            P(),
            P("batch", "wide"),
            P(),
            P("batch", "wide"),
            P(),
            P(),
            P(),
            P(),
            P(),
        ),
        check_vma=False,
    )
```

profile of v0, /device:TPU:0, one launch (start us, length us, event | category | flops | bytes accessed | tf_op | source)
XLA Modules:
  0.0 1346.5 jit_solution(8290527931595110936)
XLA Ops:
  16.6 51.7 %all-gather.11.cloned.1.call-done = bf16[768,768]{1,0:T(8,128)(2,1)} async-done(((bf16[24,768]{1,0:T(8,128)(2,1)}), bf16[768,768]{1,0:T(8,128)(2,1)}) %all-gather.11.cloned.1.call-update) | async-done | bytes 1179664 | tf_op jit(solution)/shard_map/all_gather | solution.py:119
  80.4 44.4 %all-gather.9.cloned.1.call-done = bf16[768,768]{1,0:T(8,128)(2,1)} async-done(((bf16[24,768]{1,0:T(8,128)(2,1)}), bf16[768,768]{1,0:T(8,128)(2,1)}) %all-gather.9.cloned.1.call-update) | async-done | bytes 1179664 | tf_op jit(solution)/shard_map/all_gather | solution.py:118
  124.7 3.8 broadcast_multiply_fusion.1
  137.0 44.3 %all-gather.13.cloned.1.call-done = bf16[768,768]{1,0:T(8,128)(2,1)} async-done(((bf16[24,768]{1,0:T(8,128)(2,1)}), bf16[768,768]{1,0:T(8,128)(2,1)}) %all-gather.13.cloned.1.call-update) | async-done | bytes 1179664 | tf_op jit(solution)/shard_map/all_gather | solution.py:120
  185.1 113.5 %while.30 = (s32[]{:T(128)}, bf16[12,512,64]{1,2,0:T(8,128)(2,1)}, f32[12,1024]{1,0:T(8,128)}, bf16[12,512,64]{2,1,0:T(8,128)(2,1)}, bf16[12,512,64]{2,1,0:T(8,1...) while((s32[]{:T(128)}, bf16[12,512,64]{1,2,0:T(8,128)(2,1)}, ...), condition=%wide.region_4.5_spmd.clone.clone, body=%wide.region_2.4_spmd.clone.sunk.clone | while | flops 68943360 | bytes 18378840 | solution.py:136
  305.0 25.6 %all-gather.17.cloned.1.call-done = bf16[2048,768]{1,0:T(8,128)(2,1)} async-done(((bf16[512,768]{1,0:T(8,128)(2,1)}), bf16[2048,768]{1,0:T(8,128)(2,1)}) %all-gather.17.cloned.1.call-update) | async-done | bytes 3145744 | tf_op jit(solution)/shard_map/all_gather | solution.py:147
  330.6 18.9 %multiply_convert_fusion.1 = (bf16[2048,768]{1,0:T(8,128)(2,1)}, f32[2048,768]{1,0:T(8,128)}, f32[2048,768]{1,0:T(8,128)}) fusion(f32[768]{0:T(1024)S(1)} %dynamic_slice.32, bf16[2048,768]{1,0:T(8,128)(2,1)} %all-gather.17.cloned.1.call-done, bf16[768,768]{1,0:T(8,128)(2,1)} %all-gather.19.cloned.1.call-done), kind=kOutput, calls=%fused_computation.59 | convolution fusion | flops 2519728128 | bytes 20057088 | tf_op jit(solution)/shard_map/dot_general | solution.py:148
  349.5 25.0 %all-gather.21.cloned.1.call-done = bf16[768,768]{1,0:T(8,128)(2,1)} async-done(((bf16[96,768]{1,0:T(8,128)(2,1)}), bf16[768,768]{1,0:T(8,128)(2,1)}) %all-gather.21.cloned.1.call-update) | async-done | bytes 1179664 | tf_op jit(solution)/shard_map/all_gather | solution.py:125
  374.4 6.5 convolution_convert_fusion.1
  381.1 36.8 %reduce-scatter.15.cloned.1.call-done = bf16[512,768]{1,0:T(8,128)(2,1)} async-done(((bf16[2048,768]{1,0:T(8,128)(2,1)}), bf16[512,768]{1,0:T(8,128)(2,1)}) %reduce-scatter.15.cloned.1.call-update) | async-done | bytes 786448 | tf_op jit(solution)/shard_map/reduce_scatter | solution.py:153
  425.7 28.5 %all-gather.23.cloned.1.call-done = bf16[2048,768]{1,0:T(8,128)(2,1)} async-done(((bf16[512,768]{1,0:T(8,128)(2,1)}), bf16[2048,768]{1,0:T(8,128)(2,1)}) %all-gather.23.cloned.1.call-update) | async-done | bytes 3145744 | tf_op jit(solution)/shard_map/all_gather | solution.py:170
  454.2 10.6 convert_reduce_fusion
  466.4 4.0 convolution_convert_fusion
  470.5 6.5 convolution_convert_fusion.2
  477.5 7.4 convolution_convert_fusion.3
  485.1 23.4 %reduce-scatter.17.cloned.1.call-done = bf16[512,768]{1,0:T(8,128)(2,1)} async-done(((bf16[2048,768]{1,0:T(8,128)(2,1)}), bf16[512,768]{1,0:T(8,128)(2,1)}) %reduce-scatter.17.cloned.1.call-update) | async-done | bytes 786448 | tf_op jit(solution)/shard_map/reduce_scatter | solution.py:184
  515.3 272.2 %while.31 = (s32[]{:T(128)}, f32[12,512,64]{1,2,0:T(8,128)}, f32[12,512,64]{1,2,0:T(8,128)}, bf16[12,512,64]{1,2,0:T(8,128)(2,1)}, f32[12,1024]{1,0:T(8,128)}, /...) while((s32[]{:T(128)}, f32[12,512,64]{1,2,0:T(8,128)}, ...), condition=%wide.region_19.20_spmd.clone.clone, body=%wide.region_15.0_spmd.clone.sunk.clone | while | flops 173013504 | bytes 51068068 | solution.py:215
  787.6 4.0 fusion.68
  810.2 3.9 fusion.50
  833.1 78.5 %all-reduce.5.cloned.1.call-done = (f32[12,1024]{1,0:T(8,128)}, f32[3072]{0:T(1024)}, f32[768]{0:T(1024)}, f32[768]{0:T(1024)}, f32[768]{0:T(1024)}, /*index=5*/f32[768]{0:T(1024)}, f32[768]{0:T(1024)}) async-done(((f32[12,1024]{1,0:T(8,128)}, f32[3072]{0:T(1024)}, f32[768]{0:T(1024)}, f32[768]{0:T(1024)}, f32[768]{0:T(1024)}, /*index=5*/f32[768]{0:T(1024)}, f32[768]{0:T(1024)}), (f32[12,1024]{1,0:T(8,128)}, ...) | async-done | bytes 76816 | tf_op jit(solution)/shard_map/psum | solution.py:259
  911.6 105.9 %reduce-scatter.19.cloned.1.call-done = f32[24,768]{1,0:T(8,128)} async-done(((f32[768,768]{1,0:T(8,128)}), f32[24,768]{1,0:T(8,128)}) %reduce-scatter.19.cloned.1.call-update) | async-done | bytes 73744 | tf_op jit(solution)/shard_map/reduce_scatter | solution.py:239
  1017.5 104.5 %reduce-scatter.25.cloned.1.call-done = f32[24,768]{1,0:T(8,128)} async-done(((f32[768,768]{1,0:T(8,128)}), f32[24,768]{1,0:T(8,128)}) %reduce-scatter.25.cloned.1.call-update) | async-done | bytes 73744
  1122.0 103.8 %reduce-scatter.27.cloned.1.call-done = f32[24,768]{1,0:T(8,128)} async-done(((f32[768,768]{1,0:T(8,128)}), f32[24,768]{1,0:T(8,128)}) %reduce-scatter.27.cloned.1.call-update) | async-done | bytes 73744
  1225.9 104.5 %reduce-scatter.29.cloned.1.call-done = f32[24,768]{1,0:T(8,128)} async-done(((f32[768,768]{1,0:T(8,128)}), f32[24,768]{1,0:T(8,128)}) %reduce-scatter.29.cloned.1.call-update) | async-done | bytes 73744
  (576 shorter events, 487.6 us)
Async XLA Ops:
  7.2 67.6 %copy-start = (f32[64,64]{1,0:T(8,128)S(1)}, f32[64,64]{1,0:T(8,128)}, u32[]{:S(2)}) copy-start(f32[64,64]{1,0:T(8,128)} %param.30) | copy-start | bytes 49156
  7.2 8.2 copy-start.30
  7.2 61.1 %all-gather.11.cloned.1.call-start = ((), (), s32[]{:S(2)}) async-start(), calls=%async_computation.9 | async-start | bytes 1216512 | tf_op jit(solution)/shard_map/all_gather | solution.py:119
  8.8 116.0 %all-gather.9.cloned.1.call-start = ((), (), s32[]{:S(2)}) async-start(), calls=%async_computation.8 | async-start | bytes 1216512 | tf_op jit(solution)/shard_map/all_gather | solution.py:118
  10.4 170.9 %all-gather.13.cloned.1.call-start = ((), (), s32[]{:S(2)}) async-start(), calls=%async_computation.10 | async-start | bytes 1216512 | tf_op jit(solution)/shard_map/all_gather | solution.py:120
  11.9 56.4 %copy-start.2 = (bf16[512,768]{1,0:T(8,128)(2,1)S(1)}, bf16[512,768]{1,0:T(8,128)(2,1)}, u32[]{:S(2)}) copy-start(bf16[512,768]{1,0:T(8,128)(2,1)} %param.22) | copy-start | bytes 2359300
  12.0 286.6 %all-gather.15.cloned.1.call-start = ((), (), s32[]{:S(2)}) async-start(), calls=%async_computation.11 | async-start | bytes 1216512 | tf_op jit(solution)/shard_map/all_gather | solution.py:121
  13.6 291.4 %all-gather.19.cloned.1.call-start = ((), (), s32[]{:S(2)}) async-start(), calls=%async_computation.13 | async-start | bytes 1327104 | tf_op jit(solution)/shard_map/all_gather | solution.py:124
  15.3 315.3 %all-gather.17.cloned.1.call-start = ((), (), s32[]{:S(2)}) async-start(), calls=%async_computation.12 | async-start | bytes 3932160 | tf_op jit(solution)/shard_map/all_gather | solution.py:147
  15.4 56.6 %copy-start.8 = (bf16[12,512,64]{1,2,0:T(8,128)(2,1)}, bf16[12,512,64]{1,2,0:T(8,128)(2,1)S(1)}, u32[]{:S(2)}) copy-start(bf16[12,512,64]{1,2,0:T(8,128)(2,1)S(1)} %fusion.76) | copy-start | bytes 2359300
  302.9 71.5 %all-gather.21.cloned.1.call-start = ((), (), s32[]{:S(2)}) async-start(), calls=%async_computation.14 | async-start | bytes 1327104 | tf_op jit(solution)/shard_map/all_gather | solution.py:125
  303.7 114.2 %reduce-scatter.15.cloned.1.call-start = ((), (), s32[]{:S(2)}) async-start(), calls=%async_computation.15 | async-start | bytes 3932160 | tf_op jit(solution)/shard_map/reduce_scatter | solution.py:153
  381.0 36.9 %copy-start.28 = (f32[768]{0:T(1024)S(1)}, f32[768]{0:T(1024)}, u32[]{:S(2)}) copy-start(f32[768]{0:T(1024)} %param.34) | copy-start | bytes 9220
  381.0 73.2 %all-gather.23.cloned.1.call-start = ((), (), s32[]{:S(2)}) async-start(), calls=%async_computation.16 | async-start | bytes 3932160 | tf_op jit(solution)/shard_map/all_gather | solution.py:170
  425.5 83.1 %reduce-scatter.17.cloned.1.call-start = ((), (), s32[]{:S(2)}) async-start(), calls=%async_computation.17 | async-start | bytes 3932160 | tf_op jit(solution)/shard_map/reduce_scatter | solution.py:184
  454.2 12.3 copy-start.33
  470.5 353.7 %reduce-scatter.23.cloned.1.call-start = ((), (), s32[]{:S(2)}) async-start(), calls=%async_computation.20 | async-start | bytes 1327104 | tf_op jit(solution)/shard_map/reduce_scatter | solution.py:202
  477.1 348.9 %reduce-scatter.21.cloned.1.call-start = ((), (), s32[]{:S(2)}) async-start(), calls=%async_computation.19 | async-start | bytes 1327104 | tf_op jit(solution)/shard_map/reduce_scatter | solution.py:199
  477.5 7.4 copy-start.25
  484.9 426.7 %all-reduce.5.cloned.1.call-start = ((), (), s32[]{:S(2)}) async-start(), calls=%async_computation.24 | async-start | bytes 196608 | tf_op jit(solution)/shard_map/psum | solution.py:259
  787.5 230.0 %reduce-scatter.19.cloned.1.call-start = ((), (), s32[]{:S(2)}) async-start(), calls=%async_computation.18 | async-start | bytes 2433024 | tf_op jit(solution)/shard_map/reduce_scatter | solution.py:239
  791.6 330.5 %reduce-scatter.25.cloned.1.call-start = ((), (), s32[]{:S(2)}) async-start(), calls=%async_computation.21 | async-start | bytes 2433024
  807.1 418.8 %reduce-scatter.27.cloned.1.call-start = ((), (), s32[]{:S(2)}) async-start(), calls=%async_computation.22 | async-start | bytes 2433024
  817.7 512.6 %reduce-scatter.29.cloned.1.call-start = ((), (), s32[]{:S(2)}) async-start(), calls=%async_computation.23 | async-start | bytes 2433024
  (39 other events, 75.6 us)
Sparse Core Ops, SparseCore 0:
  11.5 56.7 all-gather.10
  71.7 52.9 all-gather.8
  128.2 52.9 all-gather.12
  184.6 52.9 all-gather.14
  240.2 39.9 all-gather.18
  303.0 27.5 all-gather.16
  333.3 41.0 all-gather.20
  381.1 36.7 reduce-scatter.14
  425.6 28.5 all-gather.22
  470.6 37.9 reduce-scatter.16
  512.0 64.1 reduce-scatter.22
  579.4 63.1 reduce-scatter.20
  787.6 123.9 all-reduce.4
  917.3 100.1 reduce-scatter.18
  1024.1 97.9 reduce-scatter.24
  1127.7 98.0 reduce-scatter.26
  1232.4 97.9 reduce-scatter.28
where the time goes:
time: 1360 us; the launch traced here: 1350 us
  waiting for transfers between devices  777 us (57%)
  local copies, waits for them, and re-layouts  285 us (21%)
  matrix products  231 us (17%)
  other arithmetic  34.5 us (3%)
  between operations  14.9 us (1%)
    unnamed x20, waiting for transfers between devices  313 us
    reduce_scatter x1, waiting for transfers between devices, per_device(): lax.psum_scatter(grad_out_local, ('batch', 'wide'), scatter_dimension=0,...  106 us
    psum x1, waiting for transfers between devices, per_device(): lax.psum((grad_up_bias, grad_down_bias, grad_gain_one, grad_shift_one, gr...  78.5 us
    reshape x24, local copies, waits for them, and re-layouts, toeplitz_from(): tiled_flat[:length * (2 * length - 1)].reshape(length, 2 * length - 1)  66.9 us
    all_gather x1, waiting for transfers between devices, per_device(): lax.all_gather(key_weight.astype(jnp.bfloat16), ('batch', 'wide'), axis=0...  51.7 us
    all_gather x1, waiting for transfers between devices, per_device(): lax.all_gather(query_weight.astype(jnp.bfloat16), ('batch', 'wide'), axis...  44.4 us
    all_gather x1, waiting for transfers between devices, per_device(): lax.all_gather(value_weight.astype(jnp.bfloat16), ('batch', 'wide'), axis...  44.3 us
    slice x24, local copies, waits for them, and re-layouts, toeplitz_from(): tiled_flat[:length * (2 * length - 1)].reshape(length, 2 * length - 1)  39.7 us
  transfers between devices with their start and end apart: 17, of which 13 were waited for; matrix products, arithmetic and copies ran while one was open for 37% of the time, Pallas kernels for 0%

commit v1 on v0

v1 whole, which is shorter than its diff:
```python
from functools import partial

import jax
import jax.numpy as jnp
from jax import lax
from jax.experimental import pallas as pl
from jax.experimental.pallas import tpu as pltpu
from jax.sharding import PartitionSpec as P

BLK = 128
f32 = jnp.float32
bf16 = jnp.bfloat16
nt_dims = (((1,), (1,)), ((), ()))


def dot(a, b):
    return jnp.dot(a, b, preferred_element_type=f32)


def dot_nt(a, b):
    return lax.dot_general(a, b, nt_dims, preferred_element_type=f32)


def split_low(x):
    high = x.astype(bf16)
    return high, (x - high.astype(f32)).astype(bf16)


def toeplitz_kernel(bias_ref, out_ref):
    heads = bias_ref.shape[0]
    rels = bias_ref.shape[1]
    for h in range(heads):
        row = jnp.broadcast_to(jnp.exp(bias_ref[h : h + 1, :]), (BLK, rels))
        out_ref[h] = pltpu.roll(row, rels - BLK + 1, 1, stride=1, stride_axis=0)


def toeplitz_tables(flipped_bias):
    heads, rels = flipped_bias.shape
    step = 2
    return pl.pallas_call(
        toeplitz_kernel,
        grid=(heads // step,),
        in_specs=[pl.BlockSpec((None, step, rels), lambda h: (h, 0, 0))],
        out_specs=pl.BlockSpec((step, BLK, rels), lambda h: (h, 0, 0)),
        out_shape=jax.ShapeDtypeStruct((heads, BLK, rels), f32),
        name="toeplitz",
    )(flipped_bias.reshape(heads // step, step, rels))


def pair_features(u, feat_ref):
    high, low = split_low(u)
    projected = dot(jnp.concatenate([high, high, low], axis=1), feat_ref[...])
    size = u.shape[1] // 2
    square = u * u
    norm_a = jnp.sum(square[:, :size], axis=1, keepdims=True)
    norm_b = jnp.sum(square[:, size:], axis=1, keepdims=True)
    lane = lax.broadcasted_iota(jnp.int32, u.shape, 1)
    norm = jnp.where(lane < size, norm_a, norm_b)
    return jnp.exp(projected - 0.5 * norm)


def attend_kernel(
    scale, tok_ref, w_ref, table_ref, mask_ref, feat_ref, mixed_ref, u_ref, phi_ref, val_ref
):
    length = tok_ref.shape[0]
    pair = mixed_ref.shape[1]
    size = pair // 2
    blocks = length // BLK
    qkv = dot(tok_ref[...], w_ref[...])
    uq = qkv[:, :pair] * scale
    uk = qkv[:, pair : 2 * pair] * scale
    value = qkv[:, 2 * pair :].astype(bf16)
    pq = pair_features(uq, feat_ref)
    pk = pair_features(uk, feat_ref)
    u_ref[:, :pair] = uq
    u_ref[:, pair:] = uk
    phi_ref[:, :pair] = pq
    phi_ref[:, pair:] = pk
    val_ref[...] = value
    pq = pq.astype(bf16)
    pk = pk.astype(bf16)
    for h in range(2):
        cols = slice(h * size, (h + 1) * size)
        key = pk[:, cols]
        val = value[:, cols]
        for b in range(blocks):
            rows = slice(b * BLK, (b + 1) * BLK)
            start = (blocks - 1 - b) * BLK
            scores = dot_nt(pq[rows, cols], key)
            weights = table_ref[h, :, start : start + length] * mask_ref[b : b + 1, :] * scores
            total = jnp.sum(weights, axis=1, keepdims=True)
            probs = (weights * (1.0 / total)).astype(bf16)
            mixed_ref[rows, cols] = dot(probs, val).astype(bf16)


def attend(tokens, weights, tables, mask, feat_split, heads):
    length, width = tokens.shape
    pair = 2 * width // heads
    pairs = heads // 2
    rels = tables.shape[2]
    scale = float((pair // 2) ** (-0.25))
    whole = lambda shape: pl.BlockSpec(shape, lambda h: (0,) * len(shape))
    column = lambda cols: pl.BlockSpec((length, cols), lambda h: (0, h))
    return pl.pallas_call(
        partial(attend_kernel, scale),
        grid=(pairs,),
        in_specs=[
            whole((length, width)),
            pl.BlockSpec((width, 3 * pair), lambda h: (0, h)),
            pl.BlockSpec((2, BLK, rels), lambda h: (h, 0, 0)),
            whole(mask.shape),
            whole(feat_split.shape),
        ],
        out_specs=[column(pair), column(2 * pair), column(2 * pair), column(pair)],
        out_shape=[
            jax.ShapeDtypeStruct((length, width), bf16),
            jax.ShapeDtypeStruct((length, 2 * width), f32),
            jax.ShapeDtypeStruct((length, 2 * width), f32),
            jax.ShapeDtypeStruct((length, width), bf16),
        ],
        name="attend",
    )(tokens, weights, tables, mask, feat_split)


def pair_backward(scale, grad_phi, phi, u, feat_ref):
    gp = grad_phi * phi
    high, low = split_low(gp)
    back = dot(jnp.concatenate([high, high, low], axis=1), feat_ref[...])
    size = u.shape[1] // 2
    sum_a = jnp.sum(gp[:, :size], axis=1, keepdims=True)
    sum_b = jnp.sum(gp[:, size:], axis=1, keepdims=True)
    lane = lax.broadcasted_iota(jnp.int32, u.shape, 1)
    return (scale * (back - u * jnp.where(lane < size, sum_a, sum_b))).astype(bf16)


def attend_back_kernel(
    scale,
    tok_t_ref,
    w_ref,
    table_ref,
    mask_ref,
    feat_ref,
    u_ref,
    phi_ref,
    val_ref,
    ga_ref,
    wo_ref,
    grad_one_ref,
    dw_ref,
    dbias_ref,
    gtok_ref,
    diag_ref,
):
    length, pair = val_ref.shape
    size = pair // 2
    blocks = length // BLK
    rels = table_ref.shape[2]

    @pl.when(pl.program_id(0) == 0)
    def _():
        gtok_ref[...] = grad_one_ref[...]

    gm = dot_nt(ga_ref[...], wo_ref[...]).astype(bf16)
    gm_t = gm.astype(f32).T.astype(bf16)
    phi = phi_ref[...]
    pq32, pk32 = phi[:, :pair], phi[:, pair:]
    pq = pq32.astype(bf16)
    pk = pk32.astype(bf16)
    pq_t = pq32.T.astype(bf16)
    value = val_ref[...]
    gq_heads = []
    gk_heads = []
    gv_heads = []
    for h in range(2):
        cols = slice(h * size, (h + 1) * size)
        key = pk[:, cols]
        val = value[:, cols]
        diag_ref[...] = jnp.zeros_like(diag_ref)
        gq_rows = []
        gk_t = None
        gv_t = None
        for b in range(blocks):
            rows = slice(b * BLK, (b + 1) * BLK)
            start = (blocks - 1 - b) * BLK
            window = slice(start, start + length)
            scores = dot_nt(pq[rows, cols], key)
            coupling = table_ref[h, :, window] * mask_ref[b : b + 1, :]
            weights = coupling * scores
            inverse = 1.0 / jnp.sum(weights, axis=1, keepdims=True)
            shares = weights * inverse
            grad_probs = dot_nt(gm[rows, cols], val)
            inner = jnp.sum(grad_probs * shares, axis=1, keepdims=True)
            grad_weights = (grad_probs - inner) * inverse
            diag_ref[:, window] += grad_weights * weights
            grad_scores = (grad_weights * coupling).astype(bf16)
            probs = shares.astype(bf16)
            gq_rows.append(dot(grad_scores, key))
            gk_part = dot(pq_t[cols, rows], grad_scores)
            gv_part = dot(gm_t[cols, rows], probs)
            gk_t = gk_part if gk_t is None else gk_t + gk_part
            gv_t = gv_part if gv_t is None else gv_t + gv_part
        gq_heads.append(jnp.concatenate(gq_rows, axis=0))
        gk_heads.append(gk_t)
        gv_heads.append(gv_t)
        folded = diag_ref[...]
        half = BLK // 2
        while half >= 1:
            folded = pltpu.roll(folded[:half], half, 1) + folded[half:]
            half //= 2
        dbias_ref[h : h + 1, :] = folded
    gq = jnp.concatenate(gq_heads, axis=1)
    gk = jnp.concatenate(gk_heads, axis=0).T
    gv = jnp.concatenate(gv_heads, axis=0).T.astype(bf16)
    u = u_ref[...]
    dq = pair_backward(scale, gq, pq32, u[:, :pair], feat_ref)
    dk = pair_backward(scale, gk, pk32, u[:, pair:], feat_ref)
    dqkv = jnp.concatenate([dq, dk, gv], axis=1)
    dw_ref[...] = dot(tok_t_ref[...], dqkv).astype(dw_ref.dtype)
    gtok_ref[...] += dot_nt(dqkv, w_ref[...])


def attend_back(
    tokens_t, weights, tables, mask, feat_back, u, phi, value, grad_attention, grad_one, heads
):
    width, length = tokens_t.shape
    pair = 2 * width // heads
    pairs = heads // 2
    rels = tables.shape[2]
    scale = float((pair // 2) ** (-0.25))
    whole = lambda shape: pl.BlockSpec(shape, lambda h: (0,) * len(shape))
    column = lambda rows, cols: pl.BlockSpec((rows, cols), lambda h: (0, h))
    dw, dbias, gtok = pl.pallas_call(
        partial(attend_back_kernel, scale),
        grid=(pairs,),
        in_specs=[
            whole((width, length)),
            column(width, 3 * pair),
            pl.BlockSpec((2, BLK, rels), lambda h: (h, 0, 0)),
            whole(mask.shape),
            whole(feat_back.shape),
            column(length, 2 * pair),
            column(length, 2 * pair),
            column(length, pair),
            whole((length, width)),
            pl.BlockSpec((pair, width), lambda h: (h, weights.shape[1] // width - 1)),
            whole((length, width)),
        ],
        out_specs=[
            column(width, 3 * pair),
            pl.BlockSpec((None, 2, rels), lambda h: (h, 0, 0)),
            whole((length, width)),
        ],
        out_shape=[
            jax.ShapeDtypeStruct((width, 3 * width), bf16),
            jax.ShapeDtypeStruct((pairs, 2, rels), f32),
            jax.ShapeDtypeStruct((length, width), f32),
        ],
        scratch_shapes=[pltpu.VMEM((BLK, rels), f32)],
        name="attend_back",
    )(
        tokens_t, weights, tables, mask, feat_back, u, phi, value, grad_attention, weights, grad_one
    )
    return dw, dbias.reshape(heads, rels), gtok


def block_diagonal(matrix):
    zero = jnp.zeros_like(matrix)
    return jnp.concatenate(
        [jnp.concatenate([matrix, zero], axis=1), jnp.concatenate([zero, matrix], axis=1)], axis=0
    )


def split_rows(matrix):
    high, low = split_low(matrix)
    return jnp.concatenate([high, low, high], axis=0)


root_half = 0.7071067811865476
inv_root_two_pi = 0.3989422804014327
eps = 1e-05


def norm_stats(residual):
    centered = residual - jnp.mean(residual, axis=1, keepdims=True)
    inverse = lax.rsqrt(jnp.mean(centered * centered, axis=1, keepdims=True) + eps)
    return centered * inverse, inverse


def norm_back(grad, xhat, inverse, gain):
    scaled = grad * gain
    mean_grad = jnp.mean(scaled, axis=1, keepdims=True)
    mean_dot = jnp.mean(scaled * xhat, axis=1, keepdims=True)
    return (scaled - mean_grad - xhat * mean_dot) * inverse


def column_sum(x):
    return jnp.sum(x, axis=0, keepdims=True)


def ffn_kernel(
    rows_up,
    tok_ref,
    mixed_ref,
    wo_ref,
    w_ref,
    up_bias_ref,
    vec_ref,
    live_ref,
    cot_ref,
    out_ref,
    grad_one_ref,
    grad_att_ref,
    dw_ref,
    dup_bias_ref,
    dvec_ref,
    normed_ref,
    low_ref,
    low_t_ref,
    xhat_ref,
    inv_ref,
    act_ref,
    slope_ref,
    acc_ref,
    grad_two_ref,
    gb_ref,
    gb_t_ref,
):
    phase = pl.program_id(0)
    part = pl.program_id(1)
    parts = pl.num_programs(1)
    length, width = tok_ref.shape
    hidden = w_ref.shape[2]
    chunk = 256 if hidden % 256 == 0 else hidden
    chunks = [slice(k, k + chunk) for k in range(0, hidden, chunk)]
    vec = vec_ref[...]
    down_bias, gain_one, shift_one, gain_two, shift_two = (vec[i : i + 1] for i in range(5))

    @pl.when((phase == 0) & (part == 0))
    def _():
        residual = tok_ref[...].astype(f32) + dot(mixed_ref[...], wo_ref[...])
        xhat, inverse = norm_stats(residual)
        normed = xhat * gain_one + shift_one
        xhat_ref[...] = xhat
        inv_ref[...] = inverse
        normed_ref[...] = normed
        low_ref[...] = normed.astype(bf16)
        low_t_ref[...] = normed.T.astype(bf16)
        acc_ref[...] = jnp.zeros_like(acc_ref)

    @pl.when(phase == 0)
    def _():
        for cols in chunks:
            up = w_ref[:, :rows_up, cols].reshape(width, chunk)
            down = w_ref[:, rows_up:, cols].reshape(width, chunk)
            v = dot(low_ref[...], up) + up_bias_ref[:, cols]
            half = 0.5 + 0.5 * lax.erf(v * root_half)
            act = (v * half).astype(bf16)
            act_ref[part, :, cols] = act
            slope_ref[part, :, cols] = half + v * (jnp.exp(-0.5 * v * v) * inv_root_two_pi)
            acc_ref[...] += dot_nt(act, down)

    @pl.when((phase == 0) & (part == parts - 1))
    def _():
        live = live_ref[...]
        xhat, inverse = norm_stats(normed_ref[...] + (acc_ref[...] + down_bias))
        out_ref[...] = ((xhat * gain_two + shift_two) * live).astype(bf16)
        grad = cot_ref[...].astype(f32) * live
        grad_two = norm_back(grad, xhat, inverse, gain_two)
        low = grad_two.astype(bf16)
        grad_two_ref[...] = grad_two
        gb_ref[...] = low
        gb_t_ref[...] = grad_two.T.astype(bf16)
        dvec_ref[0:1, :] = column_sum(low.astype(f32))
        dvec_ref[3:4, :] = column_sum(grad * xhat)
        dvec_ref[4:5, :] = column_sum(grad)
        acc_ref[...] = grad_two

    @pl.when(phase == 1)
    def _():
        for cols in chunks:
            up = w_ref[:, :rows_up, cols].reshape(width, chunk)
            down = w_ref[:, rows_up:, cols].reshape(width, chunk)
            grad_act = dot(gb_ref[...], down)
            grad_hidden = (grad_act * slope_ref[part, :, cols]).astype(bf16)
            dup_bias_ref[:, cols] = column_sum(grad_hidden.astype(f32))
            d_up = dot(low_t_ref[...], grad_hidden).astype(bf16)
            d_down = dot(gb_t_ref[...], act_ref[part, :, cols]).astype(bf16)
            dw_ref[:, :rows_up, cols] = d_up.reshape(-1, rows_up, chunk)
            dw_ref[:, rows_up:, cols] = d_down.reshape(-1, rows_up, chunk)
            acc_ref[...] += dot_nt(grad_hidden, up)

    @pl.when((phase == 1) & (part == parts - 1))
    def _():
        grad = acc_ref[...]
        xhat = xhat_ref[...]
        grad_one = norm_back(grad, xhat, inv_ref[...], gain_one)
        grad_one_ref[...] = grad_one
        grad_att_ref[...] = grad_one.astype(bf16)
        dvec_ref[1:2, :] = column_sum(grad * xhat)
        dvec_ref[2:3, :] = column_sum(grad)


def feed_forward(tokens, mixed, attention_weights, weights, up_bias, vectors, live, cotangent):
    length, width = tokens.shape
    parts, shards, double_rows, hidden = weights.shape
    whole = lambda shape: pl.BlockSpec(shape, lambda p, w: (0,) * len(shape))
    once = lambda shape: pl.BlockSpec(
        shape, lambda p, w: (0,) * len(shape), pipeline_mode=pl.Buffered(1)
    )
    wo_column = attention_weights.shape[1] // width - 1
    wide = (length, width)
    return pl.pallas_call(
        partial(ffn_kernel, double_rows // 2),
        grid=(2, parts),
        in_specs=[
            once(wide),
            once(wide),
            pl.BlockSpec(
                (width, width), lambda p, w: (0, wo_column), pipeline_mode=pl.Buffered(1)
            ),
            pl.BlockSpec((None, shards, double_rows, hidden), lambda p, w: (w, 0, 0, 0)),
            pl.BlockSpec((None, 1, hidden), lambda p, w: (w, 0, 0)),
            whole(vectors.shape),
            once((length, 1)),
            once(wide),
        ],
        out_specs=[
            whole(wide),
            whole(wide),
            whole(wide),
            pl.BlockSpec((None, shards, double_rows, hidden), lambda p, w: (w * p, 0, 0, 0)),
            pl.BlockSpec((None, 1, hidden), lambda p, w: (w * p, 0, 0)),
            whole((8, width)),
        ],
        out_shape=[
            jax.ShapeDtypeStruct(wide, bf16),
            jax.ShapeDtypeStruct(wide, f32),
            jax.ShapeDtypeStruct(wide, bf16),
            jax.ShapeDtypeStruct(weights.shape, bf16),
            jax.ShapeDtypeStruct((parts, 1, hidden), f32),
            jax.ShapeDtypeStruct((8, width), f32),
        ],
        scratch_shapes=[
            pltpu.VMEM(wide, f32),
            pltpu.VMEM(wide, bf16),
            pltpu.VMEM((width, length), bf16),
            pltpu.VMEM(wide, f32),
            pltpu.VMEM((length, 1), f32),
            pltpu.VMEM((parts, length, hidden), bf16),
            pltpu.VMEM((parts, length, hidden), f32),
            pltpu.VMEM(wide, f32),
            pltpu.VMEM(wide, f32),
            pltpu.VMEM(wide, bf16),
            pltpu.VMEM((width, length), bf16),
        ],
        compiler_params=pltpu.CompilerParams(vmem_limit_bytes=56 * 1024 * 1024),
        name="feed_forward",
    )(tokens, mixed, attention_weights, weights, up_bias, vectors, live, cotangent)


def exchange_sum(value, axes, devices):
    step = 1
    while step < devices:
        pairs = [(i, i ^ step) for i in range(devices)]
        value = value + lax.ppermute(value, axes, pairs)
        step *= 2
    return value


def per_device(
    batch,
    wide,
    tokens,
    block_row,
    block_live,
    query_weight,
    key_weight,
    value_weight,
    out_weight,
    position_bias,
    features,
    up_weight,
    up_bias,
    down_weight,
    down_bias,
    gain_one,
    shift_one,
    gain_two,
    shift_two,
    cotangent,
):
    axes = ("batch", "wide")
    devices = batch * wide
    length, width = tokens.shape
    heads = position_bias.shape[0]
    pairs = heads // 2
    own = query_weight.shape[0]
    lanes = width // pairs
    shard = jnp.stack(
        [w.astype(bf16).reshape(own, pairs, lanes) for w in (query_weight, key_weight, value_weight)],
        axis=2,
    ).reshape(own, 3 * width)
    shard = jnp.concatenate([shard, out_weight.astype(bf16)], axis=1)
    attention_weights = lax.all_gather(shard, axes, axis=0, tiled=True)
    up_rows, hidden = up_weight.shape
    ffn_shard = jnp.concatenate([up_weight.astype(bf16), down_weight.astype(bf16)], axis=0)
    ffn_weights = lax.all_gather(ffn_shard, ("wide", "batch"), axis=0, tiled=False)
    ffn_weights = ffn_weights.reshape(wide, batch, 2 * up_rows, hidden)

    offsets = jnp.arange(BLK, dtype=jnp.int32)
    live = (offsets[None, :] < block_live[:, None]).astype(f32).reshape(1, length)
    rows = jnp.broadcast_to(block_row[:, None], (block_row.shape[0], BLK)).reshape(1, length)
    mask = jnp.where(block_row[:, None] == rows, live, 0.0)
    tables = toeplitz_tables(position_bias[:, ::-1])
    feat = block_diagonal(features)
    mixed, u, phi, value = attend(tokens, attention_weights, tables, mask, split_rows(feat), heads)

    vectors = jnp.stack([down_bias, gain_one, shift_one, gain_two, shift_two] + [down_bias] * 3)
    out_tokens, grad_one, grad_attention, dw_ffn, dup_bias, dvec = feed_forward(
        tokens,
        mixed,
        attention_weights,
        ffn_weights,
        up_bias.reshape(wide, 1, hidden),
        vectors,
        live.reshape(length, 1),
        cotangent,
    )
    ffn_own = lax.psum_scatter(
        dw_ffn.reshape(devices, 2 * up_rows, hidden),
        ("wide", "batch"),
        scatter_dimension=0,
        tiled=False,
    ).astype(f32)
    dw_qkv, dbias, grad_tokens = attend_back(
        tokens.T,
        attention_weights,
        tables,
        mask,
        split_rows(feat.T),
        u,
        phi,
        value,
        grad_attention,
        grad_one,
        heads,
    )
    dw_out = lax.dot_general(
        mixed, grad_attention, (((0,), (0,)), ((), ())), preferred_element_type=f32
    )
    dw_att = jnp.concatenate([dw_qkv, dw_out.astype(bf16)], axis=1)
    att_own = lax.psum_scatter(dw_att, axes, scatter_dimension=0, tiled=True).astype(f32)
    qkv_own = att_own[:, : 3 * width].reshape(own, pairs, 3, lanes)
    dq, dk, dv = (qkv_own[:, :, i].reshape(own, width) for i in range(3))
    small = exchange_sum(
        jnp.concatenate([dup_bias.reshape(-1, 256), dvec.reshape(-1, 256)], axis=0), axes, devices
    )
    dbias = exchange_sum(dbias, axes, devices)
    count = up_bias.shape[0] // 256
    dvec = small[count:].reshape(8, width)
    return (
        out_tokens,
        grad_tokens,
        dq,
        dk,
        dv,
        att_own[:, 3 * width :],
        dbias[:, ::-1],
        ffn_own[:up_rows],
        small[:count].reshape(-1),
        ffn_own[up_rows:],
        dvec[0],
        dvec[1],
        dvec[2],
        dvec[3],
        dvec[4],
    )


def solution(mesh):
    both = P(("batch", "wide"), None)
    placed = (
        both,
        P(("batch", "wide")),
        P(("batch", "wide")),
        both,
        both,
        both,
        both,
        P(),
        P(),
        P("batch", "wide"),
        P(),
        P("batch", "wide"),
        P(),
        P(),
        P(),
        P(),
        P(),
        both,
    )
    outs = (
        both,
        both,
        both,
        both,
        both,
        both,
        P(),
        P("batch", "wide"),
        P(),
        P("batch", "wide"),
        P(),
        P(),
        P(),
        P(),
        P(),
    )
    return jax.shard_map(
        partial(per_device, mesh.shape["batch"], mesh.shape["wide"]),
        mesh=mesh,
        in_specs=placed,
        out_specs=outs,
        check_vma=False,
    )
```

time: 1360 us -> 498 us (0.37)
  waiting for transfers between devices: 777 us -> 330 us
  local copies, waits for them, and re-layouts: 285 us -> 20.4 us
  matrix products: 231 us -> 1.94 us
  Pallas kernels: 0 us -> 103 us
  other arithmetic: 34.5 us -> 14.7 us
    unnamed x20 -> x4, waiting for transfers between devices: 313 us -> 0.53 us
    dot_general x106 -> x1, matrix products: 231 us -> 1.94 us  [per_device(): lax.dot_general(mixed, grad_attention, (((0,), (0,)), ((), ())), preferre...]
    all_gather x8 -> x2, waiting for transfers between devices: 219 us -> 107 us  [the longest x1 58.8 us: per_device(): lax.all_gather(ffn_shard, ('wide', 'batch'), axis=0, tiled=False)]
    reshape x36 -> x7, local copies, waits for them, and re-layouts: 105 us -> 1.52 us  [the longest x1 0.65 us: toeplitz_tables(): flipped_bias.reshape(heads // step, step, rels)]
    pallas_call x0 -> x4, Pallas kernels: none -> 103 us  [the longest x1 41.3 us: attend_back(): pl.pallas_call(partial(attend_back_kernel, scale), grid=(pairs,), in_spec...]
    psum x1 -> x0, waiting for transfers between devices: 78.5 us -> none  [per_device(): lax.psum((grad_up_bias, grad_down_bias, grad_gain_one, grad_shift_one, gr...]
    reduce_scatter x5 -> x2, waiting for transfers between devices: 166 us -> 214 us  [the longest x1 137 us: per_device(): lax.psum_scatter(dw_ffn.reshape(devices, 2 * up_rows, hidden), ('wide', '...]
    slice x48 -> x6, local copies, waits for them, and re-layouts: 41.5 us -> 3.74 us  [the longest x1 1.41 us: per_device(): att_own[:, 3 * width:]]
  transfers between devices with their start and end apart: 17 -> 14, of which waited for: 13 -> 10; matrix products, arithmetic and copies ran while one was open for 37% -> 5% of each run, Pallas kernels for 0% -> 6%
where the time goes in v1:
time: 498 us; the launch traced here: 497 us
  waiting for transfers between devices  330 us (66%)
  Pallas kernels  103 us (21%)
  local copies, waits for them, and re-layouts  20.4 us (4%)
  other arithmetic  14.7 us (3%)
  between operations  14.1 us (3%)
  starting transfers between devices  13.6 us (3%)
    reduce_scatter x1, waiting for transfers between devices, per_device(): lax.psum_scatter(dw_ffn.reshape(devices, 2 * up_rows, hidden), ('wide', '...  137 us
    reduce_scatter x1, waiting for transfers between devices, per_device(): lax.psum_scatter(dw_att, axes, scatter_dimension=0, tiled=True).astype(f32)  77.1 us
    all_gather x1, waiting for transfers between devices, per_device(): lax.all_gather(ffn_shard, ('wide', 'batch'), axis=0, tiled=False)  58.8 us
    all_gather x1, waiting for transfers between devices, per_device(): attention_weights = lax.all_gather(shard, axes, axis=0, tiled=True)  48.2 us
    pallas_call x1, Pallas kernels, attend_back(): pl.pallas_call(partial(attend_back_kernel, scale), grid=(pairs,), in_spec...  41.3 us
    pallas_call x1, Pallas kernels, feed_forward(): pl.pallas_call(partial(ffn_kernel, double_rows // 2), grid=(2, parts), in...  30.4 us
    pallas_call x1, Pallas kernels, attend(): pl.pallas_call(partial(attend_kernel, scale), grid=(pairs,), in_specs=[wh...  25.5 us
    ppermute x10, starting transfers between devices, exchange_sum(): value = value + lax.ppermute(value, axes, pairs)  13.4 us
  transfers between devices with their start and end apart: 14, of which 10 were waited for; matrix products, arithmetic and copies ran while one was open for 5% of the time, Pallas kernels for 6%

profile of v1, /device:TPU:0, one launch (start us, length us, event | category | flops | bytes accessed | tf_op | source)
XLA Modules:
  0.0 497.0 jit_solution(14631243599783803400)
XLA Ops:
  12.0 1.1 convert_element_type.77
  16.7 3.1 rev.6
  20.5 5.5 %toeplitz.1.table_ref = f32[12,128,1024]{2,1,0:T(8,128)} custom-call(f32[6,2,1024]{2,1,0:T(2,128)} %reshape.124.bias_ref), custom_call_target="tpu_custom_call" | custom-call | tf_op jit(solution)/shard_map/toeplitz/pallas_call | solution.py:40
  27.1 1.2 copy.46
  30.3 48.2 %all-gather.4.cloned.1.call-done.w_ref.wo_ref = bf16[768,3072]{1,0:T(8,128)(2,1)} async-done(((bf16[24,3072]{1,0:T(8,128)(2,1)}), bf16[768,3072]{1,0:T(8,128)(2,1)}) %all-gather.4.cloned.1.call-update) | async-done | bytes 4718608 | tf_op jit(solution)/shard_map/all_gather | solution.py:504
  78.5 25.5 %attend.1 = (bf16[512,768]{1,0:T(8,128)(2,1)}, f32[512,1536]{1,0:T(8,128)}, f32[512,1536]{1,0:T(8,128)}, bf16[512,768]{1,0:T(8,128)(2,1)}) custom-call(bf16[512,768]{1,0:T(8,128)(2,1)} %tok_ref.3, bf16[768,3072]{1,0:T(8,128)(2,1)} %all-gather.4.cloned.1.call-done.w_ref.wo_ref, f32[12,128,1024]{2,1,0:T(8,128)} %toeplitz.1.table_ref, ...), custom_call_target="tpu_custom_call" | custom-call | tf_op jit(solution)/shard_map/attend/pallas_call | solution.py:104
  104.0 58.8 %all-gather.6.cloned.1.call-done = bf16[6144,768]{1,0:T(8,128)(2,1)} async-done(((bf16[192,768]{1,0:T(8,128)(2,1)}), bf16[6144,768]{1,0:T(8,128)(2,1)}) %all-gather.6.cloned.1.call-update) | async-done | bytes 9437200 | tf_op jit(solution)/shard_map/all_gather | solution.py:507
  162.8 30.4 %feed_forward.1 = (bf16[512,768]{1,0:T(8,128)(2,1)}, f32[512,768]{1,0:T(8,128)}, bf16[512,768]{1,0:T(8,128)(2,1)}, bf16[4,8,192,768]{3,2,1,0:T(8,128)(2,1)}, f32[4,1,768]{2,1,0:T(1,128)}, /*index=5*/f32[8,768]{1,0:T(8,128)}) custom-call(bf16[512,768]{1,0:T(8,128)(2,1)} %tok_ref.3, bf16[512,768]{1,0:T(8,128)(2,1)} %get-tuple-element.28.mixed_ref, ...), custom_call_target="tpu_custom_call" | custom-call | tf_op jit(solution)/shard_map/feed_forward/pallas_call | solution.py:412
  193.3 1.9 convolution_convert_fusion
  195.2 41.3 %attend_back.1 = (bf16[768,2304]{1,0:T(8,128)(2,1)}, f32[6,2,1024]{2,1,0:T(2,128)}, f32[512,768]{1,0:T(8,128)}) custom-call(bf16[768,512]{1,0:T(8,128)(2,1)} %bitcast.34, bf16[768,3072]{1,0:T(8,128)(2,1)} %all-gather.4.cloned.1.call-done.w_ref.wo_ref, f32[12,128,1024]{2,1,0:T(8,128)} %toeplitz.1.table_ref, f32[4,512]{1,0:T(4,128)} %compare_select_fusion.mask_ref, ...), custom_call_target="tpu_custom_call" | custom-call | tf_op jit(solution)/shard_map/attend_back/pallas_call | solution.py:232
  236.5 4.9 pad_maximum_fusion
  243.6 1.5 collective-permute-start.6
  245.7 1.9 collective-permute-done.6
  247.6 1.9 collective-permute-start.7
  250.3 1.7 collective-permute-done.7
  252.1 1.5 collective-permute-start.8
  253.9 1.5 collective-permute-start.3
  256.1 2.3 collective-permute-start.9
  258.4 2.6 collective-permute-done.9
  261.0 2.6 collective-permute-start.4
  267.2 2.8 rev.7
  270.0 77.1 %reduce-scatter.3.cloned.1.call-done = bf16[24,3072]{1,0:T(8,128)(2,1)} async-done(((bf16[768,3072]{1,0:T(8,128)(2,1)}), bf16[24,3072]{1,0:T(8,128)(2,1)}) %reduce-scatter.3.cloned.1.call-update) | async-done | bytes 147472 | tf_op jit(solution)/shard_map/reduce_scatter | solution.py:552
  349.4 1.4 slice.75
  351.5 137.1 %reduce-scatter.5.cloned.1.call-done = bf16[1,192,768]{2,1,0:T(8,128)(2,1)} async-done(((bf16[32,192,768]{2,1,0:T(8,128)(2,1)}), bf16[1,192,768]{2,1,0:T(8,128)(2,1)}) %reduce-scatter.5.cloned.1.call-update) | async-done | bytes 294928 | tf_op jit(solution)/shard_map/reduce_scatter | solution.py:529
  (104 shorter events, 25.1 us)
Async XLA Ops:
  7.2 71.3 %all-gather.4.cloned.1.call-start = ((), (), s32[]{:S(2)}) async-start(), calls=%async_computation.2 | async-start | bytes 4866048 | tf_op jit(solution)/shard_map/all_gather | solution.py:504
  11.3 14.8 %copy-start.11 = (s32[4]{0:T(128)S(1)}, s32[4]{0:T(128)}, u32[]{:S(2)}) copy-start(s32[4]{0:T(128)} %param.20) | copy-start | bytes 52
  11.9 15.0 %copy-start.5 = (f32[768]{0:T(1024)S(1)}, f32[768]{0:T(1024)}, u32[]{:S(2)}) copy-start(f32[768]{0:T(1024)} %param.30) | copy-start | bytes 9220
  11.9 15.0 %copy-start.6 = (f32[768]{0:T(1024)S(1)}, f32[768]{0:T(1024)}, u32[]{:S(2)}) copy-start(f32[768]{0:T(1024)} %param.31) | copy-start | bytes 9220
  11.9 15.1 %copy-start.7 = (f32[768]{0:T(1024)S(1)}, f32[768]{0:T(1024)}, u32[]{:S(2)}) copy-start(f32[768]{0:T(1024)} %param.32) | copy-start | bytes 9220
  11.9 15.1 %copy-start.8 = (f32[768]{0:T(1024)S(1)}, f32[768]{0:T(1024)}, u32[]{:S(2)}) copy-start(f32[768]{0:T(1024)} %param.33) | copy-start | bytes 9220
  11.9 15.1 %copy-start.9 = (f32[768]{0:T(1024)S(1)}, f32[768]{0:T(1024)}, u32[]{:S(2)}) copy-start(f32[768]{0:T(1024)} %param.34) | copy-start | bytes 9220
  11.9 15.1 %copy-start = (bf16[512,768]{1,0:T(8,128)(2,1)S(1)}, bf16[512,768]{1,0:T(8,128)(2,1)}, u32[]{:S(2)}) copy-start(bf16[512,768]{1,0:T(8,128)(2,1)} %tok_ref.3) | copy-start | bytes 2359300
  12.0 150.9 %all-gather.6.cloned.1.call-start = ((), (), s32[]{:S(2)}) async-start(), calls=%async_computation.5 | async-start | bytes 9732096 | tf_op jit(solution)/shard_map/all_gather | solution.py:507
  14.9 14.7 %copy-start.10 = (s32[4]{0:T(128)S(1)}, s32[4]{0:T(128)}, u32[]{:S(2)}) copy-start(s32[4]{0:T(128)} %param.19) | copy-start | bytes 52
  14.9 332.3 %reduce-scatter.3.cloned.1.call-start = ((), (), s32[]{:S(2)}) async-start(), calls=%async_computation.3 | async-start | bytes 4866048 | tf_op jit(solution)/shard_map/reduce_scatter | solution.py:552
  162.8 30.4 %copy-start.1 = (bf16[512,768]{1,0:T(8,128)(2,1)S(1)}, bf16[512,768]{1,0:T(8,128)(2,1)}, u32[]{:S(2)}) copy-start(bf16[512,768]{1,0:T(8,128)(2,1)} %get-tuple-element.28.mixed_ref) | copy-start | bytes 2359300
  241.4 247.2 %reduce-scatter.5.cloned.1.call-start = ((), (), s32[]{:S(2)}) async-start(), calls=%async_computation.4 | async-start | bytes 9732096 | tf_op jit(solution)/shard_map/reduce_scatter | solution.py:529
  241.5 1.1 copy-start.2
  242.3 1.3 collective-permute-start.5
  242.6 2.4 collective-permute-start
  243.6 4.1 collective-permute-start.6
  245.1 4.4 collective-permute-start.1
  247.6 4.4 collective-permute-start.7
  249.5 4.3 collective-permute-start.2
  252.1 4.0 collective-permute-start.8
  253.9 7.1 %collective-permute-start.3 = (f32[12,1024]{1,0:T(8,128)S(1)}, f32[12,1024]{1,0:T(8,128)S(1)}, u32[]{:S(2)}, u32[]{:S(2)}) collective-permute-start(f32[12,1024]{1,0:T(8,128)S(1)} %add.40), channel_id=1, source_target_pairs={{0,8},{1,9},{2,10},{3,11},{4,12},{5,13},{6,14},{7,15},{8,0},{9,1},... | collective-permute-start | bytes 147464 | tf_op jit(solution)/shard_map/ppermute | solution.py:465
  256.1 4.9 collective-permute-start.9
  261.0 6.2 %collective-permute-start.4 = (f32[12,1024]{1,0:T(8,128)S(1)}, f32[12,1024]{1,0:T(8,128)S(1)}, u32[]{:S(2)}, u32[]{:S(2)}) collective-permute-start(f32[12,1024]{1,0:T(8,128)S(1)} %add.41), channel_id=1, source_target_pairs={{0,16},{1,17},{2,18},{3,19},{4,20},{5,21},{6,22},{7,23},{8,24},{9,... | collective-permute-start | bytes 147464 | tf_op jit(solution)/shard_map/ppermute | solution.py:465
  (2 other events, 1.5 us)
Sparse Core Ops, SparseCore 0:
  12.1 66.3 all-gather.3
  82.0 80.8 all-gather.5
  241.5 105.5 reduce-scatter.2
  353.9 134.6 reduce-scatter.4

commit v2 on v1

v2 whole, which is shorter than its diff:
```python
import itertools
from functools import partial

import jax
import jax.numpy as jnp
from jax import lax
from jax.experimental import pallas as pl
from jax.experimental.pallas import tpu as pltpu
from jax.sharding import PartitionSpec as P

BLK = 128
f32 = jnp.float32
bf16 = jnp.bfloat16
nt_dims = (((1,), (1,)), ((), ()))


def dot(a, b):
    return jnp.dot(a, b, preferred_element_type=f32)


def dot_nt(a, b):
    return lax.dot_general(a, b, nt_dims, preferred_element_type=f32)


def split_low(x):
    high = x.astype(bf16)
    return high, (x - high.astype(f32)).astype(bf16)


def toeplitz_kernel(bias_ref, out_ref):
    heads = bias_ref.shape[0]
    rels = bias_ref.shape[1]
    for h in range(heads):
        row = jnp.broadcast_to(jnp.exp(bias_ref[h : h + 1, :]), (BLK, rels))
        out_ref[h] = pltpu.roll(row, rels - BLK + 1, 1, stride=1, stride_axis=0)


def toeplitz_tables(flipped_bias):
    heads, rels = flipped_bias.shape
    step = 2
    return pl.pallas_call(
        toeplitz_kernel,
        grid=(heads // step,),
        in_specs=[pl.BlockSpec((None, step, rels), lambda h: (h, 0, 0))],
        out_specs=pl.BlockSpec((step, BLK, rels), lambda h: (h, 0, 0)),
        out_shape=jax.ShapeDtypeStruct((heads, BLK, rels), f32),
        cost_estimate=pl.CostEstimate(
            flops=5_000_000_000, bytes_accessed=8_000_000, transcendentals=0
        ),
        name="toeplitz",
    )(flipped_bias.reshape(heads // step, step, rels))


def lane_half(shape):
    return lax.broadcasted_iota(jnp.int32, shape, 1) < shape[1] // 2


def pair_features(u, feat_ref):
    high, low = split_low(u)
    square = u * u
    s_high, rest = split_low(square)
    rest = square - s_high.astype(f32)
    s_mid, s_low = split_low(rest)
    lhs = jnp.concatenate([high, high, low, s_high, s_mid, s_low], axis=1)
    return jnp.exp(dot(lhs, feat_ref[...]))


def attend_kernel(
    scale,
    tok_ref,
    w_ref,
    table_ref,
    mask_ref,
    feat_ref,
    mixed_ref,
    mixed32_ref,
    u_ref,
    phi_ref,
    val_ref,
    inv_ref,
    weights_ref,
):
    length = tok_ref.shape[0]
    pair = mixed_ref.shape[1]
    size = pair // 2
    blocks = length // BLK
    qkv = dot(tok_ref[...], w_ref[...])
    uq = qkv[:, :pair] * scale
    uk = qkv[:, pair : 2 * pair] * scale
    value = qkv[:, 2 * pair :].astype(bf16)
    pq = pair_features(uq, feat_ref)
    pk = pair_features(uk, feat_ref)
    u_ref[:, :pair] = uq
    u_ref[:, pair:] = uk
    phi_ref[:, :pair] = pq
    phi_ref[:, pair:] = pk
    val_ref[...] = value
    pq = pq.astype(bf16)
    pk = pk.astype(bf16)
    first = lane_half(value.shape)
    zero = jnp.zeros_like(value)
    one = jnp.ones_like(value)
    out = None
    for h in range(2):
        cols = slice(h * size, (h + 1) * size)
        here = first if h == 0 else jnp.logical_not(first)
        for b in range(blocks):
            rows = slice(b * BLK, (b + 1) * BLK)
            start = (blocks - 1 - b) * BLK
            scores = dot_nt(pq[rows, cols], pk[:, cols])
            coupling = table_ref[h, :, start : start + length] * mask_ref[b : b + 1, :]
            weights_ref[rows, :] = (coupling * scores).astype(bf16)
        rhs = jnp.concatenate([jnp.where(here, value, zero), jnp.where(here, one, zero)], axis=1)
        part = dot(weights_ref[...], rhs)
        out = part if out is None else out + part
    inverse = 1.0 / out[:, pair:]
    mixed = out[:, :pair] * inverse
    inv_ref[...] = inverse
    mixed32_ref[...] = mixed
    mixed_ref[...] = mixed.astype(bf16)


def attend(tokens, weights, tables, mask, feat_split, heads):
    length, width = tokens.shape
    pair = 2 * width // heads
    pairs = heads // 2
    rels = tables.shape[2]
    scale = float((pair // 2) ** (-0.25))
    whole = lambda shape: pl.BlockSpec(shape, lambda h: (0,) * len(shape))
    column = lambda cols: pl.BlockSpec((length, cols), lambda h: (0, h))
    return pl.pallas_call(
        partial(attend_kernel, scale),
        grid=(pairs,),
        in_specs=[
            whole((length, width)),
            pl.BlockSpec((width, 3 * pair), lambda h: (0, h)),
            pl.BlockSpec((2, BLK, rels), lambda h: (h, 0, 0)),
            whole(mask.shape),
            whole(feat_split.shape),
        ],
        out_specs=[
            column(pair),
            column(pair),
            column(2 * pair),
            column(2 * pair),
            column(pair),
            column(pair),
        ],
        out_shape=[
            jax.ShapeDtypeStruct((length, width), bf16),
            jax.ShapeDtypeStruct((length, width), f32),
            jax.ShapeDtypeStruct((length, 2 * width), f32),
            jax.ShapeDtypeStruct((length, 2 * width), f32),
            jax.ShapeDtypeStruct((length, width), bf16),
            jax.ShapeDtypeStruct((length, width), f32),
        ],
        scratch_shapes=[pltpu.VMEM((length, length), bf16)],
        cost_estimate=pl.CostEstimate(flops=0, bytes_accessed=0, transcendentals=0),
        name="attend",
    )(tokens, weights, tables, mask, feat_split)


def pair_backward(scale, grad_phi, phi, u, feat_ref):
    pair = u.shape[1]
    high, low = split_low(grad_phi * phi)
    back = dot(jnp.concatenate([high, high, low], axis=1), feat_ref[...])
    return (scale * (back[:, :pair] - u * back[:, pair:])).astype(bf16)


def attend_back_kernel(
    scale,
    place_ref,
    tok_t_ref,
    table_ref,
    mask_ref,
    feat_ref,
    swap_ref,
    turn_ref,
    u_ref,
    phi_ref,
    val_ref,
    inv_ref,
    mixed_ref,
    gm_ref,
    dw_mine_ref,
    dw_other_ref,
    dqkv_ref,
    dbias_ref,
    probs_ref,
    gs_ref,
    diag_ref,
):
    length, pair = val_ref.shape
    size = pair // 2
    blocks = length // BLK
    gm = gm_ref[...].astype(f32)
    scaled = gm * inv_ref[...]
    g_high, g_low = split_low(scaled)
    gt = scaled.T
    gt_high, gt_low = split_low(gt)
    d_high, d_low = split_low(scaled * mixed_ref[...])
    inner = dot(jnp.concatenate([d_high, d_low], axis=1), swap_ref[...])
    i_high, i_low = split_low(inner)
    phi = phi_ref[...]
    pq32, pk32 = phi[:, :pair], phi[:, pair:]
    pq = pq32.astype(bf16)
    pk = pk32.astype(bf16)
    pq_t = pq32.T.astype(bf16)
    value = val_ref[...]
    first = lane_half(value.shape)
    unit = jnp.full_like(value, 1.0 / size)
    zero = jnp.zeros_like(value)
    gq = None
    gk_heads = []
    gv_heads = []
    for h in range(2):
        cols = slice(h * size, (h + 1) * size)
        here = first if h == 0 else jnp.logical_not(first)
        lhs = jnp.concatenate(
            [jnp.where(here, g_high, i_high), jnp.where(here, g_low, i_low)], axis=1
        )
        rhs = jnp.where(here, value, unit)
        rhs = jnp.concatenate([rhs, rhs], axis=1)
        diag_ref[...] = jnp.zeros_like(diag_ref)
        for b in range(blocks):
            rows = slice(b * BLK, (b + 1) * BLK)
            start = (blocks - 1 - b) * BLK
            window = slice(start, start + length)
            mask = mask_ref[b : b + 1, :]
            scores = dot_nt(pq[rows, cols], pk[:, cols])
            coupling = table_ref[h, :, window] * mask
            probs_ref[rows, :] = (coupling * scores).astype(bf16)
            grad_scores = dot_nt(lhs[rows], rhs) * coupling
            gs_ref[rows, :] = grad_scores.astype(bf16)
            diag_ref[:, window] += grad_scores * scores
        part = dot(gs_ref[...], jnp.where(here, pk, zero))
        gq = part if gq is None else gq + part
        gk_heads.append(dot(pq_t[cols, :], gs_ref[...]))
        both = dot(jnp.concatenate([gt_high[cols], gt_low[cols]], axis=0), probs_ref[...])
        gv_heads.append(both[:size] + both[size:])
        folded = diag_ref[...]
        half = BLK // 2
        while half >= 1:
            folded = pltpu.roll(folded[:half], half, 1) + folded[half:]
            half //= 2
        split = [folded[:, n : n + BLK] for n in range(0, folded.shape[1], BLK)]
        f_high, rest = split_low(jnp.concatenate(split, axis=0))
        f_mid, f_low = split_low(jnp.concatenate(split, axis=0) - f_high.astype(f32))
        turned = dot(jnp.concatenate([f_high, f_mid, f_low], axis=1), turn_ref[...])
        for n in range(len(split)):
            dbias_ref[h : h + 1, n * BLK : (n + 1) * BLK] = turned[len(split) - 1 - n][None]
    gk = jnp.concatenate(gk_heads, axis=0).T
    gv = jnp.concatenate(gv_heads, axis=0).T.astype(bf16)
    u = u_ref[...]
    dq = pair_backward(scale, gq, pq32, u[:, :pair], feat_ref)
    dk = pair_backward(scale, gk, pk32, u[:, pair:], feat_ref)
    dqkv_ref[:, :pair] = dq
    dqkv_ref[:, pair : 2 * pair] = dk
    dqkv_ref[:, 2 * pair :] = gv
    half = tok_t_ref.shape[0] // 2
    place = place_ref[0]
    mine = pl.ds(pl.multiple_of(place * half, half), half)
    other = pl.ds(pl.multiple_of((1 - place) * half, half), half)
    dw_mine_ref[...] = dot(tok_t_ref[mine, :], dqkv_ref[...]).astype(bf16)
    dw_other_ref[...] = dot(tok_t_ref[other, :], dqkv_ref[...]).astype(bf16)


def attend_back(
    place,
    tokens_t,
    tables,
    mask,
    feat_back,
    swap,
    turn,
    u,
    phi,
    value,
    inverse,
    mixed,
    grad_mixed,
    heads,
    first,
    count,
):
    width, length = tokens_t.shape
    pair = 2 * width // heads
    rels = tables.shape[2]
    scale = float((pair // 2) ** (-0.25))
    whole = lambda shape: pl.BlockSpec(shape, lambda h, p: (0,) * len(shape))
    column = lambda cols: pl.BlockSpec((length, cols), lambda h, p: (0, h + first))
    own_column = lambda rows: pl.BlockSpec((rows, 3 * pair), lambda h, p: (0, h))
    return pl.pallas_call(
        partial(attend_back_kernel, scale),
        grid_spec=pltpu.PrefetchScalarGridSpec(
            num_scalar_prefetch=1,
            grid=(count,),
            in_specs=[
                whole((width, length)),
                pl.BlockSpec((2, BLK, rels), lambda h, p: (h + first, 0, 0)),
                whole(mask.shape),
                whole(feat_back.shape),
                whole(swap.shape),
                whole(turn.shape),
                column(2 * pair),
                column(2 * pair),
                column(pair),
                column(pair),
                column(pair),
                column(pair),
            ],
            out_specs=[
                own_column(width // 2),
                own_column(width // 2),
                own_column(length),
                pl.BlockSpec((None, 2, rels), lambda h, p: (h, 0, 0)),
            ],
            scratch_shapes=[
                pltpu.VMEM((length, length), bf16),
                pltpu.VMEM((length, length), bf16),
                pltpu.VMEM((BLK, rels), f32),
            ],
        ),
        out_shape=[
            jax.ShapeDtypeStruct((width // 2, count * 3 * pair), bf16),
            jax.ShapeDtypeStruct((width // 2, count * 3 * pair), bf16),
            jax.ShapeDtypeStruct((length, count * 3 * pair), bf16),
            jax.ShapeDtypeStruct((count, 2, rels), f32),
        ],
        cost_estimate=pl.CostEstimate(flops=0, bytes_accessed=0, transcendentals=0),
        name="attend_back",
    )(place, tokens_t, tables, mask, feat_back, swap, turn, u, phi, value, inverse, mixed, grad_mixed)


def block_diagonal(matrix):
    zero = jnp.zeros_like(matrix)
    return jnp.concatenate(
        [jnp.concatenate([matrix, zero], axis=1), jnp.concatenate([zero, matrix], axis=1)], axis=0
    )


def feature_tables(features):
    size = features.shape[0]
    ones = block_diagonal(jnp.ones((size, size), f32)).astype(bf16)
    high, low = split_low(block_diagonal(features))
    half = ones * -0.5
    forward = jnp.concatenate([high, low, high, half, half, half], axis=0)
    high, low = split_low(block_diagonal(features.T))
    none = jnp.zeros_like(ones)
    backward = jnp.concatenate(
        [jnp.concatenate([high, low, high], axis=0), jnp.concatenate([ones, none, ones], axis=0)],
        axis=1,
    )
    swap = jnp.concatenate([-ones[:, size:], -ones[:, :size]], axis=1)
    turn = jnp.eye(BLK, dtype=bf16)[::-1]
    return forward, backward, jnp.concatenate([swap, swap], axis=0), jnp.tile(turn, (3, 1))


def prepare_kernel(q_ref, k_ref, v_ref, o_ref, up_ref, down_ref, att_ref, ffn_ref):
    width = o_ref.shape[1]
    lanes = att_ref.shape[1] // 4 // (width // 128)
    for j, ref in enumerate((q_ref, k_ref, v_ref)):
        for p in range(width // lanes):
            to = (3 * p + j) * lanes
            att_ref[:, to : to + lanes] = ref[:, p * lanes : (p + 1) * lanes].astype(bf16)
    att_ref[:, 3 * width :] = o_ref[...].astype(bf16)
    rows = up_ref.shape[0]
    ffn_ref[:rows] = up_ref[...].astype(bf16)
    ffn_ref[rows:] = down_ref[...].astype(bf16)


def prepare(query, key, value, out, up, down):
    own, width = query.shape
    return pl.pallas_call(
        prepare_kernel,
        out_shape=[
            jax.ShapeDtypeStruct((own, 4 * width), bf16),
            jax.ShapeDtypeStruct((2 * up.shape[0], up.shape[1]), bf16),
        ],
        name="prepare",
    )(query, key, value, out, up, down)


root_half = 0.7071067811865476
inv_root_two_pi = 0.3989422804014327
eps = 1e-05


def norm_stats(residual):
    centered = residual - jnp.mean(residual, axis=1, keepdims=True)
    inverse = lax.rsqrt(jnp.mean(centered * centered, axis=1, keepdims=True) + eps)
    return centered * inverse, inverse


def norm_back(grad, xhat, inverse, gain):
    scaled = grad * gain
    mean_grad = jnp.mean(scaled, axis=1, keepdims=True)
    mean_dot = jnp.mean(scaled * xhat, axis=1, keepdims=True)
    return (scaled - mean_grad - xhat * mean_dot) * inverse


def column_sum(x):
    return jnp.sum(x, axis=0, keepdims=True)


def ffn_kernel(
    place_ref,
    tok_ref,
    mixed_ref,
    mixed_t_ref,
    wo_ref,
    up_ref,
    down_ref,
    up_bias_ref,
    vec_ref,
    live_ref,
    cot_ref,
    out_ref,
    grad_one_ref,
    gm_ref,
    up_other_ref,
    up_mine_ref,
    down_other_ref,
    down_mine_ref,
    wo_other_ref,
    wo_mine_ref,
    dup_bias_ref,
    dvec_ref,
    normed_ref,
    low_ref,
    low_t_ref,
    xhat_ref,
    inv_ref,
    act_ref,
    slope_ref,
    acc_ref,
    gb_ref,
    gb_t_ref,
):
    phase = pl.program_id(0)
    part = pl.program_id(1)
    parts = pl.num_programs(1)
    length, width = tok_ref.shape
    rows, hidden = up_ref.shape[1:]
    chunk = 256 if hidden % 256 == 0 else hidden
    chunks = [slice(k, k + chunk) for k in range(0, hidden, chunk)]
    vec = vec_ref[...]
    down_bias, gain_one, shift_one, gain_two, shift_two = (vec[i : i + 1] for i in range(5))

    @pl.when((phase == 0) & (part == 0))
    def _():
        residual = tok_ref[...].astype(f32) + dot(mixed_ref[...], wo_ref[...])
        xhat, inverse = norm_stats(residual)
        normed = xhat * gain_one + shift_one
        xhat_ref[...] = xhat
        inv_ref[...] = inverse
        normed_ref[...] = normed
        low_ref[...] = normed.astype(bf16)
        low_t_ref[...] = normed.T.astype(bf16)
        acc_ref[...] = jnp.zeros_like(acc_ref)

    @pl.when(phase == 0)
    def _():
        for cols in chunks:
            up = up_ref[:, :, cols].reshape(width, chunk)
            down = down_ref[:, :, cols].reshape(width, chunk)
            v = dot(low_ref[...], up) + up_bias_ref[:, cols]
            half = 0.5 + 0.5 * lax.erf(v * root_half)
            act = (v * half).astype(bf16)
            act_ref[part, :, cols] = act
            slope_ref[part, :, cols] = half + v * (jnp.exp(-0.5 * v * v) * inv_root_two_pi)
            acc_ref[...] += dot_nt(act, down)

    @pl.when((phase == 0) & (part == parts - 1))
    def _():
        live = live_ref[...]
        xhat, inverse = norm_stats(normed_ref[...] + (acc_ref[...] + down_bias))
        out_ref[...] = ((xhat * gain_two + shift_two) * live).astype(bf16)
        grad = cot_ref[...].astype(f32) * live
        grad_two = norm_back(grad, xhat, inverse, gain_two)
        low = grad_two.astype(bf16)
        gb_ref[...] = low
        gb_t_ref[...] = grad_two.T.astype(bf16)
        dvec_ref[0:1, :] = column_sum(low.astype(f32))
        dvec_ref[3:4, :] = column_sum(grad * xhat)
        dvec_ref[4:5, :] = column_sum(grad)
        dvec_ref[5:8, :] = jnp.zeros((3, width), f32)
        acc_ref[...] = grad_two

    def backward(d_up_ref, d_down_ref):
        for cols in chunks:
            up = up_ref[:, :, cols].reshape(width, chunk)
            down = down_ref[:, :, cols].reshape(width, chunk)
            grad_act = dot(gb_ref[...], down)
            grad_hidden = (grad_act * slope_ref[part, :, cols]).astype(bf16)
            dup_bias_ref[:, cols] = column_sum(grad_hidden.astype(f32))
            d_up = dot(low_t_ref[...], grad_hidden).astype(bf16)
            d_down = dot(gb_t_ref[...], act_ref[part, :, cols]).astype(bf16)
            d_up_ref[:, :, cols] = d_up.reshape(-1, rows, chunk)
            d_down_ref[:, :, cols] = d_down.reshape(-1, rows, chunk)
            acc_ref[...] += dot_nt(grad_hidden, up)

    @pl.when((phase == 1) & (part < parts // 2))
    def _():
        backward(up_other_ref, down_other_ref)

    @pl.when((phase == 1) & (part >= parts // 2))
    def _():
        backward(up_mine_ref, down_mine_ref)

    @pl.when((phase == 1) & (part == parts - 1))
    def _():
        grad = acc_ref[...]
        xhat = xhat_ref[...]
        grad_one = norm_back(grad, xhat, inv_ref[...], gain_one)
        grad_one_ref[...] = grad_one
        grad_att = grad_one.astype(bf16)
        gm_ref[...] = dot_nt(grad_att, wo_ref[...]).astype(bf16)
        half = width // 2
        place = place_ref[0]
        mine = pl.ds(pl.multiple_of(place * half, half), half)
        other = pl.ds(pl.multiple_of((1 - place) * half, half), half)
        wo_mine_ref[...] = dot(mixed_t_ref[mine, :], grad_att).astype(bf16)
        wo_other_ref[...] = dot(mixed_t_ref[other, :], grad_att).astype(bf16)
        dvec_ref[1:2, :] = column_sum(grad * xhat)
        dvec_ref[2:3, :] = column_sum(grad)


def feed_forward(
    place, tokens, mixed, mixed_t, attention_weights, weights, up_bias, vectors, live, cotangent
):
    length, width = tokens.shape
    parts, shards, _, rows, hidden = weights.shape
    xs = parts // 2
    whole = lambda shape: pl.BlockSpec(shape, lambda p, w, c: (0,) * len(shape))
    once = lambda shape: pl.BlockSpec(
        shape, lambda p, w, c: (0,) * len(shape), pipeline_mode=pl.Buffered(1)
    )
    wo_column = attention_weights.shape[1] // width - 1
    wide = (length, width)
    part_of = lambda w, c: 2 * lax.rem(w, xs) + jnp.where(w < xs, 1 - c[0], c[0])
    weight_spec = lambda which: pl.BlockSpec(
        (None, shards, None, rows, hidden), lambda p, w, c: (part_of(w, c), 0, which, 0, 0)
    )
    other_spec = pl.BlockSpec(
        (None, shards, rows, hidden), lambda p, w, c: (p * jnp.minimum(w, xs - 1), 0, 0, 0)
    )
    mine_spec = pl.BlockSpec(
        (None, shards, rows, hidden), lambda p, w, c: (p * jnp.maximum(w - xs, 0), 0, 0, 0)
    )
    grads = jax.ShapeDtypeStruct((xs, shards, rows, hidden), bf16)
    return pl.pallas_call(
        ffn_kernel,
        grid_spec=pltpu.PrefetchScalarGridSpec(
            num_scalar_prefetch=1,
            grid=(2, parts),
            in_specs=[
                once(wide),
                once(wide),
                once((width, length)),
                pl.BlockSpec(
                    (width, width), lambda p, w, c: (0, wo_column), pipeline_mode=pl.Buffered(1)
                ),
                weight_spec(0),
                weight_spec(1),
                pl.BlockSpec((None, 1, hidden), lambda p, w, c: (part_of(w, c), 0, 0)),
                whole(vectors.shape),
                once((length, 1)),
                once(wide),
            ],
            out_specs=[
                whole(wide),
                whole(wide),
                whole(wide),
                other_spec,
                mine_spec,
                other_spec,
                mine_spec,
                whole((width // 2, width)),
                whole((width // 2, width)),
                pl.BlockSpec(
                    (None, 1, hidden), lambda p, w, c: (part_of(w * p, c), 0, 0)
                ),
                whole((8, width)),
            ],
            scratch_shapes=[
                pltpu.VMEM(wide, f32),
                pltpu.VMEM(wide, bf16),
                pltpu.VMEM((width, length), bf16),
                pltpu.VMEM(wide, f32),
                pltpu.VMEM((length, 1), f32),
                pltpu.VMEM((parts, length, hidden), bf16),
                pltpu.VMEM((parts, length, hidden), f32),
                pltpu.VMEM(wide, f32),
                pltpu.VMEM(wide, bf16),
                pltpu.VMEM((width, length), bf16),
            ],
        ),
        out_shape=[
            jax.ShapeDtypeStruct(wide, bf16),
            jax.ShapeDtypeStruct(wide, f32),
            jax.ShapeDtypeStruct(wide, bf16),
            grads,
            grads,
            grads,
            grads,
            jax.ShapeDtypeStruct((width // 2, width), bf16),
            jax.ShapeDtypeStruct((width // 2, width), bf16),
            jax.ShapeDtypeStruct((parts, 1, hidden), f32),
            jax.ShapeDtypeStruct((8, width), f32),
        ],
        compiler_params=pltpu.CompilerParams(vmem_limit_bytes=58 * 1024 * 1024),
        cost_estimate=pl.CostEstimate(flops=0, bytes_accessed=0, transcendentals=0),
        name="feed_forward",
    )(
        place,
        tokens,
        mixed,
        mixed_t,
        attention_weights,
        weights,
        weights,
        up_bias,
        vectors,
        live,
        cotangent,
    )


class Grid:
    def __init__(self, batch, wide):
        self.devices = batch * wide
        self.sizes = dict(z=4, y=batch // 4, x=wide // 2, c=2)
        self.strides = dict(z=batch // 4 * wide, y=wide, x=2, c=1)
        flat = lax.axis_index("batch") * wide + lax.axis_index("wide")
        self.place = {d: lax.rem(flat // self.strides[d], n) for d, n in self.sizes.items()}
        self.vector = jnp.stack([self.place[d] for d in "zyxc"])

    def shift(self, value, **offsets):
        pairs = []
        for i in range(self.devices):
            target = i
            for d, o in offsets.items():
                s, n = self.strides[d], self.sizes[d]
                target += ((i // s + o) % n - i // s % n) * s
            pairs.append((i, target))
        return lax.ppermute(value, ("batch", "wide"), pairs)

    def at(self, d, offset):
        return lax.rem(self.place[d] + (offset + self.sizes[d]), self.sizes[d])

    def block_at(self, d, offset):
        k, n = "zyxc".index(d), self.sizes[d]
        return lambda vector: lax.rem(vector[k] + offset, n)

    def offsets(self, dims):
        ranges = [range(self.sizes[d]) for d in dims]
        return [dict(zip(dims, o)) for o in itertools.product(*ranges)]

    def gather(self, value, names, dims):
        parts = [(o, self.shift(value, **o) if any(o.values()) else value) for o in self.offsets(dims)]
        if len(parts) == 2:
            (d,) = dims
            own, other = value, parts[1][1]
            first = self.place[d] == 0
            return jnp.concatenate(
                [jnp.where(first, own, other), jnp.where(first, other, own)], axis=names.index(d)
            )
        shape = [self.sizes[d] if d in dims else n for d, n in zip(names, value.shape)]
        out = jnp.zeros(shape + list(value.shape[len(names) :]), value.dtype)
        for o, part in parts:
            start = [self.at(d, -o[d]) if d in dims else 0 for d in names]
            out = lax.dynamic_update_slice(out, part, start + [0] * (value.ndim - len(names)))
        return out

    def send(self, sends, dims):
        return [self.shift(value, **o) for o, value in zip(self.offsets(dims)[1:], sends)]


class Combine:
    def __init__(self, grid, steps):
        self.grid, self.steps = grid, steps
        self.inputs, self.in_specs, self.shapes, self.out_specs, self.terms = [], [], [], [], []

    def spec(self, block, where):
        picks = []
        for w in where:
            if w is None:
                picks.append(lambda i, v: 0)
            elif w == "step":
                picks.append(lambda i, v: i)
            else:
                at = self.grid.block_at(*w)
                picks.append(lambda i, v, at=at: at(v))
        return pl.BlockSpec(block, lambda i, v: tuple(p(i, v) for p in picks))

    def read(self, arrays, where):
        numbers = []
        for a in arrays:
            block = tuple(n if w is None else None for n, w in zip(a.shape, where))
            numbers.append(len(self.inputs))
            self.inputs.append(a)
            self.in_specs.append(self.spec(block, where))
        return numbers

    def add(self, addends, picks):
        numbers = []
        for names, array in addends:
            where = tuple(picks.get(d) for d in names)
            where = tuple((d, w) if isinstance(w, int) else w for d, w in zip(names, where))
            numbers += self.read([array], where + (None,) * (array.ndim - len(names)))
        return numbers

    def write(self, shape, dtype, terms, stepped=False):
        where = ("step",) + (None,) * (len(shape) - 1) if stepped else (None,) * len(shape)
        block = tuple(n if w is None else None for n, w in zip(shape, where))
        self.shapes.append(jax.ShapeDtypeStruct(shape, dtype))
        self.out_specs.append(self.spec(block, where))
        self.terms.append(terms)

    def run(self, name):
        count = len(self.inputs)

        def kernel(vector_ref, *refs):
            for out_ref, terms in zip(refs[count:], self.terms):
                for target, *rest in terms:
                    total = None
                    for source, numbers in [rest] if len(rest) == 2 else rest[0]:
                        for n in numbers:
                            value = refs[n][source].astype(f32)
                            total = value if total is None else total + value
                    total = total.astype(out_ref.dtype)
                    if len(out_ref.shape) == 1:
                        total = total.reshape(out_ref.shape)
                    out_ref[target] = total

        return pl.pallas_call(
            kernel,
            grid_spec=pltpu.PrefetchScalarGridSpec(
                num_scalar_prefetch=1,
                grid=(self.steps,),
                in_specs=self.in_specs,
                out_specs=self.out_specs,
            ),
            out_shape=self.shapes,
            compiler_params=pltpu.CompilerParams(vmem_limit_bytes=60 * 1024 * 1024),
            cost_estimate=pl.CostEstimate(flops=0, bytes_accessed=0, transcendentals=0),
            name=name,
        )(self.grid.vector, *self.inputs)


everything = (Ellipsis,)


def hold(value, *others):
    return lax.optimization_barrier((value, others))


def per_device(
    batch,
    wide,
    tokens,
    block_row,
    block_live,
    query_weight,
    key_weight,
    value_weight,
    out_weight,
    position_bias,
    features,
    up_weight,
    up_bias,
    down_weight,
    down_bias,
    gain_one,
    shift_one,
    gain_two,
    shift_two,
    cotangent,
):
    grid = Grid(batch, wide)
    zs, ys, xs, cs = (grid.sizes[d] for d in "zyxc")
    length, width = tokens.shape
    heads, rels = position_bias.shape
    pairs = heads // 2
    own = query_weight.shape[0]
    lanes = width // pairs
    shard, ffn_shard = prepare(
        query_weight, key_weight, value_weight, out_weight, up_weight, down_weight
    )
    tables = toeplitz_tables(position_bias[:, ::-1])
    feat_forward, feat_back, swap, turn = feature_tables(features)
    offsets = jnp.arange(BLK, dtype=jnp.int32)
    live = (offsets[None, :] < block_live[:, None]).astype(f32).reshape(1, length)
    rows = jnp.broadcast_to(block_row[:, None], (block_row.shape[0], BLK)).reshape(1, length)
    mask = jnp.where(block_row[:, None] == rows, live, 0.0)
    by_core = lambda m: m.reshape(-1, cs, own, length).swapaxes(0, 1).reshape(width, length)
    tokens_t = by_core(tokens.T)
    vectors = jnp.stack([down_bias, gain_one, shift_one, gain_two, shift_two] + [down_bias] * 3)
    live_column = live.reshape(length, 1)

    up_rows, hidden = up_weight.shape
    gathered = grid.gather(shard.reshape(1, 1, 1, 1, own, 4 * width), "zyxc", "z")
    gathered = grid.gather(gathered, "zyxc", "yx")
    early = (tables, feat_forward, feat_back, swap, turn, mask, tokens_t, vectors, live_column)
    gathered, early = hold(gathered, *early)
    tables, feat_forward, feat_back, swap, turn, mask, tokens_t, vectors, live_column = early
    attention_weights = grid.gather(gathered, "zyxc", "c").reshape(width, 4 * width)
    ffn_weights = lax.all_gather(ffn_shard, ("wide", "batch"), axis=0, tiled=False)
    ffn_weights = ffn_weights.reshape(wide, batch, 2, up_rows, hidden)
    mixed, mixed32, u, phi, value, inverse = attend(
        tokens, attention_weights, tables, mask, feat_forward, heads
    )
    place = grid.place["c"].reshape(1)
    (
        out_tokens,
        grad_one,
        grad_mixed,
        up_other_grad,
        up_mine_grad,
        down_other,
        down_mine,
        out_other,
        out_mine,
        dup_bias,
        dvec,
    ) = feed_forward(
        place,
        tokens,
        mixed,
        by_core(mixed.T),
        attention_weights,
        ffn_weights,
        up_bias.reshape(wide, 1, hidden),
        vectors,
        live_column,
        cotangent,
    )
    ffn_view = lambda m: ("xzy", m.reshape(xs, zs, ys, up_rows, hidden))
    att_view = lambda m: ("zyx", m.reshape(zs, ys, xs, own, -1))
    down = [ffn_view(down_mine), ffn_view(grid.shift(down_other, c=1))]
    up = [ffn_view(up_mine_grad), ffn_view(grid.shift(up_other_grad, c=1))]
    out = [att_view(out_mine), att_view(grid.shift(out_other, c=1))]

    step = Combine(grid, 1)
    for y in range(1, ys):
        terms = [(everything, everything, step.add(down, dict(y=y)))]
        step.write((xs, zs, up_rows, hidden), bf16, terms)
    down_sends = step.run("down_sum_core")
    step = Combine(grid, 1)
    for x in range(1, xs):
        terms = [(everything, everything, step.add(up, dict(x=x)))]
        step.write((zs, ys, up_rows, hidden), bf16, terms)
    up_sends = step.run("up_sum_core")
    grad_mixed, (down_sends, up_sends) = hold(grad_mixed, down_sends, up_sends)
    down_new = grid.send(down_sends, "y")
    up_new = grid.send(up_sends, "x")

    dw_mine, dw_other, dqkv, dbias = attend_back(
        place,
        tokens_t,
        tables,
        mask,
        feat_back,
        swap,
        turn,
        u,
        phi,
        value,
        inverse,
        mixed32,
        grad_mixed,
        heads,
        0,
        pairs,
    )
    dw_mine, (dw_other, dqkv, dbias, down_new, up_new) = hold(
        dw_mine, dw_other, dqkv, dbias, down_new, up_new
    )
    down += [("xz", v) for v in down_new]
    up += [("zy", v) for v in up_new]
    att = [att_view(dw_mine), att_view(grid.shift(dw_other, c=1))]

    step = Combine(grid, 1)
    block = (zs, up_rows, hidden)
    for x in range(1, xs):
        terms = [(everything, everything, step.add(down, dict(y=0, x=x)))]
        step.write(block, bf16, terms)
    for y in range(1, ys):
        terms = [(everything, everything, step.add(up, dict(x=0, y=y)))]
        step.write(block, bf16, terms)
    sends = step.run("ffn_sum_plane")
    dbias, sends = hold(dbias, *sends)
    down_new = grid.send(sends[: xs - 1], "x")
    up_new = grid.send(sends[xs - 1 :], "y")

    columns = 4 * width
    per_row = columns // rels
    total_rows = 3 + heads // per_row
    extra = -(-total_rows // 8) * 8
    places = []
    for w in range(wide):
        places.append(("up", w, 0, slice(w * hidden, (w + 1) * hidden)))
    for j in range(8):
        places.append(("vec", j, 1 + j // 4, slice(j % 4 * width, (j % 4 + 1) * width)))
    for h in range(heads):
        places.append(
            ("bias", h, 3 + h // per_row, slice(h % per_row * rels, (h % per_row + 1) * rels))
        )
    step = Combine(grid, 1)
    ins = dict(
        up=step.read([dup_bias], (None, None, None)),
        vec=step.read([dvec], (None, None)),
        bias=step.read([dbias], (None, None, None)),
    )
    sources = dict(
        up=lambda n: (n,),
        vec=lambda n: (slice(n, n + 1),),
        bias=lambda n: (n // 2, slice(n % 2, n % 2 + 1)),
    )
    terms = [
        ((slice(r, r + 1), cols), sources[kind](n), ins[kind])
        for kind, n, r, cols in places
    ]
    step.write((extra, columns), f32, terms)
    (small,) = step.run("small_rows")
    small = small + grid.shift(small, c=1)
    small = [small] + grid.send([small.astype(bf16)] * (ys * xs - 1), "yx")
    dw_mine, sends = hold(dw_mine, *sends)
    att[0] = att_view(dw_mine)
    step = Combine(grid, 1)
    for o in grid.offsets("yx")[1:]:
        terms = [
            ((..., slice(0, 3 * width)), everything, step.add(att, o)),
            ((..., slice(3 * width, None)), everything, step.add(out, o)),
        ]
        step.write((zs, own, columns), bf16, terms)
    att_sends = step.run("att_sum_core")
    down_new, (up_new, att_sends) = hold(down_new, up_new, att_sends)
    down += [("z", v) for v in down_new]
    up += [("z", v) for v in up_new]
    att_new = grid.send(att_sends, "yx")

    here = dict(z=0, y=0, x=0)
    step = Combine(grid, 1)
    for z in range(1, zs):
        terms = [
            ((j,), everything, step.add(addends, dict(z=z, y=0, x=0)))
            for j, addends in enumerate((up, down))
        ]
        step.write((2, up_rows, hidden), bf16, terms)
    sends = step.run("ffn_sum_second")
    ffn_new = grid.send(sends, "z")
    att_new, sends = hold(att_new, *sends)
    att_new = [("z", v) for v in att_new]

    step = Combine(grid, 1)
    small_in = step.read(small, (None, None))
    for z in range(1, zs):
        picks = dict(z=z, y=0, x=0)
        top = slice(0, own)
        new = step.add(att_new, picks)
        head, tail = slice(0, 3 * width), slice(3 * width, None)
        terms = [
            ((top, head), everything, step.add(att, picks)),
            ((top, tail), everything, step.add(out, picks)),
        ]
        terms = [
            (target, [(everything, numbers), ((slice(None), target[1]), new)])
            for target, _, numbers in terms
        ]
        terms.append(((slice(own, None),), everything, small_in))
        step.write((own + extra, columns), bf16, terms)
    att_sends = step.run("att_sum_plane")
    last = grid.send(att_sends, "z")

    grad_tokens = grad_one + dot_nt(dqkv, attention_weights[:, : 3 * width])

    step = Combine(grid, 1)
    new = step.read(ffn_new, (None, None, None))
    for j, addends in enumerate((up, down)):
        terms = [(everything, [(everything, step.add(addends, here)), ((j,), new)])]
        step.write((up_rows, hidden), f32, terms)
    up_own, down_own = step.run("ffn_sum_last")

    step = Combine(grid, 1)
    new = step.add(att_new, here)
    mine = step.add(att, here)
    last = step.read(last, (None, None))
    for j in range(3):
        terms = []
        for p in range(pairs):
            cols = slice((3 * p + j) * lanes, (3 * p + j + 1) * lanes)
            source = (slice(None), cols)
            terms.append(
                (
                    (slice(None), slice(p * lanes, (p + 1) * lanes)),
                    [(source, new + mine), ((slice(0, own), cols), last)],
                )
            )
        step.write((own, width), f32, terms)
    tail = slice(3 * width, None)
    terms = [
        (everything, step.add(out, here)),
        ((slice(None), tail), new),
        ((slice(0, own), tail), last),
    ]
    step.write((own, width), f32, [(everything, terms)])
    small_in = step.read(small, (None, None))

    def small_term(r, cols):
        row = lambda base: (slice(base + r, base + r + 1), cols)
        return [(row(0), small_in), (row(own), last)]

    step.write((columns,), f32, [(everything, small_term(0, slice(None)))])
    terms = []
    for kind, n, r, cols in places:
        if kind == "vec" and n < 5:
            step.write((width,), f32, [(everything, small_term(r, cols))])
        if kind == "bias":
            terms.append(((slice(n, n + 1),), small_term(r, cols)))
    step.write((heads, rels), f32, terms)
    dq, dk, dv, out_own, dup_bias, *dvec, dbias = step.run("last_sum")
    return (
        out_tokens,
        grad_tokens,
        dq,
        dk,
        dv,
        out_own,
        dbias,
        up_own,
        dup_bias,
        down_own,
        *dvec,
    )


def solution(mesh):
    both = P(("batch", "wide"), None)
    placed = (
        both,
        P(("batch", "wide")),
        P(("batch", "wide")),
        both,
        both,
        both,
        both,
        P(),
        P(),
        P("batch", "wide"),
        P(),
        P("batch", "wide"),
        P(),
        P(),
        P(),
        P(),
        P(),
        both,
    )
    outs = (
        both,
        both,
        both,
        both,
        both,
        both,
        P(),
        P("batch", "wide"),
        P(),
        P("batch", "wide"),
        P(),
        P(),
        P(),
        P(),
        P(),
    )
    return jax.shard_map(
        partial(per_device, mesh.shape["batch"], mesh.shape["wide"]),
        mesh=mesh,
        in_specs=placed,
        out_specs=outs,
        check_vma=False,
    )
```

time: 498 us -> 278 us (0.56)
  waiting for transfers between devices: 330 us -> 74.8 us
  starting transfers between devices: 13.6 us -> 33.3 us
  Pallas kernels: 103 us -> 113 us
    reduce_scatter x2 -> x0, waiting for transfers between devices: 214 us -> none  [the longest x1 137 us: per_device(): lax.psum_scatter(dw_ffn.reshape(devices, 2 * up_rows, hidden), ('wide', '...]
    ppermute x10 -> x28, waiting for transfers between devices: 7.78 us -> 71.3 us  [shift(): return lax.ppermute(value, ('batch', 'wide'), pairs)]
    all_gather x1, waiting for transfers between devices: 58.8 us -> 3.44 us  [per_device(): lax.all_gather(ffn_shard, ('wide', 'batch'), axis=0, tiled=False)]
    all_gather x1 -> x0, waiting for transfers between devices: 48.2 us -> none  [per_device(): attention_weights = lax.all_gather(shard, axes, axis=0, tiled=True)]
    ppermute x10 -> x28, starting transfers between devices: 13.4 us -> 33.2 us  [shift(): return lax.ppermute(value, ('batch', 'wide'), pairs)]
    pallas_call x2 -> x12, Pallas kernels: 71.7 us -> 91.3 us  [the longest x1 34 us: feed_forward(): pl.pallas_call(ffn_kernel, grid_spec=pltpu.PrefetchScalarGridSpec(num_sca...]
    pallas_call x1, Pallas kernels: 25.5 us -> 15.8 us  [attend(): pl.pallas_call(partial(attend_kernel, scale), grid=(pairs,), in_specs=[wh...]
    convert_element_type x7 -> x2, other arithmetic: 6.63 us -> 0.67 us  [the longest x1 0.66 us: per_device(): small = [small] + grid.send([small.astype(bf16)] * (ys * xs - 1), 'yx')]
  transfers between devices with their start and end apart: 14 -> 29, of which waited for: 10 -> 13; matrix products, arithmetic and copies ran while one was open for 5% -> 13% of each run, Pallas kernels for 6% -> 25%
where the time goes in v2:
time: 278 us; the launch traced here: 277 us
  Pallas kernels  113 us (41%)
  waiting for transfers between devices  74.8 us (27%)
  starting transfers between devices  33.3 us (12%)
  local copies, waits for them, and re-layouts  24.7 us (9%)
  between operations  14.5 us (5%)
  other arithmetic  10.9 us (4%)
  matrix products  6.33 us (2%)
    ppermute x28, waiting for transfers between devices, shift(): return lax.ppermute(value, ('batch', 'wide'), pairs)  71.3 us
    pallas_call x1, Pallas kernels, feed_forward(): pl.pallas_call(ffn_kernel, grid_spec=pltpu.PrefetchScalarGridSpec(num_sca...  34 us
    ppermute x28, starting transfers between devices, shift(): return lax.ppermute(value, ('batch', 'wide'), pairs)  33.2 us
    pallas_call x9, Pallas kernels, run(): pl.pallas_call(kernel, grid_spec=pltpu.PrefetchScalarGridSpec(num_scalar_...  31 us
    pallas_call x1, Pallas kernels, attend_back(): pl.pallas_call(partial(attend_back_kernel, scale), grid_spec=pltpu.Prefet...  24.3 us
    pallas_call x1, Pallas kernels, attend(): pl.pallas_call(partial(attend_kernel, scale), grid=(pairs,), in_specs=[wh...  15.8 us
    unnamed x66, local copies, waits for them, and re-layouts  8.49 us
    dot_general x1, matrix products, dot_nt(): return lax.dot_general(a, b, nt_dims, preferred_element_type=f32)  6.33 us
  transfers between devices with their start and end apart: 29, of which 13 were waited for; matrix products, arithmetic and copies ran while one was open for 13% of the time, Pallas kernels for 25%

profile of v2, /device:TPU:0, one launch (start us, length us, event | category | flops | bytes accessed | tf_op | source)
XLA Modules:
  0.0 277.0 jit_solution(1317410363253434330)
XLA Ops:
  9.2 4.1 %collective-permute-start.1 = (bf16[1,1,1,1,24,3072]{5,4,3,2,1,0:T(8,128)(2,1)}, bf16[1,1,1,1,24,3072]{5,4,3,2,1,0:T(8,128)(2,1)S(1)}, u32[]{:S(2)}, u32[]{:S(2)}) collective-permute-start(bf16[1,1,1,1,24,3072]{5,4,3,2,1,0:T(8,128)(2,1)} %bitcast.88), channel_id=1, source_target_pairs={{0,16},{1,17},{2,18},{3,19},{4,20},{5,21},{6,22},{7,23},{8,24},{9,... | collective-permute-start | bytes 442376 | tf_op jit(solution)/shard_map/ppermute | solution.py:647
  18.0 3.1 %rev.6 = f32[12,1024]{1,0:T(8,128)S(1)} reverse(f32[12,1024]{1,0:T(8,128)} %param.25), dimensions={1} | reverse | bytes 98304 | tf_op jit(solution)/shard_map/rev | solution.py:791
  27.0 5.5 %toeplitz.1.table_ref = f32[12,128,1024]{2,1,0:T(8,128)} custom-call(f32[6,2,1024]{2,1,0:T(2,128)} %reshape.139.bias_ref), custom_call_target="tpu_custom_call" | custom-call | flops 5000000000 | bytes 8000000 | tf_op jit(solution)/shard_map/toeplitz/pallas_call | solution.py:41
  44.5 17.4 %collective-permute-done.3 = bf16[4,1,1,1,24,3072]{5,4,3,2,1,0:T(8,128)(2,1)} collective-permute-done((bf16[4,1,1,1,24,3072]{5,4,3,2,1,0:T(8,128)(2,1)}, bf16[4,1,1,1,24,3072]{5,4,3,2,1,0:T(8,128)(2,1)}, u32[]{:S(2)}, u32[]{:S(2)}) %collective-permute-start.3) | collective-permute-done | bytes 589856 | tf_op jit(solution)/shard_map/ppermute | solution.py:647
  63.0 10.3 %collective-permute-done.5 = bf16[4,1,1,1,24,3072]{5,4,3,2,1,0:T(8,128)(2,1)S(1)} collective-permute-done((bf16[4,1,1,1,24,3072]{5,4,3,2,1,0:T(8,128)(2,1)}, bf16[4,1,1,1,24,3072]{5,4,3,2,1,0:T(8,128)(2,1)S(1)}, u32[]{:S(2)}, u32[]{:S(2)}) %collective-permute-start.5) | collective-permute-done | bytes 589856 | tf_op jit(solution)/shard_map/ppermute | solution.py:647
  74.9 4.4 %collective-permute-done.6 = bf16[4,2,2,1,24,3072]{5,4,3,2,1,0:T(8,128)(2,1)} collective-permute-done((bf16[4,2,2,1,24,3072]{5,4,3,2,1,0:T(8,128)(2,1)S(1)}, bf16[4,2,2,1,24,3072]{5,4,3,2,1,0:T(8,128)(2,1)}, u32[]{:S(2)}, u32[]{:S(2)}) %collective-permute-start.6) | collective-permute-done | bytes 2359328 | tf_op jit(solution)/shard_map/ppermute | solution.py:647
  83.8 15.8 %attend.1 = (bf16[512,768]{1,0:T(8,128)(2,1)}, f32[512,768]{1,0:T(8,128)}, f32[512,1536]{1,0:T(8,128)}, f32[512,1536]{1,0:T(8,128)}, bf16[512,768]{1,0:T(8,128)(2,1)}, /*index=5*/f32[512,768]{1,0:T(8,128)}) custom-call(bf16[512,768]{1,0:T(8,128)(2,1)} %tok_ref.3, bf16[768,3072]{1,0:T(8,128)(2,1)} %bitcast.68, f32[12,128,1024]{2,1,0:T(8,128)} %toeplitz.1.table_ref, ...), custom_call_target="tpu_custom_call" | custom-call | tf_op jit(solution)/shard_map/attend/pallas_call | solution.py:131
  102.1 3.4 %all-gather.3.cloned.1.call-done = bf16[6144,768]{1,0:T(8,128)(2,1)} async-done(((bf16[192,768]{1,0:T(8,128)(2,1)}), bf16[6144,768]{1,0:T(8,128)(2,1)}) %all-gather.3.cloned.1.call-update) | async-done | bytes 9437200 | tf_op jit(solution)/shard_map/all_gather | solution.py:809
  105.5 34.0 %feed_forward.1 = (bf16[512,768]{1,0:T(8,128)(2,1)}, f32[512,768]{1,0:T(8,128)}, bf16[512,768]{1,0:T(8,128)(2,1)}, bf16[2,8,96,768]{3,2,1,0:T(8,128)(2,1)}, bf16...) custom-call(s32[1]{0:T(128)} %bitcast.place_ref, ...), custom_call_target="tpu_custom_call" | custom-call | tf_op jit(solution)/shard_map/feed_forward/pallas_call | solution.py:552
  140.7 4.4 %collective-permute-done.7 = bf16[2,8,96,768]{3,2,1,0:T(8,128)(2,1)S(1)} collective-permute-done((bf16[2,8,96,768]{3,2,1,0:T(8,128)(2,1)}, bf16[2,8,96,768]{3,2,1,0:T(8,128)(2,1)S(1)}, u32[]{:S(2)}, u32[]{:S(2)}) %collective-permute-start.7) | collective-permute-done | bytes 2359328 | tf_op jit(solution)/shard_map/ppermute | solution.py:647
  146.5 3.6 %down_sum_core.1 = bf16[2,4,96,768]{3,2,1,0:T(8,128)(2,1)} custom-call(s32[4]{0:T(128)} %pad_add_fusion.vector_ref, bf16[2,4,2,96,768]{4,3,2,1,0:T(8,128)(2,1)} %bitcast.56, bf16[2,4,2,96,768]{4,3,2,1,0:T(8,128)(2,1)} %bitcast.62), custom_call_target="tpu_custom_call" | custom-call | tf_op jit(solution)/shard_map/down_sum_core/pallas_call | solution.py:737
  150.1 3.7 %up_sum_core.1 = bf16[4,2,96,768]{3,2,1,0:T(8,128)(2,1)} custom-call(s32[4]{0:T(128)} %pad_add_fusion.vector_ref, bf16[2,4,2,96,768]{4,3,2,1,0:T(8,128)(2,1)} %bitcast.50, bf16[2,4,2,96,768]{4,3,2,1,0:T(8,128)(2,1)} %bitcast.24.refs_1_.refs_4_.refs_9_.refs_17_), custom_call_target="tpu_custom_call" | custom-call | tf_op jit(solution)/shard_map/up_sum_core/pallas_call | solution.py:737
  155.9 24.3 %attend_back.1 = (bf16[384,2304]{1,0:T(8,128)(2,1)}, bf16[384,2304]{1,0:T(8,128)(2,1)}, bf16[512,2304]{1,0:T(8,128)(2,1)}, f32[6,2,1024]{2,1,0:T(2,128)}) custom-call(s32[1]{0:T(128)} %bitcast.place_ref, bf16[768,512]{1,0:T(8,128)(2,1)} %bitcast.80, f32[12,128,1024]{2,1,0:T(8,128)} %toeplitz.1.table_ref, f32[4,512]{1,0:T(4,128)} %compare_select_fusion.mask_ref, ...), custom_call_target="tpu_custom_call" | custom-call | tf_op jit(solution)/shard_map/attend_back/pallas_call | solution.py:293
  184.5 3.9 %ffn_sum_plane.1 = (bf16[4,96,768]{2,1,0:T(8,128)(2,1)}, bf16[4,96,768]{2,1,0:T(8,128)(2,1)}) custom-call(s32[4]{0:T(128)} %pad_add_fusion.vector_ref, bf16[2,4,2,96,768]{4,3,2,1,0:T(8,128)(2,1)} %bitcast.57, bf16[2,4,2,96,768]{4,3,2,1,0:T(8,128)(2,1)} %bitcast.63, bf16[2,4,96,768]{3,2,1,0:T(8,128)(2,1)} %copy-done.2, bf16[2,4,2,96,768]{4,3,2,1,0:T(8,128)(2,1)} %bitcast.51, ...), custom_call_target="tpu_custom_call" | custom-call | tf_op jit(solution)/shard_map/ffn_sum_plane/pallas_call | solution.py:737
  193.7 4.0 %att_sum_core.1 = (bf16[4,24,3072]{2,1,0:T(8,128)(2,1)}, bf16[4,24,3072]{2,1,0:T(8,128)(2,1)}, bf16[4,24,3072]{2,1,0:T(8,128)(2,1)}) custom-call(s32[4]{0:T(128)} %pad_add_fusion.vector_ref, bf16[4,2,2,24,2304]{4,3,2,1,0:T(8,128)(2,1)} %bitcast.36, bf16[4,2,2,24,2304]{4,3,2,1,0:T(8,128)(2,1)} %bitcast.43, bf16[4,2,2,24,768]{4,3,2,1,0:T(8,128)(2,1)} %bitcast.73, ...), custom_call_target="tpu_custom_call" | custom-call | tf_op jit(solution)/shard_map/att_sum_core/pallas_call | solution.py:737
  197.7 5.6 %collective-permute-done.11.refs_7_.refs_15_.refs_23_.refs_10_ = bf16[4,96,768]{2,1,0:T(8,128)(2,1)S(1)} collective-permute-done((bf16[4,96,768]{2,1,0:T(8,128)(2,1)}, bf16[4,96,768]{2,1,0:T(8,128)(2,1)S(1)}, u32[]{:S(2)}, u32[]{:S(2)}) %collective-permute-start.11) | collective-permute-done | bytes 589856 | tf_op jit(solution)/shard_map/ppermute | solution.py:647
  207.1 3.9 %ffn_sum_second.1 = (bf16[2,96,768]{2,1,0:T(8,128)(2,1)}, bf16[2,96,768]{2,1,0:T(8,128)(2,1)}, bf16[2,96,768]{2,1,0:T(8,128)(2,1)}) custom-call(s32[4]{0:T(128)} %pad_add_fusion.vector_ref, bf16[2,4,2,96,768]{4,3,2,1,0:T(8,128)(2,1)} %bitcast.52, bf16[2,4,2,96,768]{4,3,2,1,0:T(8,128)(2,1)} %bitcast.24.refs_1_.refs_4_.refs_9_.refs_17_, ...), custom_call_target="tpu_custom_call" | custom-call | tf_op jit(solution)/shard_map/ffn_sum_second/pallas_call | solution.py:737
  214.6 5.5 %collective-permute-done.15.refs_4_.refs_11_.refs_18_.refs_0_ = bf16[4,24,3072]{2,1,0:T(8,128)(2,1)S(1)} collective-permute-done((bf16[4,24,3072]{2,1,0:T(8,128)(2,1)}, bf16[4,24,3072]{2,1,0:T(8,128)(2,1)S(1)}, u32[]{:S(2)}, u32[]{:S(2)}) %collective-permute-start.15) | collective-permute-done | bytes 589856 | tf_op jit(solution)/shard_map/ppermute | solution.py:647
  221.5 11.3 %collective-permute-done.16.refs_5_.refs_12_.refs_19_.refs_1_ = bf16[4,24,3072]{2,1,0:T(8,128)(2,1)S(1)} collective-permute-done((bf16[4,24,3072]{2,1,0:T(8,128)(2,1)}, bf16[4,24,3072]{2,1,0:T(8,128)(2,1)S(1)}, u32[]{:S(2)}, u32[]{:S(2)}) %collective-permute-start.16) | collective-permute-done | bytes 589856 | tf_op jit(solution)/shard_map/ppermute | solution.py:647
  237.8 3.4 %att_sum_plane.1 = (bf16[32,3072]{1,0:T(8,128)(2,1)}, bf16[32,3072]{1,0:T(8,128)(2,1)}, bf16[32,3072]{1,0:T(8,128)(2,1)}) custom-call(s32[4]{0:T(128)} %pad_add_fusion.vector_ref, f32[8,3072]{1,0:T(8,128)} %get-tuple-element.172.refs_0_.refs_10_, bf16[8,3072]{1,0:T(8,128)(2,1)} %copy-done.22, bf16[8,3072]{1,0:T(8,128)(2,1)} %copy-done.21, ...), custom_call_target="tpu_custom_call" | custom-call | tf_op jit(solution)/shard_map/att_sum_plane/pallas_call | solution.py:737
  245.7 6.3 %fusion.9 = f32[512,768]{1,0:T(8,128)} fusion(f32[512,768]{1,0:T(8,128)} %get-tuple-element.103, bf16[512,2304]{1,0:T(8,128)(2,1)} %get-tuple-element.125, bf16[768,3072]{1,0:T(8,128)(2,1)} %bitcast.70), kind=kOutput, calls=%fused_computation.37 | convolution fusion | flops 1812332544 | bytes 9043968 | tf_op jit(solution)/shard_map/dot_general | solution.py:22
  254.2 3.2 %ffn_sum_last.1 = (f32[96,768]{1,0:T(8,128)}, f32[96,768]{1,0:T(8,128)}) custom-call(s32[4]{0:T(128)} %pad_add_fusion.vector_ref, bf16[2,96,768]{2,1,0:T(8,128)(2,1)} %copy-done.12, bf16[2,96,768]{2,1,0:T(8,128)(2,1)} %copy-done.13, bf16[2,96,768]{2,1,0:T(8,128)(2,1)} %copy-done.14, bf16[2,4,2,96,768]{4,3,2,1,0:T(8,128)(2,1)} %bitcast.55, ...), custom_call_target="tpu_custom_call" | custom-call | tf_op jit(solution)/shard_map/ffn_sum_last/pallas_call | solution.py:737
  257.4 8.3 %collective-permute-done.23.refs_6_ = bf16[32,3072]{1,0:T(8,128)(2,1)S(1)} collective-permute-done((bf16[32,3072]{1,0:T(8,128)(2,1)}, bf16[32,3072]{1,0:T(8,128)(2,1)S(1)}, u32[]{:S(2)}, u32[]{:S(2)}) %collective-permute-start.23) | collective-permute-done | bytes 196640 | tf_op jit(solution)/shard_map/ppermute | solution.py:647
  267.0 3.2 %last_sum.1 = (f32[24,768]{1,0:T(8,128)}, f32[24,768]{1,0:T(8,128)}, f32[24,768]{1,0:T(8,128)}, f32[24,768]{1,0:T(8,128)}, f32[3072]{0:T(1024)}, /*index=5*/f32[...) custom-call(s32[4]{0:T(128)} %pad_add_fusion.vector_ref, ...), custom_call_target="tpu_custom_call" | custom-call | tf_op jit(solution)/shard_map/last_sum/pallas_call | solution.py:737
  (155 shorter events, 70.0 us)
Async XLA Ops:
  7.2 98.3 %all-gather.3.cloned.1.call-start = ((), (), s32[]{:S(2)}) async-start(), calls=%async_computation | async-start | bytes 9732096 | tf_op jit(solution)/shard_map/all_gather | solution.py:809
  9.2 26.3 %collective-permute-start.1 = (bf16[1,1,1,1,24,3072]{5,4,3,2,1,0:T(8,128)(2,1)}, bf16[1,1,1,1,24,3072]{5,4,3,2,1,0:T(8,128)(2,1)S(1)}, u32[]{:S(2)}, u32[]{:S(2)}) collective-permute-start(bf16[1,1,1,1,24,3072]{5,4,3,2,1,0:T(8,128)(2,1)} %bitcast.88), channel_id=1, source_target_pairs={{0,16},{1,17},{2,18},{3,19},{4,20},{5,21},{6,22},{7,23},{8,24},{9,... | collective-permute-start | bytes 442376 | tf_op jit(solution)/shard_map/ppermute | solution.py:647
  13.3 21.5 %collective-permute-start = (bf16[1,1,1,1,24,3072]{5,4,3,2,1,0:T(8,128)(2,1)}, bf16[1,1,1,1,24,3072]{5,4,3,2,1,0:T(8,128)(2,1)S(1)}, u32[]{:S(2)}, u32[]{:S(2)}) collective-permute-start(bf16[1,1,1,1,24,3072]{5,4,3,2,1,0:T(8,128)(2,1)} %bitcast.89), channel_id=1, source_target_pairs={{0,8},{1,9},{2,10},{3,11},{4,12},{5,13},{6,14},{7,15},{8,16},{9,17... | collective-permute-start | bytes 442376 | tf_op jit(solution)/shard_map/ppermute | solution.py:647
  14.9 21.2 %collective-permute-start.2 = (bf16[1,1,1,1,24,3072]{5,4,3,2,1,0:T(8,128)(2,1)}, bf16[1,1,1,1,24,3072]{5,4,3,2,1,0:T(8,128)(2,1)S(1)}, u32[]{:S(2)}, u32[]{:S(2)}) collective-permute-start(bf16[1,1,1,1,24,3072]{5,4,3,2,1,0:T(8,128)(2,1)} %bitcast.90), channel_id=1, source_target_pairs={{0,24},{1,25},{2,26},{3,27},{4,28},{5,29},{6,30},{7,31},{8,0},{9,1... | collective-permute-start | bytes 442376 | tf_op jit(solution)/shard_map/ppermute | solution.py:647
  36.8 25.0 %collective-permute-start.3 = (bf16[4,1,1,1,24,3072]{5,4,3,2,1,0:T(8,128)(2,1)}, bf16[4,1,1,1,24,3072]{5,4,3,2,1,0:T(8,128)(2,1)}, u32[]{:S(2)}, u32[]{:S(2)}) collective-permute-start(bf16[4,1,1,1,24,3072]{5,4,3,2,1,0:T(8,128)(2,1)} %constant_dynamic-update-slice_fusion.9), channel_id=1, source_target_pairs={{0,2},{1,3},{2,0},{3,1},{4,6},{5,7},{6,4},{7,5},{8,10},{9,11},{10,... | collective-permute-start | bytes 1769480 | tf_op jit(solution)/shard_map/ppermute | solution.py:647
  41.1 32.2 %collective-permute-start.5 = (bf16[4,1,1,1,24,3072]{5,4,3,2,1,0:T(8,128)(2,1)}, bf16[4,1,1,1,24,3072]{5,4,3,2,1,0:T(8,128)(2,1)S(1)}, u32[]{:S(2)}, u32[]{:S(2)}) collective-permute-start(bf16[4,1,1,1,24,3072]{5,4,3,2,1,0:T(8,128)(2,1)} %constant_dynamic-update-slice_fusion.9), channel_id=1, source_target_pairs={{0,6},{1,7},{2,4},{3,5},{4,2},{5,3},{6,0},{7,1},{8,14},{9,15},{10,... | collective-permute-start | bytes 1769480 | tf_op jit(solution)/shard_map/ppermute | solution.py:647
  42.6 20.4 %collective-permute-start.4 = (bf16[4,1,1,1,24,3072]{5,4,3,2,1,0:T(8,128)(2,1)}, bf16[4,1,1,1,24,3072]{5,4,3,2,1,0:T(8,128)(2,1)S(1)}, u32[]{:S(2)}, u32[]{:S(2)}) collective-permute-start(bf16[4,1,1,1,24,3072]{5,4,3,2,1,0:T(8,128)(2,1)} %constant_dynamic-update-slice_fusion.9), channel_id=1, source_target_pairs={{0,4},{1,5},{2,6},{3,7},{4,0},{5,1},{6,2},{7,3},{8,12},{9,13},{10,... | collective-permute-start | bytes 1769480 | tf_op jit(solution)/shard_map/ppermute | solution.py:647
  139.8 10.3 %collective-permute-start.8 = (bf16[2,8,96,768]{3,2,1,0:T(8,128)(2,1)}, bf16[2,8,96,768]{3,2,1,0:T(8,128)(2,1)}, u32[]{:S(2)}, u32[]{:S(2)}) collective-permute-start(bf16[2,8,96,768]{3,2,1,0:T(8,128)(2,1)} %get-tuple-element.117), channel_id=1, source_target_pairs={{0,1},{1,0},{2,3},{3,2},{4,5},{5,4},{6,7},{7,6},{8,9},{9,8},{10,11... | collective-permute-start | bytes 7077896 | tf_op jit(solution)/shard_map/ppermute | solution.py:647
  153.8 28.2 %collective-permute-start.9 = (bf16[2,4,96,768]{3,2,1,0:T(8,128)(2,1)S(1)}, bf16[2,4,96,768]{3,2,1,0:T(8,128)(2,1)S(1)}, u32[]{:S(2)}, u32[]{:S(2)}) collective-permute-start(bf16[2,4,96,768]{3,2,1,0:T(8,128)(2,1)S(1)} %copy-done.10), channel_id=1, source_target_pairs={{0,4},{1,5},{2,6},{3,7},{4,0},{5,1},{6,2},{7,3},{8,12},{9,13},{10,... | collective-permute-start | bytes 3538952 | tf_op jit(solution)/shard_map/ppermute | solution.py:647
  155.3 28.1 %collective-permute-start.10 = (bf16[4,2,96,768]{3,2,1,0:T(8,128)(2,1)}, bf16[4,2,96,768]{3,2,1,0:T(8,128)(2,1)S(1)}, u32[]{:S(2)}, u32[]{:S(2)}) collective-permute-start(bf16[4,2,96,768]{3,2,1,0:T(8,128)(2,1)} %up_sum_core.1), channel_id=1, source_target_pairs={{0,2},{1,3},{2,0},{3,1},{4,6},{5,7},{6,4},{7,5},{8,10},{9,11},{10,... | collective-permute-start | bytes 3538952 | tf_op jit(solution)/shard_map/ppermute | solution.py:647
  188.3 15.0 %collective-permute-start.11 = (bf16[4,96,768]{2,1,0:T(8,128)(2,1)}, bf16[4,96,768]{2,1,0:T(8,128)(2,1)S(1)}, u32[]{:S(2)}, u32[]{:S(2)}) collective-permute-start(bf16[4,96,768]{2,1,0:T(8,128)(2,1)} %get-tuple-element.131), channel_id=1, source_target_pairs={{0,2},{1,3},{2,0},{3,1},{4,6},{5,7},{6,4},{7,5},{8,10},{9,11},{10,... | collective-permute-start | bytes 1769480 | tf_op jit(solution)/shard_map/ppermute | solution.py:647
  188.9 14.7 %collective-permute-start.12 = (bf16[4,96,768]{2,1,0:T(8,128)(2,1)}, bf16[4,96,768]{2,1,0:T(8,128)(2,1)S(1)}, u32[]{:S(2)}, u32[]{:S(2)}) collective-permute-start(bf16[4,96,768]{2,1,0:T(8,128)(2,1)} %get-tuple-element.132), channel_id=1, source_target_pairs={{0,4},{1,5},{2,6},{3,7},{4,0},{5,1},{6,2},{7,3},{8,12},{9,13},{10,... | collective-permute-start | bytes 1769480 | tf_op jit(solution)/shard_map/ppermute | solution.py:647
  192.5 20.0 %collective-permute-start.18 = (f32[8,3072]{1,0:T(8,128)}, f32[8,3072]{1,0:T(8,128)S(1)}, u32[]{:S(2)}, u32[]{:S(2)}) collective-permute-start(f32[8,3072]{1,0:T(8,128)} %small_rows.1), channel_id=1, source_target_pairs={{0,1},{1,0},{2,3},{3,2},{4,5},{5,4},{6,7},{7,6},{8,9},{9,8},{10,11... | collective-permute-start | bytes 294920 | tf_op jit(solution)/shard_map/ppermute | solution.py:647
  203.6 16.5 %collective-permute-start.15 = (bf16[4,24,3072]{2,1,0:T(8,128)(2,1)}, bf16[4,24,3072]{2,1,0:T(8,128)(2,1)S(1)}, u32[]{:S(2)}, u32[]{:S(2)}) collective-permute-start(bf16[4,24,3072]{2,1,0:T(8,128)(2,1)} %get-tuple-element.141), channel_id=1, source_target_pairs={{0,2},{1,3},{2,0},{3,1},{4,6},{5,7},{6,4},{7,5},{8,10},{9,11},{10,... | collective-permute-start | bytes 1769480 | tf_op jit(solution)/shard_map/ppermute | solution.py:647
  205.1 27.7 %collective-permute-start.16 = (bf16[4,24,3072]{2,1,0:T(8,128)(2,1)}, bf16[4,24,3072]{2,1,0:T(8,128)(2,1)S(1)}, u32[]{:S(2)}, u32[]{:S(2)}) collective-permute-start(bf16[4,24,3072]{2,1,0:T(8,128)(2,1)} %get-tuple-element.142), channel_id=1, source_target_pairs={{0,4},{1,5},{2,6},{3,7},{4,0},{5,1},{6,2},{7,3},{8,12},{9,13},{10,... | collective-permute-start | bytes 1769480 | tf_op jit(solution)/shard_map/ppermute | solution.py:647
  205.6 27.8 %collective-permute-start.17 = (bf16[4,24,3072]{2,1,0:T(8,128)(2,1)}, bf16[4,24,3072]{2,1,0:T(8,128)(2,1)S(1)}, u32[]{:S(2)}, u32[]{:S(2)}) collective-permute-start(bf16[4,24,3072]{2,1,0:T(8,128)(2,1)} %get-tuple-element.143), channel_id=1, source_target_pairs={{0,6},{1,7},{2,4},{3,5},{4,2},{5,3},{6,0},{7,1},{8,14},{9,15},{10,... | collective-permute-start | bytes 1769480 | tf_op jit(solution)/shard_map/ppermute | solution.py:647
  211.0 32.4 %collective-permute-start.25 = (bf16[2,96,768]{2,1,0:T(8,128)(2,1)}, bf16[2,96,768]{2,1,0:T(8,128)(2,1)S(1)}, u32[]{:S(2)}, u32[]{:S(2)}) collective-permute-start(bf16[2,96,768]{2,1,0:T(8,128)(2,1)} %get-tuple-element.146), channel_id=1, source_target_pairs={{0,8},{1,9},{2,10},{3,11},{4,12},{5,13},{6,14},{7,15},{8,16},{9,17... | collective-permute-start | bytes 884744 | tf_op jit(solution)/shard_map/ppermute | solution.py:647
  213.1 22.2 %collective-permute-start.21 = (bf16[8,3072]{1,0:T(8,128)(2,1)S(1)}, bf16[8,3072]{1,0:T(8,128)(2,1)S(1)}, u32[]{:S(2)}, u32[]{:S(2)}) collective-permute-start(bf16[8,3072]{1,0:T(8,128)(2,1)S(1)} %get-tuple-element.171), channel_id=1, source_target_pairs={{0,6},{1,7},{2,4},{3,5},{4,2},{5,3},{6,0},{7,1},{8,14},{9,15},{10,... | collective-permute-start | bytes 147464 | tf_op jit(solution)/shard_map/ppermute | solution.py:647
  220.1 17.1 %collective-permute-start.20 = (bf16[8,3072]{1,0:T(8,128)(2,1)S(1)}, bf16[8,3072]{1,0:T(8,128)(2,1)S(1)}, u32[]{:S(2)}, u32[]{:S(2)}) collective-permute-start(bf16[8,3072]{1,0:T(8,128)(2,1)S(1)} %get-tuple-element.171), channel_id=1, source_target_pairs={{0,4},{1,5},{2,6},{3,7},{4,0},{5,1},{6,2},{7,3},{8,12},{9,13},{10,... | collective-permute-start | bytes 147464 | tf_op jit(solution)/shard_map/ppermute | solution.py:647
  233.4 19.3 %collective-permute-start.26 = (bf16[2,96,768]{2,1,0:T(8,128)(2,1)}, bf16[2,96,768]{2,1,0:T(8,128)(2,1)S(1)}, u32[]{:S(2)}, u32[]{:S(2)}) collective-permute-start(bf16[2,96,768]{2,1,0:T(8,128)(2,1)} %get-tuple-element.147), channel_id=1, source_target_pairs={{0,16},{1,17},{2,18},{3,19},{4,20},{5,21},{6,22},{7,23},{8,24},{9,... | collective-permute-start | bytes 884744 | tf_op jit(solution)/shard_map/ppermute | solution.py:647
  235.3 17.4 %collective-permute-start.27 = (bf16[2,96,768]{2,1,0:T(8,128)(2,1)}, bf16[2,96,768]{2,1,0:T(8,128)(2,1)S(1)}, u32[]{:S(2)}, u32[]{:S(2)}) collective-permute-start(bf16[2,96,768]{2,1,0:T(8,128)(2,1)} %get-tuple-element.148), channel_id=1, source_target_pairs={{0,24},{1,25},{2,26},{3,27},{4,28},{5,29},{6,30},{7,31},{8,0},{9,1... | collective-permute-start | bytes 884744 | tf_op jit(solution)/shard_map/ppermute | solution.py:647
  241.3 16.1 %collective-permute-start.22 = (bf16[32,3072]{1,0:T(8,128)(2,1)}, bf16[32,3072]{1,0:T(8,128)(2,1)S(1)}, u32[]{:S(2)}, u32[]{:S(2)}) collective-permute-start(bf16[32,3072]{1,0:T(8,128)(2,1)} %get-tuple-element.155), channel_id=1, source_target_pairs={{0,8},{1,9},{2,10},{3,11},{4,12},{5,13},{6,14},{7,15},{8,16},{9,17... | collective-permute-start | bytes 589832 | tf_op jit(solution)/shard_map/ppermute | solution.py:647
  242.3 23.3 %collective-permute-start.23 = (bf16[32,3072]{1,0:T(8,128)(2,1)}, bf16[32,3072]{1,0:T(8,128)(2,1)S(1)}, u32[]{:S(2)}, u32[]{:S(2)}) collective-permute-start(bf16[32,3072]{1,0:T(8,128)(2,1)} %get-tuple-element.156), channel_id=1, source_target_pairs={{0,16},{1,17},{2,18},{3,19},{4,20},{5,21},{6,22},{7,23},{8,24},{9,... | collective-permute-start | bytes 589832 | tf_op jit(solution)/shard_map/ppermute | solution.py:647
  243.4 22.3 %collective-permute-start.24 = (bf16[32,3072]{1,0:T(8,128)(2,1)}, bf16[32,3072]{1,0:T(8,128)(2,1)S(1)}, u32[]{:S(2)}, u32[]{:S(2)}) collective-permute-start(bf16[32,3072]{1,0:T(8,128)(2,1)} %get-tuple-element.157), channel_id=1, source_target_pairs={{0,24},{1,25},{2,26},{3,27},{4,28},{5,29},{6,30},{7,31},{8,0},{9,1... | collective-permute-start | bytes 589832 | tf_op jit(solution)/shard_map/ppermute | solution.py:647
  (36 other events, 175.2 us)
Sparse Core Ops, SparseCore 0:
  11.5 93.9 all-gather.2

commit v3 on v2

--- a/solution.py
+++ b/solution.py
@@ -182,10 +182,11 @@
     inv_ref,
     mixed_ref,
     gm_ref,
+    top_ref,
     dw_mine_ref,
     dw_other_ref,
     dqkv_ref,
-    dbias_ref,
+    small_ref,
     probs_ref,
     gs_ref,
     diag_ref,
@@ -193,6 +194,11 @@
     length, pair = val_ref.shape
     size = pair // 2
     blocks = length // BLK
+
+    @pl.when(pl.program_id(0) == 0)
+    def _():
+        small_ref[...] = top_ref[...]
+
     gm = gm_ref[...].astype(f32)
     scaled = gm * inv_ref[...]
     g_high, g_low = split_low(scaled)
@@ -247,8 +253,13 @@
         f_high, rest = split_low(jnp.concatenate(split, axis=0))
         f_mid, f_low = split_low(jnp.concatenate(split, axis=0) - f_high.astype(f32))
         turned = dot(jnp.concatenate([f_high, f_mid, f_low], axis=1), turn_ref[...])
-        for n in range(len(split)):
-            dbias_ref[h : h + 1, n * BLK : (n + 1) * BLK] = turned[len(split) - 1 - n][None]
+        turned = [turned[n : n + 1] for n in reversed(range(len(split)))]
+        head = 2 * pl.program_id(0) + h
+        rels = table_ref.shape[2]
+        per_row = small_ref.shape[1] // rels
+        column = pl.multiple_of(lax.rem(head, per_row) * rels, rels)
+        row = small_ref.shape[0] - pl.num_programs(0) * 2 // per_row + head // per_row
+        small_ref[pl.ds(row, 1), pl.ds(column, rels)] = jnp.concatenate(turned, axis=1)
     gk = jnp.concatenate(gk_heads, axis=0).T
     gv = jnp.concatenate(gv_heads, axis=0).T.astype(bf16)
     u = u_ref[...]
@@ -279,25 +290,24 @@
     inverse,
     mixed,
     grad_mixed,
+    small_top,
     heads,
-    first,
-    count,
 ):
     width, length = tokens_t.shape
     pair = 2 * width // heads
     rels = tables.shape[2]
     scale = float((pair // 2) ** (-0.25))
     whole = lambda shape: pl.BlockSpec(shape, lambda h, p: (0,) * len(shape))
-    column = lambda cols: pl.BlockSpec((length, cols), lambda h, p: (0, h + first))
+    column = lambda cols: pl.BlockSpec((length, cols), lambda h, p: (0, h))
     own_column = lambda rows: pl.BlockSpec((rows, 3 * pair), lambda h, p: (0, h))
     return pl.pallas_call(
         partial(attend_back_kernel, scale),
         grid_spec=pltpu.PrefetchScalarGridSpec(
             num_scalar_prefetch=1,
-            grid=(count,),
+            grid=(heads // 2,),
             in_specs=[
                 whole((width, length)),
-                pl.BlockSpec((2, BLK, rels), lambda h, p: (h + first, 0, 0)),
+                pl.BlockSpec((2, BLK, rels), lambda h, p: (h, 0, 0)),
                 whole(mask.shape),
                 whole(feat_back.shape),
                 whole(swap.shape),
@@ -308,12 +318,13 @@
                 column(pair),
                 column(pair),
                 column(pair),
+                whole(small_top.shape),
             ],
             out_specs=[
                 own_column(width // 2),
                 own_column(width // 2),
                 own_column(length),
-                pl.BlockSpec((None, 2, rels), lambda h, p: (h, 0, 0)),
+                whole(small_top.shape),
             ],
             scratch_shapes=[
                 pltpu.VMEM((length, length), bf16),
@@ -322,14 +333,14 @@
             ],
         ),
         out_shape=[
-            jax.ShapeDtypeStruct((width // 2, count * 3 * pair), bf16),
-            jax.ShapeDtypeStruct((width // 2, count * 3 * pair), bf16),
-            jax.ShapeDtypeStruct((length, count * 3 * pair), bf16),
-            jax.ShapeDtypeStruct((count, 2, rels), f32),
+            jax.ShapeDtypeStruct((width // 2, 3 * width), bf16),
+            jax.ShapeDtypeStruct((width // 2, 3 * width), bf16),
+            jax.ShapeDtypeStruct((length, 3 * width), bf16),
+            jax.ShapeDtypeStruct(small_top.shape, f32),
         ],
         cost_estimate=pl.CostEstimate(flops=0, bytes_accessed=0, transcendentals=0),
         name="attend_back",
-    )(place, tokens_t, tables, mask, feat_back, swap, turn, u, phi, value, inverse, mixed, grad_mixed)
+    )(place, tokens_t, tables, mask, feat_back, swap, turn, u, phi, value, inverse, mixed, grad_mixed, small_top)
 
 
 def block_diagonal(matrix):
@@ -442,8 +453,6 @@
     parts = pl.num_programs(1)
     length, width = tok_ref.shape
     rows, hidden = up_ref.shape[1:]
-    chunk = 256 if hidden % 256 == 0 else hidden
-    chunks = [slice(k, k + chunk) for k in range(0, hidden, chunk)]
     vec = vec_ref[...]
     down_bias, gain_one, shift_one, gain_two, shift_two = (vec[i : i + 1] for i in range(5))
 
@@ -461,15 +470,14 @@
 
     @pl.when(phase == 0)
     def _():
-        for cols in chunks:
-            up = up_ref[:, :, cols].reshape(width, chunk)
-            down = down_ref[:, :, cols].reshape(width, chunk)
-            v = dot(low_ref[...], up) + up_bias_ref[:, cols]
-            half = 0.5 + 0.5 * lax.erf(v * root_half)
-            act = (v * half).astype(bf16)
-            act_ref[part, :, cols] = act
-            slope_ref[part, :, cols] = half + v * (jnp.exp(-0.5 * v * v) * inv_root_two_pi)
-            acc_ref[...] += dot_nt(act, down)
+        up = up_ref[...].reshape(width, hidden)
+        down = down_ref[...].reshape(width, hidden)
+        v = dot(low_ref[...], up) + up_bias_ref[...]
+        half = 0.5 + 0.5 * lax.erf(v * root_half)
+        act = (v * half).astype(bf16)
+        act_ref[part] = act
+        slope_ref[part] = half + v * (jnp.exp(-0.5 * v * v) * inv_root_two_pi)
+        acc_ref[...] += dot_nt(act, down)
 
     @pl.when((phase == 0) & (part == parts - 1))
     def _():
@@ -488,17 +496,16 @@
         acc_ref[...] = grad_two
 
     def backward(d_up_ref, d_down_ref):
-        for cols in chunks:
-            up = up_ref[:, :, cols].reshape(width, chunk)
-            down = down_ref[:, :, cols].reshape(width, chunk)
-            grad_act = dot(gb_ref[...], down)
-            grad_hidden = (grad_act * slope_ref[part, :, cols]).astype(bf16)
-            dup_bias_ref[:, cols] = column_sum(grad_hidden.astype(f32))
-            d_up = dot(low_t_ref[...], grad_hidden).astype(bf16)
-            d_down = dot(gb_t_ref[...], act_ref[part, :, cols]).astype(bf16)
-            d_up_ref[:, :, cols] = d_up.reshape(-1, rows, chunk)
-            d_down_ref[:, :, cols] = d_down.reshape(-1, rows, chunk)
-            acc_ref[...] += dot_nt(grad_hidden, up)
+        up = up_ref[...].reshape(width, hidden)
+        down = down_ref[...].reshape(width, hidden)
+        grad_act = dot(gb_ref[...], down)
+        grad_hidden = (grad_act * slope_ref[part]).astype(bf16)
+        dup_bias_ref[...] = column_sum(grad_hidden.astype(f32))
+        d_up = dot(low_t_ref[...], grad_hidden).astype(bf16)
+        d_down = dot(gb_t_ref[...], act_ref[part]).astype(bf16)
+        d_up_ref[...] = d_up.reshape(-1, rows, hidden)
+        d_down_ref[...] = d_down.reshape(-1, rows, hidden)
+        acc_ref[...] += dot_nt(grad_hidden, up)
 
     @pl.when((phase == 1) & (part < parts // 2))
     def _():
@@ -711,8 +718,8 @@
             numbers += self.read([array], where + (None,) * (array.ndim - len(names)))
         return numbers
 
-    def write(self, shape, dtype, terms, stepped=False):
-        where = ("step",) + (None,) * (len(shape) - 1) if stepped else (None,) * len(shape)
+    def write(self, shape, dtype, terms, stepped=None):
+        where = tuple("step" if n == stepped else None for n in range(len(shape)))
         block = tuple(n if w is None else None for n, w in zip(shape, where))
         self.shapes.append(jax.ShapeDtypeStruct(shape, dtype))
         self.out_specs.append(self.spec(block, where))
@@ -838,25 +845,34 @@
     )
     ffn_view = lambda m: ("xzy", m.reshape(xs, zs, ys, up_rows, hidden))
     att_view = lambda m: ("zyx", m.reshape(zs, ys, xs, own, -1))
-    down = [ffn_view(down_mine), ffn_view(grid.shift(down_other, c=1))]
+    down_recv = grid.shift(down_other, c=1)
     up = [ffn_view(up_mine_grad), ffn_view(grid.shift(up_other_grad, c=1))]
     out = [att_view(out_mine), att_view(grid.shift(out_other, c=1))]
 
-    step = Combine(grid, 1)
+    columns = 4 * width
+    bias_rows = heads * rels // columns
+    extra = -(-(3 + bias_rows) // 8) * 8
+    first_row = extra - bias_rows
+    small_top = jnp.concatenate(
+        [dup_bias.reshape(1, columns), dvec.reshape(2, columns), jnp.zeros((extra - 3, columns), f32)]
+    )
+    down_mine, (small_top,) = hold(down_mine, small_top)
+    down = [ffn_view(down_mine), ffn_view(down_recv)]
+
+    step = Combine(grid, zs)
     for y in range(1, ys):
-        terms = [(everything, everything, step.add(down, dict(y=y)))]
-        step.write((xs, zs, up_rows, hidden), bf16, terms)
-    down_sends = step.run("down_sum_core")
-    step = Combine(grid, 1)
+        terms = [(everything, everything, step.add(down, dict(z="step", y=y)))]
+        step.write((xs, zs, up_rows, hidden), bf16, terms, stepped=1)
     for x in range(1, xs):
-        terms = [(everything, everything, step.add(up, dict(x=x)))]
-        step.write((zs, ys, up_rows, hidden), bf16, terms)
-    up_sends = step.run("up_sum_core")
+        terms = [(everything, everything, step.add(up, dict(z="step", x=x)))]
+        step.write((zs, ys, up_rows, hidden), bf16, terms, stepped=0)
+    sends = step.run("ffn_sum_core")
+    down_sends, up_sends = sends[: ys - 1], sends[ys - 1 :]
     grad_mixed, (down_sends, up_sends) = hold(grad_mixed, down_sends, up_sends)
     down_new = grid.send(down_sends, "y")
     up_new = grid.send(up_sends, "x")
 
-    dw_mine, dw_other, dqkv, dbias = attend_back(
+    dw_mine, dw_other, dqkv, small = attend_back(
         place,
         tokens_t,
         tables,
@@ -870,12 +886,11 @@
         inverse,
         mixed32,
         grad_mixed,
+        small_top,
         heads,
-        0,
-        pairs,
-    )
-    dw_mine, (dw_other, dqkv, dbias, down_new, up_new) = hold(
-        dw_mine, dw_other, dqkv, dbias, down_new, up_new
+    )
+    dw_mine, (dw_other, dqkv, small, down_new, up_new) = hold(
+        dw_mine, dw_other, dqkv, small, down_new, up_new
     )
     down += [("xz", v) for v in down_new]
     up += [("zy", v) for v in up_new]
@@ -890,40 +905,8 @@
         terms = [(everything, everything, step.add(up, dict(x=0, y=y)))]
         step.write(block, bf16, terms)
     sends = step.run("ffn_sum_plane")
-    dbias, sends = hold(dbias, *sends)
     down_new = grid.send(sends[: xs - 1], "x")
     up_new = grid.send(sends[xs - 1 :], "y")
-
-    columns = 4 * width
-    per_row = columns // rels
-    total_rows = 3 + heads // per_row
-    extra = -(-total_rows // 8) * 8
-    places = []
-    for w in range(wide):
-        places.append(("up", w, 0, slice(w * hidden, (w + 1) * hidden)))
-    for j in range(8):
-        places.append(("vec", j, 1 + j // 4, slice(j % 4 * width, (j % 4 + 1) * width)))
-    for h in range(heads):
-        places.append(
-            ("bias", h, 3 + h // per_row, slice(h % per_row * rels, (h % per_row + 1) * rels))
-        )
-    step = Combine(grid, 1)
-    ins = dict(
-        up=step.read([dup_bias], (None, None, None)),
-        vec=step.read([dvec], (None, None)),
-        bias=step.read([dbias], (None, None, None)),
-    )
-    sources = dict(
-        up=lambda n: (n,),
-        vec=lambda n: (slice(n, n + 1),),
-        bias=lambda n: (n // 2, slice(n % 2, n % 2 + 1)),
-    )
-    terms = [
-        ((slice(r, r + 1), cols), sources[kind](n), ins[kind])
-        for kind, n, r, cols in places
-    ]
-    step.write((extra, columns), f32, terms)
-    (small,) = step.run("small_rows")
     small = small + grid.shift(small, c=1)
     small = [small] + grid.send([small.astype(bf16)] * (ys * xs - 1), "yx")
     dw_mine, sends = hold(dw_mine, *sends)
@@ -936,7 +919,7 @@
         ]
         step.write((zs, own, columns), bf16, terms)
     att_sends = step.run("att_sum_core")
-    down_new, (up_new, att_sends) = hold(down_new, up_new, att_sends)
+    down_new, (up_new, att_sends, small) = hold(down_new, up_new, att_sends, small)
     down += [("z", v) for v in down_new]
     up += [("z", v) for v in up_new]
     att_new = grid.send(att_sends, "yx")
@@ -951,7 +934,8 @@
         step.write((2, up_rows, hidden), bf16, terms)
     sends = step.run("ffn_sum_second")
     ffn_new = grid.send(sends, "z")
-    att_new, sends = hold(att_new, *sends)
+    grad_tokens = grad_one + dot_nt(dqkv, attention_weights[:, : 3 * width])
+    att_new, (grad_tokens, *sends) = hold(att_new, grad_tokens, *sends)
     att_new = [("z", v) for v in att_new]
 
     step = Combine(grid, 1)
@@ -974,8 +958,6 @@
     att_sends = step.run("att_sum_plane")
     last = grid.send(att_sends, "z")
 
-    grad_tokens = grad_one + dot_nt(dqkv, attention_weights[:, : 3 * width])
-
     step = Combine(grid, 1)
     new = step.read(ffn_new, (None, None, None))
     for j, addends in enumerate((up, down)):
@@ -985,40 +967,40 @@
 
     step = Combine(grid, 1)
     new = step.add(att_new, here)
-    mine = step.add(att, here)
-    last = step.read(last, (None, None))
+    head = (slice(None), slice(0, 3 * width))
+    tail = (slice(None), slice(3 * width, None))
+    top = slice(0, own)
+    terms = [
+        ((top, head[1]), [(everything, step.add(att, here)), (head, new)]),
+        ((top, tail[1]), [(everything, step.add(out, here)), (tail, new)]),
+        ((slice(own, None),), everything, step.read(small, (None, None))),
+    ]
+    step.write((own + extra, columns), f32, terms)
+    (before,) = step.run("att_sum_own")
+
+    step = Combine(grid, 1)
+    last = step.read([before, *last], (None, None))
     for j in range(3):
         terms = []
         for p in range(pairs):
             cols = slice((3 * p + j) * lanes, (3 * p + j + 1) * lanes)
-            source = (slice(None), cols)
-            terms.append(
-                (
-                    (slice(None), slice(p * lanes, (p + 1) * lanes)),
-                    [(source, new + mine), ((slice(0, own), cols), last)],
-                )
-            )
+            terms.append(((slice(None), slice(p * lanes, (p + 1) * lanes)), (top, cols), last))
         step.write((own, width), f32, terms)
-    tail = slice(3 * width, None)
-    terms = [
-        (everything, step.add(out, here)),
-        ((slice(None), tail), new),
-        ((slice(0, own), tail), last),
-    ]
-    step.write((own, width), f32, [(everything, terms)])
-    small_in = step.read(small, (None, None))
+    step.write((own, width), f32, [(everything, (top, tail[1]), last)])
 
     def small_term(r, cols):
-        row = lambda base: (slice(base + r, base + r + 1), cols)
-        return [(row(0), small_in), (row(own), last)]
+        return [((slice(own + r, own + r + 1), cols), last)]
 
     step.write((columns,), f32, [(everything, small_term(0, slice(None)))])
+    for j in range(5):
+        at = j % 4 * width
+        step.write((width,), f32, [(everything, small_term(1 + j // 4, slice(at, at + width)))])
+    per_row = columns // rels
     terms = []
-    for kind, n, r, cols in places:
-        if kind == "vec" and n < 5:
-            step.write((width,), f32, [(everything, small_term(r, cols))])
-        if kind == "bias":
-            terms.append(((slice(n, n + 1),), small_term(r, cols)))
+    for h in range(heads):
+        at = h % per_row * rels
+        term = small_term(first_row + h // per_row, slice(at, at + rels))
+        terms.append(((slice(h, h + 1),), term))
     step.write((heads, rels), f32, terms)
     dq, dk, dv, out_own, dup_bias, *dvec, dbias = step.run("last_sum")
     return (

time: 278 us -> 264 us (0.950)
  waiting for transfers between devices: 74.8 us -> 62.9 us
  Pallas kernels: 113 us -> 108 us
    ppermute x28, waiting for transfers between devices: 71.3 us -> 59.5 us  [shift(): return lax.ppermute(value, ('batch', 'wide'), pairs)]
    pallas_call x9 -> x8, Pallas kernels: 31 us -> 28.9 us  [run(): pl.pallas_call(kernel, grid_spec=pltpu.PrefetchScalarGridSpec(num_scalar_...]
    unnamed x66 -> x62, local copies, waits for them, and re-layouts: 8.49 us -> 6.86 us
  transfers between devices with their start and end apart: 29 -> 29, of which waited for: 13 -> 13; matrix products, arithmetic and copies ran while one was open for 13% -> 15% of each run, Pallas kernels for 25% -> 26%
where the time goes in v3:
time: 264 us; the launch traced here: 262 us
  Pallas kernels  108 us (41%)
  waiting for transfers between devices  62.9 us (24%)
  starting transfers between devices  32.9 us (12%)
  local copies, waits for them, and re-layouts  23.9 us (9%)
  between operations  14.5 us (5%)
  other arithmetic  13.2 us (5%)
  matrix products  6.33 us (2%)
    ppermute x28, waiting for transfers between devices, shift(): return lax.ppermute(value, ('batch', 'wide'), pairs)  59.5 us
    ppermute x28, starting transfers between devices, shift(): return lax.ppermute(value, ('batch', 'wide'), pairs)  32.8 us
    pallas_call x1, Pallas kernels, feed_forward(): pl.pallas_call(ffn_kernel, grid_spec=pltpu.PrefetchScalarGridSpec(num_sca...  31.3 us
    pallas_call x8, Pallas kernels, run(): pl.pallas_call(kernel, grid_spec=pltpu.PrefetchScalarGridSpec(num_scalar_...  28.9 us
    pallas_call x1, Pallas kernels, attend_back(): pl.pallas_call(partial(attend_back_kernel, scale), grid_spec=pltpu.Prefet...  24.4 us
    pallas_call x1, Pallas kernels, attend(): pl.pallas_call(partial(attend_kernel, scale), grid=(pairs,), in_specs=[wh...  15.9 us
    unnamed x62, local copies, waits for them, and re-layouts  6.86 us
    dot_general x1, matrix products, dot_nt(): return lax.dot_general(a, b, nt_dims, preferred_element_type=f32)  6.33 us
  transfers between devices with their start and end apart: 29, of which 13 were waited for; matrix products, arithmetic and copies ran while one was open for 15% of the time, Pallas kernels for 26%

profile of v3, /device:TPU:0, one launch (start us, length us, event | category | flops | bytes accessed | tf_op | source)
XLA Modules:
  0.0 261.7 jit_solution(2129980043093332829)
XLA Ops:
  9.2 4.1 %collective-permute-start.1 = (bf16[1,1,1,1,24,3072]{5,4,3,2,1,0:T(8,128)(2,1)}, bf16[1,1,1,1,24,3072]{5,4,3,2,1,0:T(8,128)(2,1)S(1)}, u32[]{:S(2)}, u32[]{:S(2)}) collective-permute-start(bf16[1,1,1,1,24,3072]{5,4,3,2,1,0:T(8,128)(2,1)} %bitcast.89), channel_id=1, source_target_pairs={{0,16},{1,17},{2,18},{3,19},{4,20},{5,21},{6,22},{7,23},{8,24},{9,... | collective-permute-start | bytes 442376 | tf_op jit(solution)/shard_map/ppermute | solution.py:654
  18.0 3.1 %rev.6 = f32[12,1024]{1,0:T(8,128)S(1)} reverse(f32[12,1024]{1,0:T(8,128)} %param.25), dimensions={1} | reverse | bytes 98304 | tf_op jit(solution)/shard_map/rev | solution.py:798
  27.0 5.5 %toeplitz.1.table_ref = f32[12,128,1024]{2,1,0:T(8,128)} custom-call(f32[6,2,1024]{2,1,0:T(2,128)} %reshape.145.bias_ref), custom_call_target="tpu_custom_call" | custom-call | flops 5000000000 | bytes 8000000 | tf_op jit(solution)/shard_map/toeplitz/pallas_call | solution.py:41
  44.5 17.3 %collective-permute-done.3 = bf16[4,1,1,1,24,3072]{5,4,3,2,1,0:T(8,128)(2,1)} collective-permute-done((bf16[4,1,1,1,24,3072]{5,4,3,2,1,0:T(8,128)(2,1)}, bf16[4,1,1,1,24,3072]{5,4,3,2,1,0:T(8,128)(2,1)}, u32[]{:S(2)}, u32[]{:S(2)}) %collective-permute-start.3) | collective-permute-done | bytes 589856 | tf_op jit(solution)/shard_map/ppermute | solution.py:654
  63.0 10.3 %collective-permute-done.5 = bf16[4,1,1,1,24,3072]{5,4,3,2,1,0:T(8,128)(2,1)S(1)} collective-permute-done((bf16[4,1,1,1,24,3072]{5,4,3,2,1,0:T(8,128)(2,1)}, bf16[4,1,1,1,24,3072]{5,4,3,2,1,0:T(8,128)(2,1)S(1)}, u32[]{:S(2)}, u32[]{:S(2)}) %collective-permute-start.5) | collective-permute-done | bytes 589856 | tf_op jit(solution)/shard_map/ppermute | solution.py:654
  74.8 4.4 %collective-permute-done.6 = bf16[4,2,2,1,24,3072]{5,4,3,2,1,0:T(8,128)(2,1)} collective-permute-done((bf16[4,2,2,1,24,3072]{5,4,3,2,1,0:T(8,128)(2,1)S(1)}, bf16[4,2,2,1,24,3072]{5,4,3,2,1,0:T(8,128)(2,1)}, u32[]{:S(2)}, u32[]{:S(2)}) %collective-permute-start.6) | collective-permute-done | bytes 2359328 | tf_op jit(solution)/shard_map/ppermute | solution.py:654
  83.8 15.9 %attend.1 = (bf16[512,768]{1,0:T(8,128)(2,1)}, f32[512,768]{1,0:T(8,128)}, f32[512,1536]{1,0:T(8,128)}, f32[512,1536]{1,0:T(8,128)}, bf16[512,768]{1,0:T(8,128)(2,1)}, /*index=5*/f32[512,768]{1,0:T(8,128)}) custom-call(bf16[512,768]{1,0:T(8,128)(2,1)} %tok_ref.3, bf16[768,3072]{1,0:T(8,128)(2,1)} %bitcast.69, f32[12,128,1024]{2,1,0:T(8,128)} %toeplitz.1.table_ref, ...), custom_call_target="tpu_custom_call" | custom-call | tf_op jit(solution)/shard_map/attend/pallas_call | solution.py:131
  102.1 3.4 %all-gather.3.cloned.1.call-done = bf16[6144,768]{1,0:T(8,128)(2,1)} async-done(((bf16[192,768]{1,0:T(8,128)(2,1)}), bf16[6144,768]{1,0:T(8,128)(2,1)}) %all-gather.3.cloned.1.call-update) | async-done | bytes 9437200 | tf_op jit(solution)/shard_map/all_gather | solution.py:816
  105.5 31.3 %feed_forward.1 = (bf16[512,768]{1,0:T(8,128)(2,1)}, f32[512,768]{1,0:T(8,128)}, bf16[512,768]{1,0:T(8,128)(2,1)}, bf16[2,8,96,768]{3,2,1,0:T(8,128)(2,1)}, bf16...) custom-call(s32[1]{0:T(128)} %bitcast.place_ref, ...), custom_call_target="tpu_custom_call" | custom-call | tf_op jit(solution)/shard_map/feed_forward/pallas_call | solution.py:559
  142.4 2.7 %collective-permute-done.8 = bf16[2,8,96,768]{3,2,1,0:T(8,128)(2,1)} collective-permute-done((bf16[2,8,96,768]{3,2,1,0:T(8,128)(2,1)}, bf16[2,8,96,768]{3,2,1,0:T(8,128)(2,1)}, u32[]{:S(2)}, u32[]{:S(2)}) %collective-permute-start.8) | collective-permute-done | bytes 2359328 | tf_op jit(solution)/shard_map/ppermute | solution.py:654
  145.2 5.1 %ffn_sum_core.1 = (bf16[2,4,96,768]{3,2,1,0:T(8,128)(2,1)}, bf16[4,2,96,768]{3,2,1,0:T(8,128)(2,1)}) custom-call(s32[4]{0:T(128)} %pad_add_fusion.vector_ref, bf16[2,4,2,96,768]{4,3,2,1,0:T(8,128)(2,1)} %bitcast.57, bf16[2,4,2,96,768]{4,3,2,1,0:T(8,128)(2,1)} %bitcast.63, bf16[2,4,2,96,768]{4,3,2,1,0:T(8,128)(2,1)} %bitcast.51, ...), custom_call_target="tpu_custom_call" | custom-call | tf_op jit(solution)/shard_map/ffn_sum_core/pallas_call | solution.py:744
  152.3 24.4 %attend_back.1 = (bf16[384,2304]{1,0:T(8,128)(2,1)}, bf16[384,2304]{1,0:T(8,128)(2,1)}, bf16[512,2304]{1,0:T(8,128)(2,1)}, f32[8,3072]{1,0:T(8,128)}) custom-call(s32[1]{0:T(128)} %bitcast.place_ref, bf16[768,512]{1,0:T(8,128)(2,1)} %bitcast.81, f32[12,128,1024]{2,1,0:T(8,128)} %toeplitz.1.table_ref, f32[4,512]{1,0:T(4,128)} %compare_select_fusion.mask_ref, ...), custom_call_target="tpu_custom_call" | custom-call | tf_op jit(solution)/shard_map/attend_back/pallas_call | solution.py:303
  180.8 3.9 %ffn_sum_plane.1 = (bf16[4,96,768]{2,1,0:T(8,128)(2,1)}, bf16[4,96,768]{2,1,0:T(8,128)(2,1)}) custom-call(s32[4]{0:T(128)} %pad_add_fusion.vector_ref, bf16[2,4,2,96,768]{4,3,2,1,0:T(8,128)(2,1)} %bitcast.58, bf16[2,4,2,96,768]{4,3,2,1,0:T(8,128)(2,1)} %bitcast.64, bf16[2,4,96,768]{3,2,1,0:T(8,128)(2,1)} %copy-done.2, bf16[2,4,2,96,768]{4,3,2,1,0:T(8,128)(2,1)} %bitcast.52, ...), custom_call_target="tpu_custom_call" | custom-call | tf_op jit(solution)/shard_map/ffn_sum_plane/pallas_call | solution.py:744
  191.8 4.0 %att_sum_core.1 = (bf16[4,24,3072]{2,1,0:T(8,128)(2,1)}, bf16[4,24,3072]{2,1,0:T(8,128)(2,1)}, bf16[4,24,3072]{2,1,0:T(8,128)(2,1)}) custom-call(s32[4]{0:T(128)} %pad_add_fusion.vector_ref, bf16[4,2,2,24,2304]{4,3,2,1,0:T(8,128)(2,1)} %bitcast.37, bf16[4,2,2,24,2304]{4,3,2,1,0:T(8,128)(2,1)} %bitcast.44, bf16[4,2,2,24,768]{4,3,2,1,0:T(8,128)(2,1)} %bitcast.74, ...), custom_call_target="tpu_custom_call" | custom-call | tf_op jit(solution)/shard_map/att_sum_core/pallas_call | solution.py:744
  195.7 6.1 %collective-permute-done.18.refs_10_.refs_3_ = bf16[8,3072]{1,0:T(8,128)(2,1)S(1)} collective-permute-done((bf16[8,3072]{1,0:T(8,128)(2,1)S(1)}, bf16[8,3072]{1,0:T(8,128)(2,1)S(1)}, u32[]{:S(2)}, u32[]{:S(2)}) %collective-permute-start.18) | collective-permute-done | bytes 49184 | tf_op jit(solution)/shard_map/ppermute | solution.py:654
  206.1 3.9 %ffn_sum_second.1 = (bf16[2,96,768]{2,1,0:T(8,128)(2,1)}, bf16[2,96,768]{2,1,0:T(8,128)(2,1)}, bf16[2,96,768]{2,1,0:T(8,128)(2,1)}) custom-call(s32[4]{0:T(128)} %pad_add_fusion.vector_ref, bf16[2,4,2,96,768]{4,3,2,1,0:T(8,128)(2,1)} %bitcast.53, bf16[2,4,2,96,768]{4,3,2,1,0:T(8,128)(2,1)} %bitcast.25.refs_3_.refs_4_.refs_1_.refs_9_.refs_17_, ...), custom_call_target="tpu_custom_call" | custom-call | tf_op jit(solution)/shard_map/ffn_sum_second/pallas_call | solution.py:744
  212.6 6.6 %collective-permute-done.19.refs_0_.refs_4_.refs_11_.refs_18_ = bf16[4,24,3072]{2,1,0:T(8,128)(2,1)S(1)} collective-permute-done((bf16[4,24,3072]{2,1,0:T(8,128)(2,1)}, bf16[4,24,3072]{2,1,0:T(8,128)(2,1)S(1)}, u32[]{:S(2)}, u32[]{:S(2)}) %collective-permute-start.19) | collective-permute-done | bytes 589856 | tf_op jit(solution)/shard_map/ppermute | solution.py:654
  221.0 6.3 %fusion.9 = f32[512,768]{1,0:T(8,128)} fusion(f32[512,768]{1,0:T(8,128)} %get-tuple-element.152, bf16[512,2304]{1,0:T(8,128)(2,1)} %get-tuple-element.153, bf16[768,3072]{1,0:T(8,128)(2,1)} %bitcast.71), kind=kOutput, calls=%fused_computation.38 | convolution fusion | flops 1812332544 | bytes 9043968 | tf_op jit(solution)/shard_map/dot_general | solution.py:22
  227.4 2.9 %collective-permute-done.20.refs_1_.refs_5_.refs_12_.refs_19_ = bf16[4,24,3072]{2,1,0:T(8,128)(2,1)S(1)} collective-permute-done((bf16[4,24,3072]{2,1,0:T(8,128)(2,1)}, bf16[4,24,3072]{2,1,0:T(8,128)(2,1)S(1)}, u32[]{:S(2)}, u32[]{:S(2)}) %collective-permute-start.20) | collective-permute-done | bytes 589856 | tf_op jit(solution)/shard_map/ppermute | solution.py:654
  231.9 3.4 %att_sum_plane.1 = (bf16[32,3072]{1,0:T(8,128)(2,1)}, bf16[32,3072]{1,0:T(8,128)(2,1)}, bf16[32,3072]{1,0:T(8,128)(2,1)}) custom-call(s32[4]{0:T(128)} %pad_add_fusion.vector_ref, f32[8,3072]{1,0:T(8,128)} %get-tuple-element.163.refs_7_.refs_0_, bf16[8,3072]{1,0:T(8,128)(2,1)} %copy-done.17, bf16[8,3072]{1,0:T(8,128)(2,1)} %copy-done.16, ...), custom_call_target="tpu_custom_call" | custom-call | tf_op jit(solution)/shard_map/att_sum_plane/pallas_call | solution.py:744
  241.6 3.2 %ffn_sum_last.1 = (f32[96,768]{1,0:T(8,128)}, f32[96,768]{1,0:T(8,128)}) custom-call(s32[4]{0:T(128)} %pad_add_fusion.vector_ref, bf16[2,96,768]{2,1,0:T(8,128)(2,1)} %copy-done.10, bf16[2,96,768]{2,1,0:T(8,128)(2,1)} %copy-done.11, bf16[2,96,768]{2,1,0:T(8,128)(2,1)} %copy-done.12, bf16[2,4,2,96,768]{4,3,2,1,0:T(8,128)(2,1)} %bitcast.56, ...), custom_call_target="tpu_custom_call" | custom-call | tf_op jit(solution)/shard_map/ffn_sum_last/pallas_call | solution.py:744
  244.8 2.8 %att_sum_own.1.refs_0_ = f32[32,3072]{1,0:T(8,128)} custom-call(s32[4]{0:T(128)} %pad_add_fusion.vector_ref, bf16[4,24,3072]{2,1,0:T(8,128)(2,1)} %copy-done.4, bf16[4,24,3072]{2,1,0:T(8,128)(2,1)} %copy-done.5, bf16[4,24,3072]{2,1,0:T(8,128)(2,1)} %copy-done.6, bf16[4,2,2,24,2304]{4,3,2,1,0:T(8,128)(2,1)} %bitcast.43, ...), custom_call_target="tpu_custom_call" | custom-call | tf_op jit(solution)/shard_map/att_sum_own/pallas_call | solution.py:744
  247.6 3.2 %collective-permute-done.23.refs_2_ = bf16[32,3072]{1,0:T(8,128)(2,1)S(1)} collective-permute-done((bf16[32,3072]{1,0:T(8,128)(2,1)}, bf16[32,3072]{1,0:T(8,128)(2,1)S(1)}, u32[]{:S(2)}, u32[]{:S(2)}) %collective-permute-start.23) | collective-permute-done | bytes 196640 | tf_op jit(solution)/shard_map/ppermute | solution.py:654
  252.2 2.7 %last_sum.1 = (f32[24,768]{1,0:T(8,128)}, f32[24,768]{1,0:T(8,128)}, f32[24,768]{1,0:T(8,128)}, f32[24,768]{1,0:T(8,128)}, f32[3072]{0:T(1024)}, /*index=5*/f32[...) custom-call(s32[4]{0:T(128)} %pad_add_fusion.vector_ref, ...), custom_call_target="tpu_custom_call" | custom-call | tf_op jit(solution)/shard_map/last_sum/pallas_call | solution.py:744
  (154 shorter events, 70.7 us)
Async XLA Ops:
  7.2 98.3 %all-gather.3.cloned.1.call-start = ((), (), s32[]{:S(2)}) async-start(), calls=%async_computation | async-start | bytes 9732096 | tf_op jit(solution)/shard_map/all_gather | solution.py:816
  9.2 26.2 %collective-permute-start.1 = (bf16[1,1,1,1,24,3072]{5,4,3,2,1,0:T(8,128)(2,1)}, bf16[1,1,1,1,24,3072]{5,4,3,2,1,0:T(8,128)(2,1)S(1)}, u32[]{:S(2)}, u32[]{:S(2)}) collective-permute-start(bf16[1,1,1,1,24,3072]{5,4,3,2,1,0:T(8,128)(2,1)} %bitcast.89), channel_id=1, source_target_pairs={{0,16},{1,17},{2,18},{3,19},{4,20},{5,21},{6,22},{7,23},{8,24},{9,... | collective-permute-start | bytes 442376 | tf_op jit(solution)/shard_map/ppermute | solution.py:654
  13.3 21.5 %collective-permute-start = (bf16[1,1,1,1,24,3072]{5,4,3,2,1,0:T(8,128)(2,1)}, bf16[1,1,1,1,24,3072]{5,4,3,2,1,0:T(8,128)(2,1)S(1)}, u32[]{:S(2)}, u32[]{:S(2)}) collective-permute-start(bf16[1,1,1,1,24,3072]{5,4,3,2,1,0:T(8,128)(2,1)} %bitcast.90), channel_id=1, source_target_pairs={{0,8},{1,9},{2,10},{3,11},{4,12},{5,13},{6,14},{7,15},{8,16},{9,17... | collective-permute-start | bytes 442376 | tf_op jit(solution)/shard_map/ppermute | solution.py:654
  14.9 21.2 %collective-permute-start.2 = (bf16[1,1,1,1,24,3072]{5,4,3,2,1,0:T(8,128)(2,1)}, bf16[1,1,1,1,24,3072]{5,4,3,2,1,0:T(8,128)(2,1)S(1)}, u32[]{:S(2)}, u32[]{:S(2)}) collective-permute-start(bf16[1,1,1,1,24,3072]{5,4,3,2,1,0:T(8,128)(2,1)} %bitcast.91), channel_id=1, source_target_pairs={{0,24},{1,25},{2,26},{3,27},{4,28},{5,29},{6,30},{7,31},{8,0},{9,1... | collective-permute-start | bytes 442376 | tf_op jit(solution)/shard_map/ppermute | solution.py:654
  36.8 25.0 %collective-permute-start.3 = (bf16[4,1,1,1,24,3072]{5,4,3,2,1,0:T(8,128)(2,1)}, bf16[4,1,1,1,24,3072]{5,4,3,2,1,0:T(8,128)(2,1)}, u32[]{:S(2)}, u32[]{:S(2)}) collective-permute-start(bf16[4,1,1,1,24,3072]{5,4,3,2,1,0:T(8,128)(2,1)} %constant_dynamic-update-slice_fusion.9), channel_id=1, source_target_pairs={{0,2},{1,3},{2,0},{3,1},{4,6},{5,7},{6,4},{7,5},{8,10},{9,11},{10,... | collective-permute-start | bytes 1769480 | tf_op jit(solution)/shard_map/ppermute | solution.py:654
  41.1 32.2 %collective-permute-start.5 = (bf16[4,1,1,1,24,3072]{5,4,3,2,1,0:T(8,128)(2,1)}, bf16[4,1,1,1,24,3072]{5,4,3,2,1,0:T(8,128)(2,1)S(1)}, u32[]{:S(2)}, u32[]{:S(2)}) collective-permute-start(bf16[4,1,1,1,24,3072]{5,4,3,2,1,0:T(8,128)(2,1)} %constant_dynamic-update-slice_fusion.9), channel_id=1, source_target_pairs={{0,6},{1,7},{2,4},{3,5},{4,2},{5,3},{6,0},{7,1},{8,14},{9,15},{10,... | collective-permute-start | bytes 1769480 | tf_op jit(solution)/shard_map/ppermute | solution.py:654
  42.6 20.4 %collective-permute-start.4 = (bf16[4,1,1,1,24,3072]{5,4,3,2,1,0:T(8,128)(2,1)}, bf16[4,1,1,1,24,3072]{5,4,3,2,1,0:T(8,128)(2,1)S(1)}, u32[]{:S(2)}, u32[]{:S(2)}) collective-permute-start(bf16[4,1,1,1,24,3072]{5,4,3,2,1,0:T(8,128)(2,1)} %constant_dynamic-update-slice_fusion.9), channel_id=1, source_target_pairs={{0,4},{1,5},{2,6},{3,7},{4,0},{5,1},{6,2},{7,3},{8,12},{9,13},{10,... | collective-permute-start | bytes 1769480 | tf_op jit(solution)/shard_map/ppermute | solution.py:654
  150.3 28.3 %collective-permute-start.9 = (bf16[2,4,96,768]{3,2,1,0:T(8,128)(2,1)}, bf16[2,4,96,768]{3,2,1,0:T(8,128)(2,1)S(1)}, u32[]{:S(2)}, u32[]{:S(2)}) collective-permute-start(bf16[2,4,96,768]{3,2,1,0:T(8,128)(2,1)} %get-tuple-element.134), channel_id=1, source_target_pairs={{0,4},{1,5},{2,6},{3,7},{4,0},{5,1},{6,2},{7,3},{8,12},{9,13},{10,... | collective-permute-start | bytes 3538952 | tf_op jit(solution)/shard_map/ppermute | solution.py:654
  151.7 28.1 %collective-permute-start.10 = (bf16[4,2,96,768]{3,2,1,0:T(8,128)(2,1)}, bf16[4,2,96,768]{3,2,1,0:T(8,128)(2,1)S(1)}, u32[]{:S(2)}, u32[]{:S(2)}) collective-permute-start(bf16[4,2,96,768]{3,2,1,0:T(8,128)(2,1)} %get-tuple-element.135), channel_id=1, source_target_pairs={{0,2},{1,3},{2,0},{3,1},{4,6},{5,7},{6,4},{7,5},{8,10},{9,11},{10,... | collective-permute-start | bytes 3538952 | tf_op jit(solution)/shard_map/ppermute | solution.py:654
  179.8 10.7 %collective-permute-start.13 = (bf16[384,2304]{1,0:T(8,128)(2,1)}, bf16[384,2304]{1,0:T(8,128)(2,1)S(1)}, u32[]{:S(2)}, u32[]{:S(2)}) collective-permute-start(bf16[384,2304]{1,0:T(8,128)(2,1)} %get-tuple-element.142), channel_id=1, source_target_pairs={{0,1},{1,0},{2,3},{3,2},{4,5},{5,4},{6,7},{7,6},{8,9},{9,8},{10,11... | collective-permute-start | bytes 5308424 | tf_op jit(solution)/shard_map/ppermute | solution.py:654
  184.7 17.9 %collective-permute-start.11 = (bf16[4,96,768]{2,1,0:T(8,128)(2,1)}, bf16[4,96,768]{2,1,0:T(8,128)(2,1)S(1)}, u32[]{:S(2)}, u32[]{:S(2)}) collective-permute-start(bf16[4,96,768]{2,1,0:T(8,128)(2,1)} %get-tuple-element.138), channel_id=1, source_target_pairs={{0,2},{1,3},{2,0},{3,1},{4,6},{5,7},{6,4},{7,5},{8,10},{9,11},{10,... | collective-permute-start | bytes 1769480 | tf_op jit(solution)/shard_map/ppermute | solution.py:654
  185.3 17.3 %collective-permute-start.12 = (bf16[4,96,768]{2,1,0:T(8,128)(2,1)}, bf16[4,96,768]{2,1,0:T(8,128)(2,1)S(1)}, u32[]{:S(2)}, u32[]{:S(2)}) collective-permute-start(bf16[4,96,768]{2,1,0:T(8,128)(2,1)} %get-tuple-element.139), channel_id=1, source_target_pairs={{0,4},{1,5},{2,6},{3,7},{4,0},{5,1},{6,2},{7,3},{8,12},{9,13},{10,... | collective-permute-start | bytes 1769480 | tf_op jit(solution)/shard_map/ppermute | solution.py:654
  188.3 13.6 %collective-permute-start.18 = (bf16[8,3072]{1,0:T(8,128)(2,1)S(1)}, bf16[8,3072]{1,0:T(8,128)(2,1)S(1)}, u32[]{:S(2)}, u32[]{:S(2)}) collective-permute-start(bf16[8,3072]{1,0:T(8,128)(2,1)S(1)} %get-tuple-element.183), channel_id=1, source_target_pairs={{0,6},{1,7},{2,4},{3,5},{4,2},{5,3},{6,0},{7,1},{8,14},{9,15},{10,... | collective-permute-start | bytes 147464 | tf_op jit(solution)/shard_map/ppermute | solution.py:654
  189.8 12.8 %collective-permute-start.17 = (bf16[8,3072]{1,0:T(8,128)(2,1)S(1)}, bf16[8,3072]{1,0:T(8,128)(2,1)S(1)}, u32[]{:S(2)}, u32[]{:S(2)}) collective-permute-start(bf16[8,3072]{1,0:T(8,128)(2,1)S(1)} %get-tuple-element.183), channel_id=1, source_target_pairs={{0,4},{1,5},{2,6},{3,7},{4,0},{5,1},{6,2},{7,3},{8,12},{9,13},{10,... | collective-permute-start | bytes 147464 | tf_op jit(solution)/shard_map/ppermute | solution.py:654
  190.5 12.1 %collective-permute-start.16 = (bf16[8,3072]{1,0:T(8,128)(2,1)S(1)}, bf16[8,3072]{1,0:T(8,128)(2,1)S(1)}, u32[]{:S(2)}, u32[]{:S(2)}) collective-permute-start(bf16[8,3072]{1,0:T(8,128)(2,1)S(1)} %get-tuple-element.183), channel_id=1, source_target_pairs={{0,2},{1,3},{2,0},{3,1},{4,6},{5,7},{6,4},{7,5},{8,10},{9,11},{10,... | collective-permute-start | bytes 147464 | tf_op jit(solution)/shard_map/ppermute | solution.py:654
  202.6 16.5 %collective-permute-start.19 = (bf16[4,24,3072]{2,1,0:T(8,128)(2,1)}, bf16[4,24,3072]{2,1,0:T(8,128)(2,1)S(1)}, u32[]{:S(2)}, u32[]{:S(2)}) collective-permute-start(bf16[4,24,3072]{2,1,0:T(8,128)(2,1)} %get-tuple-element.149), channel_id=1, source_target_pairs={{0,2},{1,3},{2,0},{3,1},{4,6},{5,7},{6,4},{7,5},{8,10},{9,11},{10,... | collective-permute-start | bytes 1769480 | tf_op jit(solution)/shard_map/ppermute | solution.py:654
  204.1 26.1 %collective-permute-start.20 = (bf16[4,24,3072]{2,1,0:T(8,128)(2,1)}, bf16[4,24,3072]{2,1,0:T(8,128)(2,1)S(1)}, u32[]{:S(2)}, u32[]{:S(2)}) collective-permute-start(bf16[4,24,3072]{2,1,0:T(8,128)(2,1)} %get-tuple-element.150), channel_id=1, source_target_pairs={{0,4},{1,5},{2,6},{3,7},{4,0},{5,1},{6,2},{7,3},{8,12},{9,13},{10,... | collective-permute-start | bytes 1769480 | tf_op jit(solution)/shard_map/ppermute | solution.py:654
  204.7 25.6 %collective-permute-start.21 = (bf16[4,24,3072]{2,1,0:T(8,128)(2,1)}, bf16[4,24,3072]{2,1,0:T(8,128)(2,1)S(1)}, u32[]{:S(2)}, u32[]{:S(2)}) collective-permute-start(bf16[4,24,3072]{2,1,0:T(8,128)(2,1)} %get-tuple-element.151), channel_id=1, source_target_pairs={{0,6},{1,7},{2,4},{3,5},{4,2},{5,3},{6,0},{7,1},{8,14},{9,15},{10,... | collective-permute-start | bytes 1769480 | tf_op jit(solution)/shard_map/ppermute | solution.py:654
  210.0 27.7 %collective-permute-start.25 = (bf16[2,96,768]{2,1,0:T(8,128)(2,1)}, bf16[2,96,768]{2,1,0:T(8,128)(2,1)S(1)}, u32[]{:S(2)}, u32[]{:S(2)}) collective-permute-start(bf16[2,96,768]{2,1,0:T(8,128)(2,1)} %get-tuple-element.156), channel_id=1, source_target_pairs={{0,8},{1,9},{2,10},{3,11},{4,12},{5,13},{6,14},{7,15},{8,16},{9,17... | collective-permute-start | bytes 884744 | tf_op jit(solution)/shard_map/ppermute | solution.py:654
  211.6 28.6 %collective-permute-start.26 = (bf16[2,96,768]{2,1,0:T(8,128)(2,1)}, bf16[2,96,768]{2,1,0:T(8,128)(2,1)S(1)}, u32[]{:S(2)}, u32[]{:S(2)}) collective-permute-start(bf16[2,96,768]{2,1,0:T(8,128)(2,1)} %get-tuple-element.157), channel_id=1, source_target_pairs={{0,16},{1,17},{2,18},{3,19},{4,20},{5,21},{6,22},{7,23},{8,24},{9,... | collective-permute-start | bytes 884744 | tf_op jit(solution)/shard_map/ppermute | solution.py:654
  219.1 21.1 %collective-permute-start.27 = (bf16[2,96,768]{2,1,0:T(8,128)(2,1)}, bf16[2,96,768]{2,1,0:T(8,128)(2,1)S(1)}, u32[]{:S(2)}, u32[]{:S(2)}) collective-permute-start(bf16[2,96,768]{2,1,0:T(8,128)(2,1)} %get-tuple-element.158), channel_id=1, source_target_pairs={{0,24},{1,25},{2,26},{3,27},{4,28},{5,29},{6,30},{7,31},{8,0},{9,1... | collective-permute-start | bytes 884744 | tf_op jit(solution)/shard_map/ppermute | solution.py:654
  235.3 12.3 %collective-permute-start.22 = (bf16[32,3072]{1,0:T(8,128)(2,1)}, bf16[32,3072]{1,0:T(8,128)(2,1)S(1)}, u32[]{:S(2)}, u32[]{:S(2)}) collective-permute-start(bf16[32,3072]{1,0:T(8,128)(2,1)} %get-tuple-element.167), channel_id=1, source_target_pairs={{0,8},{1,9},{2,10},{3,11},{4,12},{5,13},{6,14},{7,15},{8,16},{9,17... | collective-permute-start | bytes 589832 | tf_op jit(solution)/shard_map/ppermute | solution.py:654
  236.8 14.0 %collective-permute-start.23 = (bf16[32,3072]{1,0:T(8,128)(2,1)}, bf16[32,3072]{1,0:T(8,128)(2,1)S(1)}, u32[]{:S(2)}, u32[]{:S(2)}) collective-permute-start(bf16[32,3072]{1,0:T(8,128)(2,1)} %get-tuple-element.168), channel_id=1, source_target_pairs={{0,16},{1,17},{2,18},{3,19},{4,20},{5,21},{6,22},{7,23},{8,24},{9,... | collective-permute-start | bytes 589832 | tf_op jit(solution)/shard_map/ppermute | solution.py:654
  237.8 13.0 %collective-permute-start.24 = (bf16[32,3072]{1,0:T(8,128)(2,1)}, bf16[32,3072]{1,0:T(8,128)(2,1)S(1)}, u32[]{:S(2)}, u32[]{:S(2)}) collective-permute-start(bf16[32,3072]{1,0:T(8,128)(2,1)} %get-tuple-element.169), channel_id=1, source_target_pairs={{0,24},{1,25},{2,26},{3,27},{4,28},{5,29},{6,30},{7,31},{8,0},{9,1... | collective-permute-start | bytes 589832 | tf_op jit(solution)/shard_map/ppermute | solution.py:654
  (34 other events, 158.4 us)
Sparse Core Ops, SparseCore 0:
  11.5 93.9 all-gather.2

commit v4 on v3

--- a/solution.py
+++ b/solution.py
@@ -367,7 +367,21 @@
     return forward, backward, jnp.concatenate([swap, swap], axis=0), jnp.tile(turn, (3, 1))
 
 
-def prepare_kernel(q_ref, k_ref, v_ref, o_ref, up_ref, down_ref, att_ref, ffn_ref):
+def prepare_ffn_kernel(up_ref, down_ref, ffn_ref):
+    rows = up_ref.shape[0]
+    ffn_ref[:rows] = up_ref[...].astype(bf16)
+    ffn_ref[rows:] = down_ref[...].astype(bf16)
+
+
+def prepare_ffn(up, down):
+    return pl.pallas_call(
+        prepare_ffn_kernel,
+        out_shape=jax.ShapeDtypeStruct((2 * up.shape[0], up.shape[1]), bf16),
+        name="prepare_ffn",
+    )(up, down)
+
+
+def prepare_kernel(q_ref, k_ref, v_ref, o_ref, att_ref):
     width = o_ref.shape[1]
     lanes = att_ref.shape[1] // 4 // (width // 128)
     for j, ref in enumerate((q_ref, k_ref, v_ref)):
@@ -375,21 +389,15 @@
             to = (3 * p + j) * lanes
             att_ref[:, to : to + lanes] = ref[:, p * lanes : (p + 1) * lanes].astype(bf16)
     att_ref[:, 3 * width :] = o_ref[...].astype(bf16)
-    rows = up_ref.shape[0]
-    ffn_ref[:rows] = up_ref[...].astype(bf16)
-    ffn_ref[rows:] = down_ref[...].astype(bf16)
-
-
-def prepare(query, key, value, out, up, down):
+
+
+def prepare(query, key, value, out):
     own, width = query.shape
     return pl.pallas_call(
         prepare_kernel,
-        out_shape=[
-            jax.ShapeDtypeStruct((own, 4 * width), bf16),
-            jax.ShapeDtypeStruct((2 * up.shape[0], up.shape[1]), bf16),
-        ],
+        out_shape=jax.ShapeDtypeStruct((own, 4 * width), bf16),
         name="prepare",
-    )(query, key, value, out, up, down)
+    )(query, key, value, out)
 
 
 root_half = 0.7071067811865476
@@ -416,10 +424,9 @@
 
 def ffn_kernel(
     place_ref,
-    tok_ref,
-    mixed_ref,
-    mixed_t_ref,
-    wo_ref,
+    low_ref,
+    low_t_ref,
+    xhat_ref,
     up_ref,
     down_ref,
     up_bias_ref,
@@ -427,45 +434,28 @@
     live_ref,
     cot_ref,
     out_ref,
-    grad_one_ref,
-    gm_ref,
+    acc_ref,
     up_other_ref,
     up_mine_ref,
     down_other_ref,
     down_mine_ref,
-    wo_other_ref,
-    wo_mine_ref,
     dup_bias_ref,
     dvec_ref,
-    normed_ref,
-    low_ref,
-    low_t_ref,
-    xhat_ref,
-    inv_ref,
     act_ref,
     slope_ref,
-    acc_ref,
     gb_ref,
     gb_t_ref,
 ):
     phase = pl.program_id(0)
     part = pl.program_id(1)
     parts = pl.num_programs(1)
-    length, width = tok_ref.shape
+    length, width = low_ref.shape
     rows, hidden = up_ref.shape[1:]
     vec = vec_ref[...]
     down_bias, gain_one, shift_one, gain_two, shift_two = (vec[i : i + 1] for i in range(5))
 
     @pl.when((phase == 0) & (part == 0))
     def _():
-        residual = tok_ref[...].astype(f32) + dot(mixed_ref[...], wo_ref[...])
-        xhat, inverse = norm_stats(residual)
-        normed = xhat * gain_one + shift_one
-        xhat_ref[...] = xhat
-        inv_ref[...] = inverse
-        normed_ref[...] = normed
-        low_ref[...] = normed.astype(bf16)
-        low_t_ref[...] = normed.T.astype(bf16)
         acc_ref[...] = jnp.zeros_like(acc_ref)
 
     @pl.when(phase == 0)
@@ -482,7 +472,8 @@
     @pl.when((phase == 0) & (part == parts - 1))
     def _():
         live = live_ref[...]
-        xhat, inverse = norm_stats(normed_ref[...] + (acc_ref[...] + down_bias))
+        normed = xhat_ref[...] * gain_one + shift_one
+        xhat, inverse = norm_stats(normed + (acc_ref[...] + down_bias))
         out_ref[...] = ((xhat * gain_two + shift_two) * live).astype(bf16)
         grad = cot_ref[...].astype(f32) * live
         grad_two = norm_back(grad, xhat, inverse, gain_two)
@@ -492,6 +483,7 @@
         dvec_ref[0:1, :] = column_sum(low.astype(f32))
         dvec_ref[3:4, :] = column_sum(grad * xhat)
         dvec_ref[4:5, :] = column_sum(grad)
+        dvec_ref[1:3, :] = jnp.zeros((2, width), f32)
         dvec_ref[5:8, :] = jnp.zeros((3, width), f32)
         acc_ref[...] = grad_two
 
@@ -515,28 +507,95 @@
     def _():
         backward(up_mine_ref, down_mine_ref)
 
-    @pl.when((phase == 1) & (part == parts - 1))
-    def _():
-        grad = acc_ref[...]
-        xhat = xhat_ref[...]
-        grad_one = norm_back(grad, xhat, inv_ref[...], gain_one)
-        grad_one_ref[...] = grad_one
-        grad_att = grad_one.astype(bf16)
-        gm_ref[...] = dot_nt(grad_att, wo_ref[...]).astype(bf16)
-        half = width // 2
-        place = place_ref[0]
-        mine = pl.ds(pl.multiple_of(place * half, half), half)
-        other = pl.ds(pl.multiple_of((1 - place) * half, half), half)
-        wo_mine_ref[...] = dot(mixed_t_ref[mine, :], grad_att).astype(bf16)
-        wo_other_ref[...] = dot(mixed_t_ref[other, :], grad_att).astype(bf16)
-        dvec_ref[1:2, :] = column_sum(grad * xhat)
-        dvec_ref[2:3, :] = column_sum(grad)
+
+def ffn_last_kernel(
+    place_ref,
+    acc_ref,
+    xhat_ref,
+    inv_ref,
+    mixed_t_ref,
+    wo_ref,
+    vec_ref,
+    dvec_in_ref,
+    grad_one_ref,
+    gm_ref,
+    wo_other_ref,
+    wo_mine_ref,
+    dvec_ref,
+):
+    width = acc_ref.shape[1]
+    grad = acc_ref[...]
+    xhat = xhat_ref[...]
+    grad_one = norm_back(grad, xhat, inv_ref[...], vec_ref[1:2, :])
+    grad_one_ref[...] = grad_one
+    grad_att = grad_one.astype(bf16)
+    gm_ref[...] = dot_nt(grad_att, wo_ref[...]).astype(bf16)
+    half = width // 2
+    place = place_ref[0]
+    mine = pl.ds(pl.multiple_of(place * half, half), half)
+    other = pl.ds(pl.multiple_of((1 - place) * half, half), half)
+    wo_mine_ref[...] = dot(mixed_t_ref[mine, :], grad_att).astype(bf16)
+    wo_other_ref[...] = dot(mixed_t_ref[other, :], grad_att).astype(bf16)
+    dvec_ref[...] = dvec_in_ref[...]
+    dvec_ref[1:2, :] = column_sum(grad * xhat)
+    dvec_ref[2:3, :] = column_sum(grad)
+
+
+def first_norm_kernel(tok_ref, mixed_ref, wo_ref, vec_ref, low_ref, low_t_ref, xhat_ref, inv_ref):
+    residual = tok_ref[...].astype(f32) + dot(mixed_ref[...], wo_ref[...])
+    xhat, inverse = norm_stats(residual)
+    normed = xhat * vec_ref[1:2, :] + vec_ref[2:3, :]
+    xhat_ref[...] = xhat
+    inv_ref[...] = inverse
+    low_ref[...] = normed.astype(bf16)
+    low_t_ref[...] = normed.T.astype(bf16)
+
+
+def first_norm(tokens, mixed, attention_weights, vectors):
+    length, width = tokens.shape
+    wo_column = attention_weights.shape[1] // width - 1
+    whole = lambda shape: pl.BlockSpec(shape, lambda i: (0,) * len(shape))
+    return pl.pallas_call(
+        first_norm_kernel,
+        grid=(1,),
+        in_specs=[
+            whole((length, width)),
+            whole((length, width)),
+            pl.BlockSpec((width, width), lambda i: (0, wo_column)),
+            whole(vectors.shape),
+        ],
+        out_specs=[
+            whole((length, width)),
+            whole((width, length)),
+            whole((length, width)),
+            whole((length, 1)),
+        ],
+        out_shape=[
+            jax.ShapeDtypeStruct((length, width), bf16),
+            jax.ShapeDtypeStruct((width, length), bf16),
+            jax.ShapeDtypeStruct((length, width), f32),
+            jax.ShapeDtypeStruct((length, 1), f32),
+        ],
+        cost_estimate=pl.CostEstimate(flops=0, bytes_accessed=0, transcendentals=0),
+        name="first_norm",
+    )(tokens, mixed, attention_weights, vectors)
 
 
 def feed_forward(
-    place, tokens, mixed, mixed_t, attention_weights, weights, up_bias, vectors, live, cotangent
+    place,
+    low,
+    low_t,
+    xhat,
+    inverse,
+    mixed_t,
+    attention_weights,
+    weights,
+    up_bias,
+    vectors,
+    live,
+    cotangent,
 ):
-    length, width = tokens.shape
+    length, width = low.shape
     parts, shards, _, rows, hidden = weights.shape
     xs = parts // 2
     whole = lambda shape: pl.BlockSpec(shape, lambda p, w, c: (0,) * len(shape))
@@ -556,18 +615,15 @@
         (None, shards, rows, hidden), lambda p, w, c: (p * jnp.maximum(w - xs, 0), 0, 0, 0)
     )
     grads = jax.ShapeDtypeStruct((xs, shards, rows, hidden), bf16)
-    return pl.pallas_call(
+    out, acc, up_other, up_mine, down_other, down_mine, dup_bias, dvec = pl.pallas_call(
         ffn_kernel,
         grid_spec=pltpu.PrefetchScalarGridSpec(
             num_scalar_prefetch=1,
             grid=(2, parts),
             in_specs=[
                 once(wide),
+                once((width, length)),
                 once(wide),
-                once((width, length)),
-                pl.BlockSpec(
-                    (width, width), lambda p, w, c: (0, wo_column), pipeline_mode=pl.Buffered(1)
-                ),
                 weight_spec(0),
                 weight_spec(1),
                 pl.BlockSpec((None, 1, hidden), lambda p, w, c: (part_of(w, c), 0, 0)),
@@ -578,27 +634,18 @@
             out_specs=[
                 whole(wide),
                 whole(wide),
-                whole(wide),
                 other_spec,
                 mine_spec,
                 other_spec,
                 mine_spec,
-                whole((width // 2, width)),
-                whole((width // 2, width)),
                 pl.BlockSpec(
                     (None, 1, hidden), lambda p, w, c: (part_of(w * p, c), 0, 0)
                 ),
                 whole((8, width)),
             ],
             scratch_shapes=[
-                pltpu.VMEM(wide, f32),
-                pltpu.VMEM(wide, bf16),
-                pltpu.VMEM((width, length), bf16),
-                pltpu.VMEM(wide, f32),
-                pltpu.VMEM((length, 1), f32),
                 pltpu.VMEM((parts, length, hidden), bf16),
                 pltpu.VMEM((parts, length, hidden), f32),
-                pltpu.VMEM(wide, f32),
                 pltpu.VMEM(wide, bf16),
                 pltpu.VMEM((width, length), bf16),
             ],
@@ -606,13 +653,10 @@
         out_shape=[
             jax.ShapeDtypeStruct(wide, bf16),
             jax.ShapeDtypeStruct(wide, f32),
-            jax.ShapeDtypeStruct(wide, bf16),
             grads,
             grads,
             grads,
             grads,
-            jax.ShapeDtypeStruct((width // 2, width), bf16),
-            jax.ShapeDtypeStruct((width // 2, width), bf16),
             jax.ShapeDtypeStruct((parts, 1, hidden), f32),
             jax.ShapeDtypeStruct((8, width), f32),
         ],
@@ -621,16 +665,60 @@
         name="feed_forward",
     )(
         place,
-        tokens,
-        mixed,
-        mixed_t,
-        attention_weights,
+        low,
+        low_t,
+        xhat,
         weights,
         weights,
         up_bias,
         vectors,
         live,
         cotangent,
+    )
+    grad_one, gm, wo_other, wo_mine, dvec = pl.pallas_call(
+        ffn_last_kernel,
+        grid_spec=pltpu.PrefetchScalarGridSpec(
+            num_scalar_prefetch=1,
+            grid=(1,),
+            in_specs=[
+                pl.BlockSpec(wide, lambda i, c: (0, 0)),
+                pl.BlockSpec(wide, lambda i, c: (0, 0)),
+                pl.BlockSpec((length, 1), lambda i, c: (0, 0)),
+                pl.BlockSpec((width, length), lambda i, c: (0, 0)),
+                pl.BlockSpec((width, width), lambda i, c: (0, wo_column)),
+                pl.BlockSpec(vectors.shape, lambda i, c: (0, 0)),
+                pl.BlockSpec((8, width), lambda i, c: (0, 0)),
+            ],
+            out_specs=[
+                pl.BlockSpec(wide, lambda i, c: (0, 0)),
+                pl.BlockSpec(wide, lambda i, c: (0, 0)),
+                pl.BlockSpec((width // 2, width), lambda i, c: (0, 0)),
+                pl.BlockSpec((width // 2, width), lambda i, c: (0, 0)),
+                pl.BlockSpec((8, width), lambda i, c: (0, 0)),
+            ],
+        ),
+        out_shape=[
+            jax.ShapeDtypeStruct(wide, f32),
+            jax.ShapeDtypeStruct(wide, bf16),
+            jax.ShapeDtypeStruct((width // 2, width), bf16),
+            jax.ShapeDtypeStruct((width // 2, width), bf16),
+            jax.ShapeDtypeStruct((8, width), f32),
+        ],
+        cost_estimate=pl.CostEstimate(flops=0, bytes_accessed=0, transcendentals=0),
+        name="ffn_last",
+    )(place, acc, xhat, inverse, mixed_t, attention_weights, vectors, dvec)
+    return (
+        out,
+        grad_one,
+        gm,
+        up_other,
+        up_mine,
+        down_other,
+        down_mine,
+        wo_other,
+        wo_mine,
+        dup_bias,
+        dvec,
     )
 
 
@@ -663,6 +751,15 @@
     def offsets(self, dims):
         ranges = [range(self.sizes[d]) for d in dims]
         return [dict(zip(dims, o)) for o in itertools.product(*ranges)]
+
+    def swap(self, value, dims):
+        groups = {}
+        for i in range(self.devices):
+            key = tuple(i // self.strides[d] % n for d, n in self.sizes.items() if d not in dims)
+            groups.setdefault(key, []).append(i)
+        return lax.all_to_all(
+            value, ("batch", "wide"), 0, 0, axis_index_groups=list(groups.values())
+        )
 
     def gather(self, value, names, dims):
         parts = [(o, self.shift(value, **o) if any(o.values()) else value) for o in self.offsets(dims)]
@@ -750,7 +847,7 @@
                 out_specs=self.out_specs,
             ),
             out_shape=self.shapes,
-            compiler_params=pltpu.CompilerParams(vmem_limit_bytes=60 * 1024 * 1024),
+            compiler_params=pltpu.CompilerParams(vmem_limit_bytes=63 * 1024 * 1024 + 900 * 1024),
             cost_estimate=pl.CostEstimate(flops=0, bytes_accessed=0, transcendentals=0),
             name=name,
         )(self.grid.vector, *self.inputs)
@@ -792,9 +889,17 @@
     pairs = heads // 2
     own = query_weight.shape[0]
     lanes = width // pairs
-    shard, ffn_shard = prepare(
-        query_weight, key_weight, value_weight, out_weight, up_weight, down_weight
-    )
+    ffn_shard = prepare_ffn(up_weight, down_weight)
+    query_weight, (ffn_shard,) = hold(query_weight, ffn_shard)
+    shard = prepare(query_weight, key_weight, value_weight, out_weight)
+    up_rows, hidden = up_weight.shape
+    half = 2 * width
+    gathered = grid.gather(shard.reshape(1, 1, 1, 1, own, 4 * width), "zyxc", "z")
+    first = grid.gather(gathered[..., :half], "zyxc", "x")
+    second = grid.gather(gathered[..., half:], "zyxc", "y")
+    inputs = (position_bias, features, block_row, block_live, tokens, down_bias)
+    first, (second, *inputs) = hold(first, second, *inputs)
+    position_bias, features, block_row, block_live, tokens, down_bias = inputs
     tables = toeplitz_tables(position_bias[:, ::-1])
     feat_forward, feat_back, swap, turn = feature_tables(features)
     offsets = jnp.arange(BLK, dtype=jnp.int32)
@@ -806,13 +911,14 @@
     vectors = jnp.stack([down_bias, gain_one, shift_one, gain_two, shift_two] + [down_bias] * 3)
     live_column = live.reshape(length, 1)
 
-    up_rows, hidden = up_weight.shape
-    gathered = grid.gather(shard.reshape(1, 1, 1, 1, own, 4 * width), "zyxc", "z")
-    gathered = grid.gather(gathered, "zyxc", "yx")
+    first = grid.gather(first, "zyxc", "y")
+    second = grid.gather(second, "zyxc", "x")
     early = (tables, feat_forward, feat_back, swap, turn, mask, tokens_t, vectors, live_column)
-    gathered, early = hold(gathered, *early)
+    first, (second, *early) = hold(first, second, *early)
     tables, feat_forward, feat_back, swap, turn, mask, tokens_t, vectors, live_column = early
-    attention_weights = grid.gather(gathered, "zyxc", "c").reshape(width, 4 * width)
+    first = grid.gather(first, "zyxc", "c").reshape(width, half)
+    second = grid.gather(second, "zyxc", "c").reshape(width, half)
+    attention_weights = jnp.concatenate([first, second], axis=1)
     ffn_weights = lax.all_gather(ffn_shard, ("wide", "batch"), axis=0, tiled=False)
     ffn_weights = ffn_weights.reshape(wide, batch, 2, up_rows, hidden)
     mixed, mixed32, u, phi, value, inverse = attend(
@@ -833,8 +939,7 @@
         dvec,
     ) = feed_forward(
         place,
-        tokens,
-        mixed,
+        *first_norm(tokens, mixed, attention_weights, vectors),
         by_core(mixed.T),
         attention_weights,
         ffn_weights,
@@ -908,7 +1013,7 @@
     down_new = grid.send(sends[: xs - 1], "x")
     up_new = grid.send(sends[xs - 1 :], "y")
     small = small + grid.shift(small, c=1)
-    small = [small] + grid.send([small.astype(bf16)] * (ys * xs - 1), "yx")
+    small_new = grid.send([small.astype(bf16)] * (zs - 1), "z")
     dw_mine, sends = hold(dw_mine, *sends)
     att[0] = att_view(dw_mine)
     step = Combine(grid, 1)
@@ -919,7 +1024,10 @@
         ]
         step.write((zs, own, columns), bf16, terms)
     att_sends = step.run("att_sum_core")
-    down_new, (up_new, att_sends, small) = hold(down_new, up_new, att_sends, small)
+    small, (*small_new, att_sends) = hold(small, *small_new, att_sends)
+    small = (small + sum(v.astype(f32) for v in small_new)).astype(bf16)
+    small = jnp.broadcast_to(small[None], (ys * xs,) + small.shape)
+    down_new, (up_new, att_sends) = hold(down_new, up_new, att_sends)
     down += [("z", v) for v in down_new]
     up += [("z", v) for v in up_new]
     att_new = grid.send(att_sends, "yx")
@@ -933,13 +1041,14 @@
         ]
         step.write((2, up_rows, hidden), bf16, terms)
     sends = step.run("ffn_sum_second")
+    dqkv, (small, *sends) = hold(dqkv, small, *sends)
+    small = grid.swap(small, "yx")
     ffn_new = grid.send(sends, "z")
     grad_tokens = grad_one + dot_nt(dqkv, attention_weights[:, : 3 * width])
     att_new, (grad_tokens, *sends) = hold(att_new, grad_tokens, *sends)
     att_new = [("z", v) for v in att_new]
 
     step = Combine(grid, 1)
-    small_in = step.read(small, (None, None))
     for z in range(1, zs):
         picks = dict(z=z, y=0, x=0)
         top = slice(0, own)
@@ -953,8 +1062,7 @@
             (target, [(everything, numbers), ((slice(None), target[1]), new)])
             for target, _, numbers in terms
         ]
-        terms.append(((slice(own, None),), everything, small_in))
-        step.write((own + extra, columns), bf16, terms)
+        step.write((own, columns), bf16, terms)
     att_sends = step.run("att_sum_plane")
     last = grid.send(att_sends, "z")
 
@@ -973,23 +1081,12 @@
     terms = [
         ((top, head[1]), [(everything, step.add(att, here)), (head, new)]),
         ((top, tail[1]), [(everything, step.add(out, here)), (tail, new)]),
-        ((slice(own, None),), everything, step.read(small, (None, None))),
     ]
-    step.write((own + extra, columns), f32, terms)
-    (before,) = step.run("att_sum_own")
-
-    step = Combine(grid, 1)
-    last = step.read([before, *last], (None, None))
-    for j in range(3):
-        terms = []
-        for p in range(pairs):
-            cols = slice((3 * p + j) * lanes, (3 * p + j + 1) * lanes)
-            terms.append(((slice(None), slice(p * lanes, (p + 1) * lanes)), (top, cols), last))
-        step.write((own, width), f32, terms)
-    step.write((own, width), f32, [(everything, (top, tail[1]), last)])
+    step.write((own, columns), f32, terms)
+    small_in = step.read([small], (None, None, None))
 
     def small_term(r, cols):
-        return [((slice(own + r, own + r + 1), cols), last)]
+        return [((k, slice(r, r + 1), cols), small_in) for k in range(ys * xs)]
 
     step.write((columns,), f32, [(everything, small_term(0, slice(None)))])
     for j in range(5):
@@ -1002,7 +1099,19 @@
         term = small_term(first_row + h // per_row, slice(at, at + rels))
         terms.append(((slice(h, h + 1),), term))
     step.write((heads, rels), f32, terms)
-    dq, dk, dv, out_own, dup_bias, *dvec, dbias = step.run("last_sum")
+    before, dup_bias, *dvec, dbias = step.run("att_sum_own")
+
+    step = Combine(grid, 1)
+    last = step.read([before, *last], (None, None))
+    for j in range(3):
+        terms = []
+        for p in range(pairs):
+            cols = slice((3 * p + j) * lanes, (3 * p + j + 1) * lanes)
+            terms.append(((slice(None), slice(p * lanes, (p + 1) * lanes)), (top, cols), last))
+        step.write((own, width), f32, terms)
+    step.write((own, width), f32, [(everything, (top, tail[1]), last)])
+
+    dq, dk, dv, out_own = step.run("last_sum")
     return (
         out_tokens,
         grad_tokens,

time: 264 us -> 259 us (0.981)
  local copies, waits for them, and re-layouts: 23.9 us -> 11.2 us
  Pallas kernels: 108 us -> 116 us
  starting transfers between devices: 32.9 us -> 39.8 us
  waiting for transfers between devices: 62.9 us -> 56.8 us
    pallas_call x1 -> x4, Pallas kernels: 1.98 us -> 14.2 us  [the longest x1 5.92 us: feed_forward(): pl.pallas_call(ffn_last_kernel, grid_spec=pltpu.PrefetchScalarGridSpec(nu...]
    ppermute x28 -> x30, waiting for transfers between devices: 59.5 us -> 47.6 us  [shift(): return lax.ppermute(value, ('batch', 'wide'), pairs)]
    all_gather x1, waiting for transfers between devices: 3.43 us -> 9.14 us  [per_device(): lax.all_gather(ffn_shard, ('wide', 'batch'), axis=0, tiled=False)]
    unnamed x62 -> x36, local copies, waits for them, and re-layouts: 6.86 us -> 1.87 us
    pallas_call x1, Pallas kernels: 31.3 us -> 27.3 us  [feed_forward(): pl.pallas_call(ffn_kernel, grid_spec=pltpu.PrefetchScalarGridSpec(num_sca...]
    dynamic_update_slice x8 -> x4, local copies, waits for them, and re-layouts: 5.01 us -> 0.98 us  [gather(): lax.dynamic_update_slice(out, part, start + [0] * (value.ndim - len(names)))]
    all_to_all x0 -> x1, starting transfers between devices: none -> 3.99 us  [swap(): lax.all_to_all(value, ('batch', 'wide'), 0, 0, axis_index_groups=list(gro...]
    ppermute x28 -> x30, starting transfers between devices: 32.8 us -> 35.8 us  [shift(): return lax.ppermute(value, ('batch', 'wide'), pairs)]
  transfers between devices with their start and end apart: 29 -> 32, of which waited for: 13 -> 17; matrix products, arithmetic and copies ran while one was open for 15% -> 11% of each run, Pallas kernels for 26% -> 31%
where the time goes in v4:
time: 259 us; the launch traced here: 257 us
  Pallas kernels  116 us (45%)
  waiting for transfers between devices  56.8 us (22%)
  starting transfers between devices  39.8 us (15%)
  between operations  14.5 us (6%)
  other arithmetic  12.2 us (5%)
  local copies, waits for them, and re-layouts  11.2 us (4%)
  matrix products  6.34 us (2%)
    ppermute x30, waiting for transfers between devices, shift(): return lax.ppermute(value, ('batch', 'wide'), pairs)  47.6 us
    ppermute x30, starting transfers between devices, shift(): return lax.ppermute(value, ('batch', 'wide'), pairs)  35.8 us
    pallas_call x8, Pallas kernels, run(): pl.pallas_call(kernel, grid_spec=pltpu.PrefetchScalarGridSpec(num_scalar_...  28.7 us
    pallas_call x1, Pallas kernels, feed_forward(): pl.pallas_call(ffn_kernel, grid_spec=pltpu.PrefetchScalarGridSpec(num_sca...  27.3 us
    pallas_call x1, Pallas kernels, attend_back(): pl.pallas_call(partial(attend_back_kernel, scale), grid_spec=pltpu.Prefet...  24.4 us
    pallas_call x1, Pallas kernels, attend(): pl.pallas_call(partial(attend_kernel, scale), grid=(pairs,), in_specs=[wh...  15.8 us
    all_gather x1, waiting for transfers between devices, per_device(): lax.all_gather(ffn_shard, ('wide', 'batch'), axis=0, tiled=False)  9.14 us
    dot_general x1, matrix products, dot_nt(): return lax.dot_general(a, b, nt_dims, preferred_element_type=f32)  6.34 us
  transfers between devices with their start and end apart: 32, of which 17 were waited for; matrix products, arithmetic and copies ran while one was open for 11% of the time, Pallas kernels for 31%

profile of v4, /device:TPU:0, one launch (start us, length us, event | category | flops | bytes accessed | tf_op | source)
XLA Modules:
  0.0 256.6 jit_solution(7576511319962678249)
XLA Ops:
  10.8 4.0 %collective-permute-start.1 = (bf16[1,1,1,1,24,3072]{5,4,3,2,1,0:T(8,128)(2,1)}, bf16[1,1,1,1,24,3072]{5,4,3,2,1,0:T(8,128)(2,1)S(1)}, u32[]{:S(2)}, u32[]{:S(2)}) collective-permute-start(bf16[1,1,1,1,24,3072]{5,4,3,2,1,0:T(8,128)(2,1)} %bitcast.75), channel_id=1, source_target_pairs={{0,16},{1,17},{2,18},{3,19},{4,20},{5,21},{6,22},{7,23},{8,24},{9,... | collective-permute-start | bytes 442376 | tf_op jit(solution)/shard_map/ppermute | solution.py:742
  19.7 4.5 %collective-permute-done = bf16[1,1,1,1,24,3072]{5,4,3,2,1,0:T(8,128)(2,1)S(1)} collective-permute-done((bf16[1,1,1,1,24,3072]{5,4,3,2,1,0:T(8,128)(2,1)}, bf16[1,1,1,1,24,3072]{5,4,3,2,1,0:T(8,128)(2,1)S(1)}, u32[]{:S(2)}, u32[]{:S(2)}) %collective-permute-start) | collective-permute-done | bytes 147488 | tf_op jit(solution)/shard_map/ppermute | solution.py:742
  31.8 3.4 %collective-permute-done.4 = bf16[4,1,1,1,24,1536]{5,4,3,2,1,0:T(8,128)(2,1)S(1)} collective-permute-done((bf16[4,1,1,1,24,1536]{5,4,3,2,1,0:T(8,128)(2,1)S(1)}, bf16[4,1,1,1,24,1536]{5,4,3,2,1,0:T(8,128)(2,1)S(1)}, u32[]{:S(2)}, u32[]{:S(2)}) %collective-permute-start.4) | collective-permute-done | bytes 294944 | tf_op jit(solution)/shard_map/ppermute | solution.py:742
  44.7 5.4 %toeplitz.1.table_ref = f32[12,128,1024]{2,1,0:T(8,128)} custom-call(f32[6,2,1024]{2,1,0:T(2,128)} %reshape.149.bias_ref), custom_call_target="tpu_custom_call" | custom-call | flops 5000000000 | bytes 8000000 | tf_op jit(solution)/shard_map/toeplitz/pallas_call | solution.py:41
  52.3 7.9 %collective-permute-done.6 = bf16[4,2,1,1,24,1536]{5,4,3,2,1,0:T(8,128)(2,1)} collective-permute-done((bf16[4,2,1,1,24,1536]{5,4,3,2,1,0:T(8,128)(2,1)S(1)}, bf16[4,2,1,1,24,1536]{5,4,3,2,1,0:T(8,128)(2,1)}, u32[]{:S(2)}, u32[]{:S(2)}) %collective-permute-start.6) | collective-permute-done | bytes 589856 | tf_op jit(solution)/shard_map/ppermute | solution.py:742
  63.5 3.3 %collective-permute-done.7 = bf16[4,2,2,1,24,1536]{5,4,3,2,1,0:T(8,128)(2,1)} collective-permute-done((bf16[4,2,2,1,24,1536]{5,4,3,2,1,0:T(8,128)(2,1)S(1)}, bf16[4,2,2,1,24,1536]{5,4,3,2,1,0:T(8,128)(2,1)}, u32[]{:S(2)}, u32[]{:S(2)}) %collective-permute-start.7) | collective-permute-done | bytes 1179680 | tf_op jit(solution)/shard_map/ppermute | solution.py:742
  73.3 15.8 %attend.1 = (bf16[512,768]{1,0:T(8,128)(2,1)}, f32[512,768]{1,0:T(8,128)}, f32[512,1536]{1,0:T(8,128)}, f32[512,1536]{1,0:T(8,128)}, bf16[512,768]{1,0:T(8,128)(2,1)}, /*index=5*/f32[512,768]{1,0:T(8,128)}) custom-call(bf16[512,768]{1,0:T(8,128)(2,1)} %tok_ref.1, bf16[768,3072]{1,0:T(8,128)(2,1)} %pad_maximum_fusion.w_ref.wo_ref, ...), custom_call_target="tpu_custom_call" | custom-call | tf_op jit(solution)/shard_map/attend/pallas_call | solution.py:131
  89.1 4.9 %first_norm.1 = (bf16[512,768]{1,0:T(8,128)(2,1)}, bf16[768,512]{1,0:T(8,128)(2,1)}, f32[512,768]{1,0:T(8,128)}, f32[512,1]{1,0:T(8,128)}) custom-call(bf16[512,768]{1,0:T(8,128)(2,1)} %tok_ref.1, bf16[512,768]{1,0:T(8,128)(2,1)} %get-tuple-element.137.mixed_ref, bf16[768,3072]{1,0:T(8,128)(2,1)} %pad_maximum_fusion.w_ref.wo_ref, f32[8,768]{1,0:T(8,128)} %stack.39.vec_ref), custom_call_target="tpu_custom_call" | custom-call | tf_op jit(solution)/shard_map/first_norm/pallas_call | solution.py:558
  94.0 9.1 %all-gather.3.cloned.1.call-done = bf16[6144,768]{1,0:T(8,128)(2,1)} async-done(((bf16[192,768]{1,0:T(8,128)(2,1)}), bf16[6144,768]{1,0:T(8,128)(2,1)}) %all-gather.3.cloned.1.call-update) | async-done | bytes 9437200 | tf_op jit(solution)/shard_map/all_gather | solution.py:922
  103.1 27.3 %feed_forward.1 = (bf16[512,768]{1,0:T(8,128)(2,1)}, f32[512,768]{1,0:T(8,128)}, bf16[2,8,96,768]{3,2,1,0:T(8,128)(2,1)}, bf16[2,8,96,768]{3,2,1,0:T(8,128)(2,1)...) custom-call(s32[1]{0:T(128)} %bitcast.place_ref, ...), custom_call_target="tpu_custom_call" | custom-call | tf_op jit(solution)/shard_map/feed_forward/pallas_call | solution.py:618
  132.9 5.9 %ffn_last.1 = (f32[512,768]{1,0:T(8,128)}, bf16[512,768]{1,0:T(8,128)(2,1)}, bf16[384,768]{1,0:T(8,128)(2,1)}, bf16[384,768]{1,0:T(8,128)(2,1)}, f32[8,768]{1,0:T(8,128)}) custom-call(s32[1]{0:T(128)} %bitcast.place_ref, f32[512,768]{1,0:T(8,128)} %get-tuple-element.147.acc_ref, f32[512,768]{1,0:T(8,128)} %get-tuple-element.141.xhat_ref, ...), custom_call_target="tpu_custom_call" | custom-call | tf_op jit(solution)/shard_map/ffn_last/pallas_call | solution.py:678
  140.3 5.1 %ffn_sum_core.1 = (bf16[2,4,96,768]{3,2,1,0:T(8,128)(2,1)}, bf16[4,2,96,768]{3,2,1,0:T(8,128)(2,1)}) custom-call(s32[4]{0:T(128)} %pad_add_fusion.vector_ref, bf16[2,4,2,96,768]{4,3,2,1,0:T(8,128)(2,1)} %bitcast.51, bf16[2,4,2,96,768]{4,3,2,1,0:T(8,128)(2,1)} %bitcast.24.refs_1_.refs_5_.refs_13_.refs_21_.refs_8_, bf16[2,4,2,96,768]{4,3,2,1,0:T(8,128)(2,1)} %bitcast.45, ...), custom_call_target="tpu_custom_call" | custom-call | tf_op jit(solution)/shard_map/ffn_sum_core/pallas_call | solution.py:841
  147.5 24.4 %attend_back.1 = (bf16[384,2304]{1,0:T(8,128)(2,1)}, bf16[384,2304]{1,0:T(8,128)(2,1)}, bf16[512,2304]{1,0:T(8,128)(2,1)}, f32[8,3072]{1,0:T(8,128)}) custom-call(s32[1]{0:T(128)} %bitcast.place_ref, bf16[768,512]{1,0:T(8,128)(2,1)} %bitcast.70, f32[12,128,1024]{2,1,0:T(8,128)} %toeplitz.1.table_ref, f32[4,512]{1,0:T(4,128)} %compare_select_fusion.mask_ref, ...), custom_call_target="tpu_custom_call" | custom-call | tf_op jit(solution)/shard_map/attend_back/pallas_call | solution.py:303
  175.6 3.9 %ffn_sum_plane.1 = (bf16[4,96,768]{2,1,0:T(8,128)(2,1)}, bf16[4,96,768]{2,1,0:T(8,128)(2,1)}) custom-call(s32[4]{0:T(128)} %pad_add_fusion.vector_ref, bf16[2,4,2,96,768]{4,3,2,1,0:T(8,128)(2,1)} %bitcast.52, bf16[2,4,2,96,768]{4,3,2,1,0:T(8,128)(2,1)} %bitcast.24.refs_1_.refs_5_.refs_13_.refs_21_.refs_8_, ...), custom_call_target="tpu_custom_call" | custom-call | tf_op jit(solution)/shard_map/ffn_sum_plane/pallas_call | solution.py:841
  187.1 4.0 %att_sum_core.1 = (bf16[4,24,3072]{2,1,0:T(8,128)(2,1)}, bf16[4,24,3072]{2,1,0:T(8,128)(2,1)}, bf16[4,24,3072]{2,1,0:T(8,128)(2,1)}) custom-call(s32[4]{0:T(128)} %pad_add_fusion.vector_ref, bf16[4,2,2,24,2304]{4,3,2,1,0:T(8,128)(2,1)} %bitcast.38, bf16[4,2,2,24,2304]{4,3,2,1,0:T(8,128)(2,1)} %bitcast.28.refs_1_.refs_5_.refs_9_.refs_4_.refs_11_.refs_18_, ...), custom_call_target="tpu_custom_call" | custom-call | tf_op jit(solution)/shard_map/att_sum_core/pallas_call | solution.py:841
  192.3 3.3 %collective-permute-done.13.refs_7_.refs_15_.refs_23_.refs_10_ = bf16[4,96,768]{2,1,0:T(8,128)(2,1)} collective-permute-done((bf16[4,96,768]{2,1,0:T(8,128)(2,1)}, bf16[4,96,768]{2,1,0:T(8,128)(2,1)}, u32[]{:S(2)}, u32[]{:S(2)}) %collective-permute-start.13) | collective-permute-done | bytes 589856 | tf_op jit(solution)/shard_map/ppermute | solution.py:742
  199.4 3.9 %ffn_sum_second.1 = (bf16[2,96,768]{2,1,0:T(8,128)(2,1)}, bf16[2,96,768]{2,1,0:T(8,128)(2,1)}, bf16[2,96,768]{2,1,0:T(8,128)(2,1)}) custom-call(s32[4]{0:T(128)} %pad_add_fusion.vector_ref, bf16[2,4,2,96,768]{4,3,2,1,0:T(8,128)(2,1)} %bitcast.47, bf16[2,4,2,96,768]{4,3,2,1,0:T(8,128)(2,1)} %bitcast.26.refs_3_.refs_4_.refs_1_.refs_9_.refs_17_, ...), custom_call_target="tpu_custom_call" | custom-call | tf_op jit(solution)/shard_map/ffn_sum_second/pallas_call | solution.py:841
  204.9 4.0 %all-to-all-start = ((bf16[4,8,3072]{2,1,0:T(8,128)(2,1)}), bf16[4,8,3072]{2,1,0:T(8,128)(2,1)}, u32[]{:S(2)}, u32[]{:S(2)}) async-start(bf16[4,8,3072]{2,1,0:T(8,128)(2,1)} %broadcast_in_dim.38), calls=%async_computation | async-start | bytes 393216 | tf_op jit(solution)/shard_map/all_to_all | solution.py:760
  214.4 6.3 %fusion.3 = f32[512,768]{1,0:T(8,128)} fusion(f32[512,768]{1,0:T(8,128)} %get-tuple-element.194, bf16[512,2304]{1,0:T(8,128)(2,1)} %get-tuple-element.205, bf16[768,1536]{1,0:T(8,128)(2,1)} %bitcast.67, bf16[768,1536]{1,0:T(8,128)(2,1)} %bitcast.69), kind=kOutput, calls=%fused_computation.7 | convolution fusion | flops 1819410432 | bytes 10223616 | tf_op jit(solution)/shard_map/dot_general | solution.py:22
  220.7 5.5 %collective-permute-done.22.refs_1_.refs_8_.refs_15_ = bf16[4,24,3072]{2,1,0:T(8,128)(2,1)} collective-permute-done((bf16[4,24,3072]{2,1,0:T(8,128)(2,1)}, bf16[4,24,3072]{2,1,0:T(8,128)(2,1)}, u32[]{:S(2)}, u32[]{:S(2)}) %collective-permute-start.22) | collective-permute-done | bytes 589856 | tf_op jit(solution)/shard_map/ppermute | solution.py:742
  226.2 3.3 %att_sum_plane.1 = (bf16[24,3072]{1,0:T(8,128)(2,1)}, bf16[24,3072]{1,0:T(8,128)(2,1)}, bf16[24,3072]{1,0:T(8,128)(2,1)}) custom-call(s32[4]{0:T(128)} %pad_add_fusion.vector_ref, bf16[4,24,3072]{2,1,0:T(8,128)(2,1)} %collective-permute-done.21.refs_0_.refs_7_.refs_14_, bf16[4,24,3072]{2,1,0:T(8,128)(2,1)} %collective-permute-done.22.refs_1_.refs_8_.refs_15_, ...), custom_call_target="tpu_custom_call" | custom-call | tf_op jit(solution)/shard_map/att_sum_plane/pallas_call | solution.py:841
  234.4 3.2 %ffn_sum_last.1 = (f32[96,768]{1,0:T(8,128)}, f32[96,768]{1,0:T(8,128)}) custom-call(s32[4]{0:T(128)} %pad_add_fusion.vector_ref, bf16[2,96,768]{2,1,0:T(8,128)(2,1)} %collective-permute-done.27.refs_0_, bf16[2,96,768]{2,1,0:T(8,128)(2,1)} %collective-permute-done.28.refs_1_, bf16[2,96,768]{2,1,0:T(8,128)(2,1)} %collective-permute-done.29.refs_2_, ...), custom_call_target="tpu_custom_call" | custom-call | tf_op jit(solution)/shard_map/ffn_sum_last/pallas_call | solution.py:841
  237.5 2.8 %att_sum_own.1 = (f32[24,3072]{1,0:T(8,128)}, f32[3072]{0:T(1024)}, f32[768]{0:T(1024)}, f32[768]{0:T(1024)}, f32[768]{0:T(1024)}, /*index=5*/f32[768]{0:T(1024)}, f32[768]{0:T(1024)}, f32[12,1024]{1,0:T(8,128)}) custom-call(s32[4]{0:T(128)} %pad_add_fusion.vector_ref, bf16[4,24,3072]{2,1,0:T(8,128)(2,1)} %collective-permute-done.21.refs_0_.refs_7_.refs_14_, ...), custom_call_target="tpu_custom_call" | custom-call | tf_op jit(solution)/shard_map/att_sum_own/pallas_call | solution.py:841
  240.4 6.8 %collective-permute-done.25.refs_2_ = bf16[24,3072]{1,0:T(8,128)(2,1)} collective-permute-done((bf16[24,3072]{1,0:T(8,128)(2,1)}, bf16[24,3072]{1,0:T(8,128)(2,1)}, u32[]{:S(2)}, u32[]{:S(2)}) %collective-permute-start.25) | collective-permute-done | bytes 147488 | tf_op jit(solution)/shard_map/ppermute | solution.py:742
  (146 shorter events, 73.9 us)
Async XLA Ops:
  7.2 95.9 %all-gather.3.cloned.1.call-start = ((), (), s32[]{:S(2)}) async-start(), calls=%async_computation.1 | async-start | bytes 9732096 | tf_op jit(solution)/shard_map/all_gather | solution.py:922
  10.8 15.3 %collective-permute-start.1 = (bf16[1,1,1,1,24,3072]{5,4,3,2,1,0:T(8,128)(2,1)}, bf16[1,1,1,1,24,3072]{5,4,3,2,1,0:T(8,128)(2,1)S(1)}, u32[]{:S(2)}, u32[]{:S(2)}) collective-permute-start(bf16[1,1,1,1,24,3072]{5,4,3,2,1,0:T(8,128)(2,1)} %bitcast.75), channel_id=1, source_target_pairs={{0,16},{1,17},{2,18},{3,19},{4,20},{5,21},{6,22},{7,23},{8,24},{9,... | collective-permute-start | bytes 442376 | tf_op jit(solution)/shard_map/ppermute | solution.py:742
  14.8 9.4 %collective-permute-start = (bf16[1,1,1,1,24,3072]{5,4,3,2,1,0:T(8,128)(2,1)}, bf16[1,1,1,1,24,3072]{5,4,3,2,1,0:T(8,128)(2,1)S(1)}, u32[]{:S(2)}, u32[]{:S(2)}) collective-permute-start(bf16[1,1,1,1,24,3072]{5,4,3,2,1,0:T(8,128)(2,1)} %bitcast.76), channel_id=1, source_target_pairs={{0,8},{1,9},{2,10},{3,11},{4,12},{5,13},{6,14},{7,15},{8,16},{9,17... | collective-permute-start | bytes 442376 | tf_op jit(solution)/shard_map/ppermute | solution.py:742
  16.4 12.0 %collective-permute-start.2 = (bf16[1,1,1,1,24,3072]{5,4,3,2,1,0:T(8,128)(2,1)}, bf16[1,1,1,1,24,3072]{5,4,3,2,1,0:T(8,128)(2,1)S(1)}, u32[]{:S(2)}, u32[]{:S(2)}) collective-permute-start(bf16[1,1,1,1,24,3072]{5,4,3,2,1,0:T(8,128)(2,1)} %bitcast.77), channel_id=1, source_target_pairs={{0,24},{1,25},{2,26},{3,27},{4,28},{5,29},{6,30},{7,31},{8,0},{9,1... | collective-permute-start | bytes 442376 | tf_op jit(solution)/shard_map/ppermute | solution.py:742
  37.1 15.1 %collective-permute-start.5 = (bf16[4,1,2,1,24,1536]{5,4,3,2,1,0:T(8,128)(2,1)S(1)}, bf16[4,1,2,1,24,1536]{5,4,3,2,1,0:T(8,128)(2,1)S(1)}, u32[]{:S(2)}, u32[]{:S(2)}) collective-permute-start(bf16[4,1,2,1,24,1536]{5,4,3,2,1,0:T(8,128)(2,1)S(1)} %pad_maximum_fusion.5), channel_id=1, source_target_pairs={{0,4},{1,5},{2,6},{3,7},{4,0},{5,1},{6,2},{7,3},{8,12},{9,13},{10,... | collective-permute-start | bytes 1769480 | tf_op jit(solution)/shard_map/ppermute | solution.py:742
  41.2 18.9 %collective-permute-start.6 = (bf16[4,2,1,1,24,1536]{5,4,3,2,1,0:T(8,128)(2,1)S(1)}, bf16[4,2,1,1,24,1536]{5,4,3,2,1,0:T(8,128)(2,1)}, u32[]{:S(2)}, u32[]{:S(2)}) collective-permute-start(bf16[4,2,1,1,24,1536]{5,4,3,2,1,0:T(8,128)(2,1)S(1)} %pad_maximum_fusion.6), channel_id=1, source_target_pairs={{0,2},{1,3},{2,0},{3,1},{4,6},{5,7},{6,4},{7,5},{8,10},{9,11},{10,... | collective-permute-start | bytes 1769480 | tf_op jit(solution)/shard_map/ppermute | solution.py:742
  130.4 10.0 %collective-permute-start.9 = (bf16[2,8,96,768]{3,2,1,0:T(8,128)(2,1)}, bf16[2,8,96,768]{3,2,1,0:T(8,128)(2,1)}, u32[]{:S(2)}, u32[]{:S(2)}) collective-permute-start(bf16[2,8,96,768]{3,2,1,0:T(8,128)(2,1)} %get-tuple-element.152), channel_id=1, source_target_pairs={{0,1},{1,0},{2,3},{3,2},{4,5},{5,4},{6,7},{7,6},{8,9},{9,8},{10,11... | collective-permute-start | bytes 7077896 | tf_op jit(solution)/shard_map/ppermute | solution.py:742
  130.7 9.6 %collective-permute-start.10 = (bf16[2,8,96,768]{3,2,1,0:T(8,128)(2,1)}, bf16[2,8,96,768]{3,2,1,0:T(8,128)(2,1)}, u32[]{:S(2)}, u32[]{:S(2)}) collective-permute-start(bf16[2,8,96,768]{3,2,1,0:T(8,128)(2,1)} %get-tuple-element.164), channel_id=1, source_target_pairs={{0,1},{1,0},{2,3},{3,2},{4,5},{5,4},{6,7},{7,6},{8,9},{9,8},{10,11... | collective-permute-start | bytes 7077896 | tf_op jit(solution)/shard_map/ppermute | solution.py:742
  145.5 28.5 %collective-permute-start.11 = (bf16[2,4,96,768]{3,2,1,0:T(8,128)(2,1)}, bf16[2,4,96,768]{3,2,1,0:T(8,128)(2,1)}, u32[]{:S(2)}, u32[]{:S(2)}) collective-permute-start(bf16[2,4,96,768]{3,2,1,0:T(8,128)(2,1)} %get-tuple-element.173), channel_id=1, source_target_pairs={{0,4},{1,5},{2,6},{3,7},{4,0},{5,1},{6,2},{7,3},{8,12},{9,13},{10,... | collective-permute-start | bytes 3538952 | tf_op jit(solution)/shard_map/ppermute | solution.py:742
  147.0 28.2 %collective-permute-start.12 = (bf16[4,2,96,768]{3,2,1,0:T(8,128)(2,1)}, bf16[4,2,96,768]{3,2,1,0:T(8,128)(2,1)}, u32[]{:S(2)}, u32[]{:S(2)}) collective-permute-start(bf16[4,2,96,768]{3,2,1,0:T(8,128)(2,1)} %get-tuple-element.174), channel_id=1, source_target_pairs={{0,2},{1,3},{2,0},{3,1},{4,6},{5,7},{6,4},{7,5},{8,10},{9,11},{10,... | collective-permute-start | bytes 3538952 | tf_op jit(solution)/shard_map/ppermute | solution.py:742
  175.1 10.9 %collective-permute-start.19 = (bf16[384,2304]{1,0:T(8,128)(2,1)}, bf16[384,2304]{1,0:T(8,128)(2,1)}, u32[]{:S(2)}, u32[]{:S(2)}) collective-permute-start(bf16[384,2304]{1,0:T(8,128)(2,1)} %get-tuple-element.182), channel_id=1, source_target_pairs={{0,1},{1,0},{2,3},{3,2},{4,5},{5,4},{6,7},{7,6},{8,9},{9,8},{10,11... | collective-permute-start | bytes 5308424 | tf_op jit(solution)/shard_map/ppermute | solution.py:742
  175.6 9.4 %collective-permute-start.20 = (bf16[384,768]{1,0:T(8,128)(2,1)}, bf16[384,768]{1,0:T(8,128)(2,1)}, u32[]{:S(2)}, u32[]{:S(2)}) collective-permute-start(bf16[384,768]{1,0:T(8,128)(2,1)} %get-tuple-element.184), channel_id=1, source_target_pairs={{0,1},{1,0},{2,3},{3,2},{4,5},{5,4},{6,7},{7,6},{8,9},{9,8},{10,11... | collective-permute-start | bytes 1769480 | tf_op jit(solution)/shard_map/ppermute | solution.py:742
  179.5 16.1 %collective-permute-start.13 = (bf16[4,96,768]{2,1,0:T(8,128)(2,1)}, bf16[4,96,768]{2,1,0:T(8,128)(2,1)}, u32[]{:S(2)}, u32[]{:S(2)}) collective-permute-start(bf16[4,96,768]{2,1,0:T(8,128)(2,1)} %get-tuple-element.177), channel_id=1, source_target_pairs={{0,2},{1,3},{2,0},{3,1},{4,6},{5,7},{6,4},{7,5},{8,10},{9,11},{10,... | collective-permute-start | bytes 1769480 | tf_op jit(solution)/shard_map/ppermute | solution.py:742
  180.1 15.8 %collective-permute-start.14 = (bf16[4,96,768]{2,1,0:T(8,128)(2,1)}, bf16[4,96,768]{2,1,0:T(8,128)(2,1)}, u32[]{:S(2)}, u32[]{:S(2)}) collective-permute-start(bf16[4,96,768]{2,1,0:T(8,128)(2,1)} %get-tuple-element.178), channel_id=1, source_target_pairs={{0,4},{1,5},{2,6},{3,7},{4,0},{5,1},{6,2},{7,3},{8,12},{9,13},{10,... | collective-permute-start | bytes 1769480 | tf_op jit(solution)/shard_map/ppermute | solution.py:742
  195.9 16.6 %collective-permute-start.21 = (bf16[4,24,3072]{2,1,0:T(8,128)(2,1)}, bf16[4,24,3072]{2,1,0:T(8,128)(2,1)}, u32[]{:S(2)}, u32[]{:S(2)}) collective-permute-start(bf16[4,24,3072]{2,1,0:T(8,128)(2,1)} %get-tuple-element.191), channel_id=1, source_target_pairs={{0,2},{1,3},{2,0},{3,1},{4,6},{5,7},{6,4},{7,5},{8,10},{9,11},{10,... | collective-permute-start | bytes 1769480 | tf_op jit(solution)/shard_map/ppermute | solution.py:742
  197.3 28.9 %collective-permute-start.22 = (bf16[4,24,3072]{2,1,0:T(8,128)(2,1)}, bf16[4,24,3072]{2,1,0:T(8,128)(2,1)}, u32[]{:S(2)}, u32[]{:S(2)}) collective-permute-start(bf16[4,24,3072]{2,1,0:T(8,128)(2,1)} %get-tuple-element.192), channel_id=1, source_target_pairs={{0,4},{1,5},{2,6},{3,7},{4,0},{5,1},{6,2},{7,3},{8,12},{9,13},{10,... | collective-permute-start | bytes 1769480 | tf_op jit(solution)/shard_map/ppermute | solution.py:742
  197.9 28.3 %collective-permute-start.23 = (bf16[4,24,3072]{2,1,0:T(8,128)(2,1)}, bf16[4,24,3072]{2,1,0:T(8,128)(2,1)}, u32[]{:S(2)}, u32[]{:S(2)}) collective-permute-start(bf16[4,24,3072]{2,1,0:T(8,128)(2,1)} %get-tuple-element.193), channel_id=1, source_target_pairs={{0,6},{1,7},{2,4},{3,5},{4,2},{5,3},{6,0},{7,1},{8,14},{9,15},{10,... | collective-permute-start | bytes 1769480 | tf_op jit(solution)/shard_map/ppermute | solution.py:742
  204.9 32.6 %all-to-all-start = ((bf16[4,8,3072]{2,1,0:T(8,128)(2,1)}), bf16[4,8,3072]{2,1,0:T(8,128)(2,1)}, u32[]{:S(2)}, u32[]{:S(2)}) async-start(bf16[4,8,3072]{2,1,0:T(8,128)(2,1)} %broadcast_in_dim.38), calls=%async_computation | async-start | bytes 393216 | tf_op jit(solution)/shard_map/all_to_all | solution.py:760
  208.9 23.1 %collective-permute-start.27 = (bf16[2,96,768]{2,1,0:T(8,128)(2,1)}, bf16[2,96,768]{2,1,0:T(8,128)(2,1)}, u32[]{:S(2)}, u32[]{:S(2)}) collective-permute-start(bf16[2,96,768]{2,1,0:T(8,128)(2,1)} %get-tuple-element.206), channel_id=1, source_target_pairs={{0,8},{1,9},{2,10},{3,11},{4,12},{5,13},{6,14},{7,15},{8,16},{9,17... | collective-permute-start | bytes 884744 | tf_op jit(solution)/shard_map/ppermute | solution.py:742
  210.4 23.9 %collective-permute-start.28 = (bf16[2,96,768]{2,1,0:T(8,128)(2,1)}, bf16[2,96,768]{2,1,0:T(8,128)(2,1)}, u32[]{:S(2)}, u32[]{:S(2)}) collective-permute-start(bf16[2,96,768]{2,1,0:T(8,128)(2,1)} %get-tuple-element.207), channel_id=1, source_target_pairs={{0,16},{1,17},{2,18},{3,19},{4,20},{5,21},{6,22},{7,23},{8,24},{9,... | collective-permute-start | bytes 884744 | tf_op jit(solution)/shard_map/ppermute | solution.py:742
  212.5 21.9 %collective-permute-start.29 = (bf16[2,96,768]{2,1,0:T(8,128)(2,1)}, bf16[2,96,768]{2,1,0:T(8,128)(2,1)}, u32[]{:S(2)}, u32[]{:S(2)}) collective-permute-start(bf16[2,96,768]{2,1,0:T(8,128)(2,1)} %get-tuple-element.208), channel_id=1, source_target_pairs={{0,24},{1,25},{2,26},{3,27},{4,28},{5,29},{6,30},{7,31},{8,0},{9,1... | collective-permute-start | bytes 884744 | tf_op jit(solution)/shard_map/ppermute | solution.py:742
  229.5 10.8 %collective-permute-start.24 = (bf16[24,3072]{1,0:T(8,128)(2,1)}, bf16[24,3072]{1,0:T(8,128)(2,1)}, u32[]{:S(2)}, u32[]{:S(2)}) collective-permute-start(bf16[24,3072]{1,0:T(8,128)(2,1)} %get-tuple-element.215), channel_id=1, source_target_pairs={{0,8},{1,9},{2,10},{3,11},{4,12},{5,13},{6,14},{7,15},{8,16},{9,17... | collective-permute-start | bytes 442376 | tf_op jit(solution)/shard_map/ppermute | solution.py:742
  231.0 16.2 %collective-permute-start.25 = (bf16[24,3072]{1,0:T(8,128)(2,1)}, bf16[24,3072]{1,0:T(8,128)(2,1)}, u32[]{:S(2)}, u32[]{:S(2)}) collective-permute-start(bf16[24,3072]{1,0:T(8,128)(2,1)} %get-tuple-element.216), channel_id=1, source_target_pairs={{0,16},{1,17},{2,18},{3,19},{4,20},{5,21},{6,22},{7,23},{8,24},{9,... | collective-permute-start | bytes 442376 | tf_op jit(solution)/shard_map/ppermute | solution.py:742
  232.0 15.2 %collective-permute-start.26 = (bf16[24,3072]{1,0:T(8,128)(2,1)}, bf16[24,3072]{1,0:T(8,128)(2,1)}, u32[]{:S(2)}, u32[]{:S(2)}) collective-permute-start(bf16[24,3072]{1,0:T(8,128)(2,1)} %get-tuple-element.217), channel_id=1, source_target_pairs={{0,24},{1,25},{2,26},{3,27},{4,28},{5,29},{6,30},{7,31},{8,0},{9,1... | collective-permute-start | bytes 442376 | tf_op jit(solution)/shard_map/ppermute | solution.py:742
  (25 other events, 249.5 us)
Sparse Core Ops, SparseCore 0:
  11.5 91.5 all-gather.2

commit v5 on v4

--- a/solution.py
+++ b/solution.py
@@ -856,6 +856,34 @@
 everything = (Ellipsis,)
 
 
+def token_gradient_kernel(d_ref, w_ref, before_ref, out_ref):
+    @pl.when(pl.program_id(0) == 0)
+    def _():
+        out_ref[...] = before_ref[...]
+
+    out_ref[...] += dot_nt(d_ref[...], w_ref[...])
+
+
+def token_gradient(dqkv, weights, before):
+    length, width = before.shape
+    parts = 3
+    columns = dqkv.shape[1] // parts
+    whole = pl.BlockSpec((length, width), lambda k: (0, 0))
+    return pl.pallas_call(
+        token_gradient_kernel,
+        grid=(parts,),
+        in_specs=[
+            pl.BlockSpec((length, columns), lambda k: (0, k)),
+            pl.BlockSpec((width, columns), lambda k: (0, k)),
+            whole,
+        ],
+        out_specs=whole,
+        out_shape=jax.ShapeDtypeStruct((length, width), f32),
+        cost_estimate=pl.CostEstimate(flops=0, bytes_accessed=0, transcendentals=0),
+        name="token_gradient",
+    )(dqkv, weights, before)
+
+
 def hold(value, *others):
     return lax.optimization_barrier((value, others))
 
@@ -925,6 +953,8 @@
         tokens, attention_weights, tables, mask, feat_forward, heads
     )
     place = grid.place["c"].reshape(1)
+    normed = first_norm(tokens, mixed, attention_weights, vectors)
+    normed, (mixed_t, grid.vector) = hold(normed, by_core(mixed.T), grid.vector)
     (
         out_tokens,
         grad_one,
@@ -939,8 +969,8 @@
         dvec,
     ) = feed_forward(
         place,
-        *first_norm(tokens, mixed, attention_weights, vectors),
-        by_core(mixed.T),
+        *normed,
+        mixed_t,
         attention_weights,
         ffn_weights,
         up_bias.reshape(wide, 1, hidden),
@@ -1024,12 +1054,11 @@
         ]
         step.write((zs, own, columns), bf16, terms)
     att_sends = step.run("att_sum_core")
-    small, (*small_new, att_sends) = hold(small, *small_new, att_sends)
+    down_new, (up_new, att_sends, small_new) = hold(down_new, up_new, att_sends, small_new)
+    down += [("z", v) for v in down_new]
+    up += [("z", v) for v in up_new]
     small = (small + sum(v.astype(f32) for v in small_new)).astype(bf16)
     small = jnp.broadcast_to(small[None], (ys * xs,) + small.shape)
-    down_new, (up_new, att_sends) = hold(down_new, up_new, att_sends)
-    down += [("z", v) for v in down_new]
-    up += [("z", v) for v in up_new]
     att_new = grid.send(att_sends, "yx")
 
     here = dict(z=0, y=0, x=0)
@@ -1044,7 +1073,7 @@
     dqkv, (small, *sends) = hold(dqkv, small, *sends)
     small = grid.swap(small, "yx")
     ffn_new = grid.send(sends, "z")
-    grad_tokens = grad_one + dot_nt(dqkv, attention_weights[:, : 3 * width])
+    grad_tokens = token_gradient(dqkv, attention_weights, grad_one)
     att_new, (grad_tokens, *sends) = hold(att_new, grad_tokens, *sends)
     att_new = [("z", v) for v in att_new]
 

time: 259 us -> 254 us (0.981)
  Pallas kernels: 116 us -> 123 us
  matrix products: 6.34 us -> 0 us
  waiting for transfers between devices: 56.8 us -> 52.7 us
    pallas_call x0 -> x1, Pallas kernels: none -> 6.43 us  [token_gradient(): pl.pallas_call(token_gradient_kernel, grid=(parts,), in_specs=[pl.BlockSp...]
    dot_general x1 -> x0, matrix products: 6.34 us -> none  [dot_nt(): return lax.dot_general(a, b, nt_dims, preferred_element_type=f32)]
    ppermute x30, waiting for transfers between devices: 47.6 us -> 42.8 us  [shift(): return lax.ppermute(value, ('batch', 'wide'), pairs)]
  transfers between devices with their start and end apart: 32 -> 32, of which waited for: 17 -> 15; matrix products, arithmetic and copies ran while one was open for 11% -> 9% of each run, Pallas kernels for 31% -> 34%
where the time goes in v5:
time: 254 us; the launch traced here: 252 us
  Pallas kernels  123 us (48%)
  waiting for transfers between devices  52.7 us (21%)
  starting transfers between devices  39.3 us (15%)
  between operations  14.5 us (6%)
  other arithmetic  12.2 us (5%)
  local copies, waits for them, and re-layouts  9.96 us (4%)
    ppermute x30, waiting for transfers between devices, shift(): return lax.ppermute(value, ('batch', 'wide'), pairs)  42.8 us
    ppermute x30, starting transfers between devices, shift(): return lax.ppermute(value, ('batch', 'wide'), pairs)  35.3 us
    pallas_call x8, Pallas kernels, run(): pl.pallas_call(kernel, grid_spec=pltpu.PrefetchScalarGridSpec(num_scalar_...  28.8 us
    pallas_call x1, Pallas kernels, feed_forward(): pl.pallas_call(ffn_kernel, grid_spec=pltpu.PrefetchScalarGridSpec(num_sca...  27.2 us
    pallas_call x1, Pallas kernels, attend_back(): pl.pallas_call(partial(attend_back_kernel, scale), grid_spec=pltpu.Prefet...  24.4 us
    pallas_call x1, Pallas kernels, attend(): pl.pallas_call(partial(attend_kernel, scale), grid=(pairs,), in_specs=[wh...  16.5 us
    all_gather x1, waiting for transfers between devices, per_device(): lax.all_gather(ffn_shard, ('wide', 'batch'), axis=0, tiled=False)  9.9 us
    pallas_call x1, Pallas kernels, token_gradient(): pl.pallas_call(token_gradient_kernel, grid=(parts,), in_specs=[pl.BlockSp...  6.43 us
  transfers between devices with their start and end apart: 32, of which 15 were waited for; matrix products, arithmetic and copies ran while one was open for 9% of the time, Pallas kernels for 34%

profile of v5, /device:TPU:0, one launch (start us, length us, event | category | flops | bytes accessed | tf_op | source)
XLA Modules:
  0.0 251.7 jit_solution(5674197566313370704)
XLA Ops:
  10.7 3.0 %collective-permute-start = (bf16[1,1,1,1,24,3072]{5,4,3,2,1,0:T(8,128)(2,1)}, bf16[1,1,1,1,24,3072]{5,4,3,2,1,0:T(8,128)(2,1)S(1)}, u32[]{:S(2)}, u32[]{:S(2)}) collective-permute-start(bf16[1,1,1,1,24,3072]{5,4,3,2,1,0:T(8,128)(2,1)} %bitcast.72), channel_id=1, source_target_pairs={{0,8},{1,9},{2,10},{3,11},{4,12},{5,13},{6,14},{7,15},{8,16},{9,17... | collective-permute-start | bytes 442376 | tf_op jit(solution)/shard_map/ppermute | solution.py:742
  20.8 5.5 %collective-permute-done.1 = bf16[1,1,1,1,24,3072]{5,4,3,2,1,0:T(8,128)(2,1)S(1)} collective-permute-done((bf16[1,1,1,1,24,3072]{5,4,3,2,1,0:T(8,128)(2,1)}, bf16[1,1,1,1,24,3072]{5,4,3,2,1,0:T(8,128)(2,1)S(1)}, u32[]{:S(2)}, u32[]{:S(2)}) %collective-permute-start.1) | collective-permute-done | bytes 147488 | tf_op jit(solution)/shard_map/ppermute | solution.py:742
  29.5 5.7 %collective-permute-done.3 = bf16[4,1,1,1,24,1536]{5,4,3,2,1,0:T(8,128)(2,1)S(1)} collective-permute-done((bf16[4,1,1,1,24,1536]{5,4,3,2,1,0:T(8,128)(2,1)S(1)}, bf16[4,1,1,1,24,1536]{5,4,3,2,1,0:T(8,128)(2,1)S(1)}, u32[]{:S(2)}, u32[]{:S(2)}) %collective-permute-start.3) | collective-permute-done | bytes 294944 | tf_op jit(solution)/shard_map/ppermute | solution.py:742
  44.7 5.4 %toeplitz.1.table_ref = f32[12,128,1024]{2,1,0:T(8,128)} custom-call(f32[6,2,1024]{2,1,0:T(2,128)} %reshape.149.bias_ref), custom_call_target="tpu_custom_call" | custom-call | flops 5000000000 | bytes 8000000 | tf_op jit(solution)/shard_map/toeplitz/pallas_call | solution.py:41
  50.7 9.2 %collective-permute-done.6 = bf16[4,2,1,1,24,1536]{5,4,3,2,1,0:T(8,128)(2,1)S(1)} collective-permute-done((bf16[4,2,1,1,24,1536]{5,4,3,2,1,0:T(8,128)(2,1)S(1)}, bf16[4,2,1,1,24,1536]{5,4,3,2,1,0:T(8,128)(2,1)S(1)}, u32[]{:S(2)}, u32[]{:S(2)}) %collective-permute-start.6) | collective-permute-done | bytes 589856 | tf_op jit(solution)/shard_map/ppermute | solution.py:742
  68.8 2.7 %pad_maximum_fusion.w_ref.wo_ref = bf16[768,3072]{1,0:T(8,128)(2,1)} fusion(bf16[768,1536]{1,0:T(8,128)(2,1)S(1)} %bitcast.66, bf16[768,1536]{1,0:T(8,128)(2,1)S(1)} %bitcast.65), kind=kLoop, calls=%fused_computation | loop fusion | flops 9437184 | bytes 9437184 | tf_op jit(solution)/shard_map/concatenate | solution.py:949
  71.5 16.5 %attend.1 = (bf16[512,768]{1,0:T(8,128)(2,1)}, f32[512,768]{1,0:T(8,128)}, f32[512,1536]{1,0:T(8,128)}, f32[512,1536]{1,0:T(8,128)}, bf16[512,768]{1,0:T(8,128)(2,1)}, /*index=5*/f32[512,768]{1,0:T(8,128)}) custom-call(bf16[512,768]{1,0:T(8,128)(2,1)} %tok_ref.1, bf16[768,3072]{1,0:T(8,128)(2,1)} %pad_maximum_fusion.w_ref.wo_ref, ...), custom_call_target="tpu_custom_call" | custom-call | tf_op jit(solution)/shard_map/attend/pallas_call | solution.py:131
  88.0 4.9 %first_norm.1 = (bf16[512,768]{1,0:T(8,128)(2,1)}, bf16[768,512]{1,0:T(8,128)(2,1)}, f32[512,768]{1,0:T(8,128)}, f32[512,1]{1,0:T(8,128)}) custom-call(bf16[512,768]{1,0:T(8,128)(2,1)} %tok_ref.1, bf16[512,768]{1,0:T(8,128)(2,1)} %get-tuple-element.139.mixed_ref, bf16[768,3072]{1,0:T(8,128)(2,1)} %pad_maximum_fusion.w_ref.wo_ref, f32[8,768]{1,0:T(8,128)} %stack.39.vec_ref), custom_call_target="tpu_custom_call" | custom-call | tf_op jit(solution)/shard_map/first_norm/pallas_call | solution.py:558
  94.1 9.9 %all-gather.3.cloned.1.call-done = bf16[6144,768]{1,0:T(8,128)(2,1)} async-done(((bf16[192,768]{1,0:T(8,128)(2,1)}), bf16[6144,768]{1,0:T(8,128)(2,1)}) %all-gather.3.cloned.1.call-update) | async-done | bytes 9437200 | tf_op jit(solution)/shard_map/all_gather | solution.py:950
  104.0 27.2 %feed_forward.1 = (bf16[512,768]{1,0:T(8,128)(2,1)}, f32[512,768]{1,0:T(8,128)}, bf16[2,8,96,768]{3,2,1,0:T(8,128)(2,1)}, bf16[2,8,96,768]{3,2,1,0:T(8,128)(2,1)...) custom-call(s32[1]{0:T(128)} %bitcast.place_ref, ...), custom_call_target="tpu_custom_call" | custom-call | tf_op jit(solution)/shard_map/feed_forward/pallas_call | solution.py:618
  131.9 5.9 %ffn_last.1 = (f32[512,768]{1,0:T(8,128)}, bf16[512,768]{1,0:T(8,128)(2,1)}, bf16[384,768]{1,0:T(8,128)(2,1)}, bf16[384,768]{1,0:T(8,128)(2,1)}, f32[8,768]{1,0:T(8,128)}) custom-call(s32[1]{0:T(128)} %bitcast.place_ref, f32[512,768]{1,0:T(8,128)} %get-tuple-element.154.acc_ref, f32[512,768]{1,0:T(8,128)} %get-tuple-element.147.xhat_ref, ...), custom_call_target="tpu_custom_call" | custom-call | tf_op jit(solution)/shard_map/ffn_last/pallas_call | solution.py:678
  139.6 5.1 %ffn_sum_core.1 = (bf16[2,4,96,768]{3,2,1,0:T(8,128)(2,1)}, bf16[4,2,96,768]{3,2,1,0:T(8,128)(2,1)}) custom-call(s32[4]{0:T(128)} %pad_add_fusion.vector_ref, bf16[2,4,2,96,768]{4,3,2,1,0:T(8,128)(2,1)} %bitcast.50, bf16[2,4,2,96,768]{4,3,2,1,0:T(8,128)(2,1)} %bitcast.24.refs_1_.refs_5_.refs_13_.refs_21_.refs_8_, bf16[2,4,2,96,768]{4,3,2,1,0:T(8,128)(2,1)} %bitcast.44, ...), custom_call_target="tpu_custom_call" | custom-call | tf_op jit(solution)/shard_map/ffn_sum_core/pallas_call | solution.py:841
  146.8 24.4 %attend_back.1 = (bf16[384,2304]{1,0:T(8,128)(2,1)}, bf16[384,2304]{1,0:T(8,128)(2,1)}, bf16[512,2304]{1,0:T(8,128)(2,1)}, f32[8,3072]{1,0:T(8,128)}) custom-call(s32[1]{0:T(128)} %bitcast.place_ref, bf16[768,512]{1,0:T(8,128)(2,1)} %bitcast.67, f32[12,128,1024]{2,1,0:T(8,128)} %toeplitz.1.table_ref, f32[4,512]{1,0:T(4,128)} %compare_select_fusion.mask_ref, ...), custom_call_target="tpu_custom_call" | custom-call | tf_op jit(solution)/shard_map/attend_back/pallas_call | solution.py:303
  174.9 3.9 %ffn_sum_plane.1 = (bf16[4,96,768]{2,1,0:T(8,128)(2,1)}, bf16[4,96,768]{2,1,0:T(8,128)(2,1)}) custom-call(s32[4]{0:T(128)} %pad_add_fusion.vector_ref, bf16[2,4,2,96,768]{4,3,2,1,0:T(8,128)(2,1)} %bitcast.51, bf16[2,4,2,96,768]{4,3,2,1,0:T(8,128)(2,1)} %bitcast.24.refs_1_.refs_5_.refs_13_.refs_21_.refs_8_, ...), custom_call_target="tpu_custom_call" | custom-call | tf_op jit(solution)/shard_map/ffn_sum_plane/pallas_call | solution.py:841
  187.2 4.0 %att_sum_core.1 = (bf16[4,24,3072]{2,1,0:T(8,128)(2,1)}, bf16[4,24,3072]{2,1,0:T(8,128)(2,1)}, bf16[4,24,3072]{2,1,0:T(8,128)(2,1)}) custom-call(s32[4]{0:T(128)} %pad_add_fusion.vector_ref, bf16[4,2,2,24,2304]{4,3,2,1,0:T(8,128)(2,1)} %bitcast.37, bf16[4,2,2,24,2304]{4,3,2,1,0:T(8,128)(2,1)} %bitcast.28.refs_1_.refs_5_.refs_9_.refs_4_.refs_11_.refs_18_, ...), custom_call_target="tpu_custom_call" | custom-call | tf_op jit(solution)/shard_map/att_sum_core/pallas_call | solution.py:841
  191.3 3.5 %collective-permute-done.13.refs_7_.refs_15_.refs_23_.refs_10_ = bf16[4,96,768]{2,1,0:T(8,128)(2,1)} collective-permute-done((bf16[4,96,768]{2,1,0:T(8,128)(2,1)}, bf16[4,96,768]{2,1,0:T(8,128)(2,1)}, u32[]{:S(2)}, u32[]{:S(2)}) %collective-permute-start.13) | collective-permute-done | bytes 589856 | tf_op jit(solution)/shard_map/ppermute | solution.py:742
  199.6 3.9 %ffn_sum_second.1 = (bf16[2,96,768]{2,1,0:T(8,128)(2,1)}, bf16[2,96,768]{2,1,0:T(8,128)(2,1)}, bf16[2,96,768]{2,1,0:T(8,128)(2,1)}) custom-call(s32[4]{0:T(128)} %pad_add_fusion.vector_ref, bf16[2,4,2,96,768]{4,3,2,1,0:T(8,128)(2,1)} %bitcast.46, bf16[2,4,2,96,768]{4,3,2,1,0:T(8,128)(2,1)} %bitcast.26.refs_3_.refs_4_.refs_1_.refs_9_.refs_17_, ...), custom_call_target="tpu_custom_call" | custom-call | tf_op jit(solution)/shard_map/ffn_sum_second/pallas_call | solution.py:841
  206.6 5.1 %collective-permute-done.21.refs_0_.refs_7_.refs_14_ = bf16[4,24,3072]{2,1,0:T(8,128)(2,1)} collective-permute-done((bf16[4,24,3072]{2,1,0:T(8,128)(2,1)}, bf16[4,24,3072]{2,1,0:T(8,128)(2,1)}, u32[]{:S(2)}, u32[]{:S(2)}) %collective-permute-start.21) | collective-permute-done | bytes 589856 | tf_op jit(solution)/shard_map/ppermute | solution.py:742
  213.6 4.0 %all-to-all-start = ((bf16[4,8,3072]{2,1,0:T(8,128)(2,1)}), bf16[4,8,3072]{2,1,0:T(8,128)(2,1)}, u32[]{:S(2)}, u32[]{:S(2)}) async-start(bf16[4,8,3072]{2,1,0:T(8,128)(2,1)} %broadcast_in_dim.38), calls=%async_computation | async-start | bytes 393216 | tf_op jit(solution)/shard_map/all_to_all | solution.py:760
  217.6 6.4 %token_gradient.1 = f32[512,768]{1,0:T(8,128)} custom-call(bf16[512,2304]{1,0:T(8,128)(2,1)} %get-tuple-element.208.d_ref, bf16[768,3072]{1,0:T(8,128)(2,1)} %pad_maximum_fusion.w_ref.wo_ref, f32[512,768]{1,0:T(8,128)} %get-tuple-element.209.before_ref), custom_call_target="tpu_custom_call" | custom-call | tf_op jit(solution)/shard_map/token_gradient/pallas_call | solution.py:872
  224.7 3.3 %att_sum_plane.1 = (bf16[24,3072]{1,0:T(8,128)(2,1)}, bf16[24,3072]{1,0:T(8,128)(2,1)}, bf16[24,3072]{1,0:T(8,128)(2,1)}) custom-call(s32[4]{0:T(128)} %pad_add_fusion.vector_ref, bf16[4,24,3072]{2,1,0:T(8,128)(2,1)} %collective-permute-done.21.refs_0_.refs_7_.refs_14_, bf16[4,24,3072]{2,1,0:T(8,128)(2,1)} %collective-permute-done.22.refs_1_.refs_8_.refs_15_, ...), custom_call_target="tpu_custom_call" | custom-call | tf_op jit(solution)/shard_map/att_sum_plane/pallas_call | solution.py:841
  232.9 3.2 %ffn_sum_last.1 = (f32[96,768]{1,0:T(8,128)}, f32[96,768]{1,0:T(8,128)}) custom-call(s32[4]{0:T(128)} %pad_add_fusion.vector_ref, bf16[2,96,768]{2,1,0:T(8,128)(2,1)} %collective-permute-done.27.refs_0_, bf16[2,96,768]{2,1,0:T(8,128)(2,1)} %collective-permute-done.28.refs_1_, bf16[2,96,768]{2,1,0:T(8,128)(2,1)} %collective-permute-done.29.refs_2_, ...), custom_call_target="tpu_custom_call" | custom-call | tf_op jit(solution)/shard_map/ffn_sum_last/pallas_call | solution.py:841
  236.0 2.8 %att_sum_own.1 = (f32[24,3072]{1,0:T(8,128)}, f32[3072]{0:T(1024)}, f32[768]{0:T(1024)}, f32[768]{0:T(1024)}, f32[768]{0:T(1024)}, /*index=5*/f32[768]{0:T(1024)}, f32[768]{0:T(1024)}, f32[12,1024]{1,0:T(8,128)}) custom-call(s32[4]{0:T(128)} %pad_add_fusion.vector_ref, bf16[4,24,3072]{2,1,0:T(8,128)(2,1)} %collective-permute-done.21.refs_0_.refs_7_.refs_14_, ...), custom_call_target="tpu_custom_call" | custom-call | tf_op jit(solution)/shard_map/att_sum_own/pallas_call | solution.py:841
  238.8 3.5 %collective-permute-done.25.refs_2_ = bf16[24,3072]{1,0:T(8,128)(2,1)} collective-permute-done((bf16[24,3072]{1,0:T(8,128)(2,1)}, bf16[24,3072]{1,0:T(8,128)(2,1)}, u32[]{:S(2)}, u32[]{:S(2)}) %collective-permute-start.25) | collective-permute-done | bytes 147488 | tf_op jit(solution)/shard_map/ppermute | solution.py:742
  (144 shorter events, 68.1 us)
Async XLA Ops:
  7.2 96.9 %all-gather.3.cloned.1.call-start = ((), (), s32[]{:S(2)}) async-start(), calls=%async_computation.1 | async-start | bytes 9732096 | tf_op jit(solution)/shard_map/all_gather | solution.py:950
  10.7 10.0 %collective-permute-start = (bf16[1,1,1,1,24,3072]{5,4,3,2,1,0:T(8,128)(2,1)}, bf16[1,1,1,1,24,3072]{5,4,3,2,1,0:T(8,128)(2,1)S(1)}, u32[]{:S(2)}, u32[]{:S(2)}) collective-permute-start(bf16[1,1,1,1,24,3072]{5,4,3,2,1,0:T(8,128)(2,1)} %bitcast.72), channel_id=1, source_target_pairs={{0,8},{1,9},{2,10},{3,11},{4,12},{5,13},{6,14},{7,15},{8,16},{9,17... | collective-permute-start | bytes 442376 | tf_op jit(solution)/shard_map/ppermute | solution.py:742
  13.7 12.5 %collective-permute-start.1 = (bf16[1,1,1,1,24,3072]{5,4,3,2,1,0:T(8,128)(2,1)}, bf16[1,1,1,1,24,3072]{5,4,3,2,1,0:T(8,128)(2,1)S(1)}, u32[]{:S(2)}, u32[]{:S(2)}) collective-permute-start(bf16[1,1,1,1,24,3072]{5,4,3,2,1,0:T(8,128)(2,1)} %bitcast.73), channel_id=1, source_target_pairs={{0,16},{1,17},{2,18},{3,19},{4,20},{5,21},{6,22},{7,23},{8,24},{9,... | collective-permute-start | bytes 442376 | tf_op jit(solution)/shard_map/ppermute | solution.py:742
  16.3 9.9 %collective-permute-start.2 = (bf16[1,1,1,1,24,3072]{5,4,3,2,1,0:T(8,128)(2,1)}, bf16[1,1,1,1,24,3072]{5,4,3,2,1,0:T(8,128)(2,1)S(1)}, u32[]{:S(2)}, u32[]{:S(2)}) collective-permute-start(bf16[1,1,1,1,24,3072]{5,4,3,2,1,0:T(8,128)(2,1)} %bitcast.74), channel_id=1, source_target_pairs={{0,24},{1,25},{2,26},{3,27},{4,28},{5,29},{6,30},{7,31},{8,0},{9,1... | collective-permute-start | bytes 442376 | tf_op jit(solution)/shard_map/ppermute | solution.py:742
  26.3 8.9 %collective-permute-start.3 = (bf16[4,1,1,1,24,1536]{5,4,3,2,1,0:T(8,128)(2,1)S(1)}, bf16[4,1,1,1,24,1536]{5,4,3,2,1,0:T(8,128)(2,1)S(1)}, u32[]{:S(2)}, u32[]{:S(2)}) collective-permute-start(bf16[4,1,1,1,24,1536]{5,4,3,2,1,0:T(8,128)(2,1)S(1)} %get-tuple-element.252), channel_id=1, source_target_pairs={{0,2},{1,3},{2,0},{3,1},{4,6},{5,7},{6,4},{7,5},{8,10},{9,11},{10,... | collective-permute-start | bytes 884744 | tf_op jit(solution)/shard_map/ppermute | solution.py:742
  37.4 22.5 %collective-permute-start.6 = (bf16[4,2,1,1,24,1536]{5,4,3,2,1,0:T(8,128)(2,1)S(1)}, bf16[4,2,1,1,24,1536]{5,4,3,2,1,0:T(8,128)(2,1)S(1)}, u32[]{:S(2)}, u32[]{:S(2)}) collective-permute-start(bf16[4,2,1,1,24,1536]{5,4,3,2,1,0:T(8,128)(2,1)S(1)} %pad_maximum_fusion.6), channel_id=1, source_target_pairs={{0,2},{1,3},{2,0},{3,1},{4,6},{5,7},{6,4},{7,5},{8,10},{9,11},{10,... | collective-permute-start | bytes 1769480 | tf_op jit(solution)/shard_map/ppermute | solution.py:742
  41.2 18.8 %collective-permute-start.5 = (bf16[4,1,2,1,24,1536]{5,4,3,2,1,0:T(8,128)(2,1)S(1)}, bf16[4,1,2,1,24,1536]{5,4,3,2,1,0:T(8,128)(2,1)}, u32[]{:S(2)}, u32[]{:S(2)}) collective-permute-start(bf16[4,1,2,1,24,1536]{5,4,3,2,1,0:T(8,128)(2,1)S(1)} %pad_maximum_fusion.5), channel_id=1, source_target_pairs={{0,4},{1,5},{2,6},{3,7},{4,0},{5,1},{6,2},{7,3},{8,12},{9,13},{10,... | collective-permute-start | bytes 1769480 | tf_op jit(solution)/shard_map/ppermute | solution.py:742
  144.7 28.5 %collective-permute-start.11 = (bf16[2,4,96,768]{3,2,1,0:T(8,128)(2,1)}, bf16[2,4,96,768]{3,2,1,0:T(8,128)(2,1)}, u32[]{:S(2)}, u32[]{:S(2)}) collective-permute-start(bf16[2,4,96,768]{3,2,1,0:T(8,128)(2,1)} %get-tuple-element.181), channel_id=1, source_target_pairs={{0,4},{1,5},{2,6},{3,7},{4,0},{5,1},{6,2},{7,3},{8,12},{9,13},{10,... | collective-permute-start | bytes 3538952 | tf_op jit(solution)/shard_map/ppermute | solution.py:742
  146.2 28.2 %collective-permute-start.12 = (bf16[4,2,96,768]{3,2,1,0:T(8,128)(2,1)}, bf16[4,2,96,768]{3,2,1,0:T(8,128)(2,1)}, u32[]{:S(2)}, u32[]{:S(2)}) collective-permute-start(bf16[4,2,96,768]{3,2,1,0:T(8,128)(2,1)} %get-tuple-element.182), channel_id=1, source_target_pairs={{0,2},{1,3},{2,0},{3,1},{4,6},{5,7},{6,4},{7,5},{8,10},{9,11},{10,... | collective-permute-start | bytes 3538952 | tf_op jit(solution)/shard_map/ppermute | solution.py:742
  174.4 10.5 %collective-permute-start.15 = (bf16[384,2304]{1,0:T(8,128)(2,1)}, bf16[384,2304]{1,0:T(8,128)(2,1)}, u32[]{:S(2)}, u32[]{:S(2)}) collective-permute-start(bf16[384,2304]{1,0:T(8,128)(2,1)} %get-tuple-element.189), channel_id=1, source_target_pairs={{0,1},{1,0},{2,3},{3,2},{4,5},{5,4},{6,7},{7,6},{8,9},{9,8},{10,11... | collective-permute-start | bytes 5308424 | tf_op jit(solution)/shard_map/ppermute | solution.py:742
  174.9 9.0 %collective-permute-start.16 = (bf16[384,768]{1,0:T(8,128)(2,1)}, bf16[384,768]{1,0:T(8,128)(2,1)}, u32[]{:S(2)}, u32[]{:S(2)}) collective-permute-start(bf16[384,768]{1,0:T(8,128)(2,1)} %get-tuple-element.191), channel_id=1, source_target_pairs={{0,1},{1,0},{2,3},{3,2},{4,5},{5,4},{6,7},{7,6},{8,9},{9,8},{10,11... | collective-permute-start | bytes 1769480 | tf_op jit(solution)/shard_map/ppermute | solution.py:742
  178.8 16.1 %collective-permute-start.13 = (bf16[4,96,768]{2,1,0:T(8,128)(2,1)}, bf16[4,96,768]{2,1,0:T(8,128)(2,1)}, u32[]{:S(2)}, u32[]{:S(2)}) collective-permute-start(bf16[4,96,768]{2,1,0:T(8,128)(2,1)} %get-tuple-element.185), channel_id=1, source_target_pairs={{0,2},{1,3},{2,0},{3,1},{4,6},{5,7},{6,4},{7,5},{8,10},{9,11},{10,... | collective-permute-start | bytes 1769480 | tf_op jit(solution)/shard_map/ppermute | solution.py:742
  179.3 15.8 %collective-permute-start.14 = (bf16[4,96,768]{2,1,0:T(8,128)(2,1)}, bf16[4,96,768]{2,1,0:T(8,128)(2,1)}, u32[]{:S(2)}, u32[]{:S(2)}) collective-permute-start(bf16[4,96,768]{2,1,0:T(8,128)(2,1)} %get-tuple-element.186), channel_id=1, source_target_pairs={{0,4},{1,5},{2,6},{3,7},{4,0},{5,1},{6,2},{7,3},{8,12},{9,13},{10,... | collective-permute-start | bytes 1769480 | tf_op jit(solution)/shard_map/ppermute | solution.py:742
  182.4 8.9 %collective-permute-start.18 = (bf16[8,3072]{1,0:T(8,128)(2,1)}, bf16[8,3072]{1,0:T(8,128)(2,1)}, u32[]{:S(2)}, u32[]{:S(2)}) collective-permute-start(bf16[8,3072]{1,0:T(8,128)(2,1)} %get-tuple-element.235), channel_id=1, source_target_pairs={{0,8},{1,9},{2,10},{3,11},{4,12},{5,13},{6,14},{7,15},{8,16},{9,17... | collective-permute-start | bytes 147464 | tf_op jit(solution)/shard_map/ppermute | solution.py:742
  195.1 16.6 %collective-permute-start.21 = (bf16[4,24,3072]{2,1,0:T(8,128)(2,1)}, bf16[4,24,3072]{2,1,0:T(8,128)(2,1)}, u32[]{:S(2)}, u32[]{:S(2)}) collective-permute-start(bf16[4,24,3072]{2,1,0:T(8,128)(2,1)} %get-tuple-element.196), channel_id=1, source_target_pairs={{0,2},{1,3},{2,0},{3,1},{4,6},{5,7},{6,4},{7,5},{8,10},{9,11},{10,... | collective-permute-start | bytes 1769480 | tf_op jit(solution)/shard_map/ppermute | solution.py:742
  196.6 27.5 %collective-permute-start.22 = (bf16[4,24,3072]{2,1,0:T(8,128)(2,1)}, bf16[4,24,3072]{2,1,0:T(8,128)(2,1)}, u32[]{:S(2)}, u32[]{:S(2)}) collective-permute-start(bf16[4,24,3072]{2,1,0:T(8,128)(2,1)} %get-tuple-element.197), channel_id=1, source_target_pairs={{0,4},{1,5},{2,6},{3,7},{4,0},{5,1},{6,2},{7,3},{8,12},{9,13},{10,... | collective-permute-start | bytes 1769480 | tf_op jit(solution)/shard_map/ppermute | solution.py:742
  197.1 27.6 %collective-permute-start.23 = (bf16[4,24,3072]{2,1,0:T(8,128)(2,1)}, bf16[4,24,3072]{2,1,0:T(8,128)(2,1)}, u32[]{:S(2)}, u32[]{:S(2)}) collective-permute-start(bf16[4,24,3072]{2,1,0:T(8,128)(2,1)} %get-tuple-element.198), channel_id=1, source_target_pairs={{0,6},{1,7},{2,4},{3,5},{4,2},{5,3},{6,0},{7,1},{8,14},{9,15},{10,... | collective-permute-start | bytes 1769480 | tf_op jit(solution)/shard_map/ppermute | solution.py:742
  204.2 26.3 %collective-permute-start.27 = (bf16[2,96,768]{2,1,0:T(8,128)(2,1)}, bf16[2,96,768]{2,1,0:T(8,128)(2,1)}, u32[]{:S(2)}, u32[]{:S(2)}) collective-permute-start(bf16[2,96,768]{2,1,0:T(8,128)(2,1)} %get-tuple-element.210), channel_id=1, source_target_pairs={{0,8},{1,9},{2,10},{3,11},{4,12},{5,13},{6,14},{7,15},{8,16},{9,17... | collective-permute-start | bytes 884744 | tf_op jit(solution)/shard_map/ppermute | solution.py:742
  205.6 27.2 %collective-permute-start.28 = (bf16[2,96,768]{2,1,0:T(8,128)(2,1)}, bf16[2,96,768]{2,1,0:T(8,128)(2,1)}, u32[]{:S(2)}, u32[]{:S(2)}) collective-permute-start(bf16[2,96,768]{2,1,0:T(8,128)(2,1)} %get-tuple-element.211), channel_id=1, source_target_pairs={{0,16},{1,17},{2,18},{3,19},{4,20},{5,21},{6,22},{7,23},{8,24},{9,... | collective-permute-start | bytes 884744 | tf_op jit(solution)/shard_map/ppermute | solution.py:742
  211.7 21.2 %collective-permute-start.29 = (bf16[2,96,768]{2,1,0:T(8,128)(2,1)}, bf16[2,96,768]{2,1,0:T(8,128)(2,1)}, u32[]{:S(2)}, u32[]{:S(2)}) collective-permute-start(bf16[2,96,768]{2,1,0:T(8,128)(2,1)} %get-tuple-element.212), channel_id=1, source_target_pairs={{0,24},{1,25},{2,26},{3,27},{4,28},{5,29},{6,30},{7,31},{8,0},{9,1... | collective-permute-start | bytes 884744 | tf_op jit(solution)/shard_map/ppermute | solution.py:742
  213.6 22.4 %all-to-all-start = ((bf16[4,8,3072]{2,1,0:T(8,128)(2,1)}), bf16[4,8,3072]{2,1,0:T(8,128)(2,1)}, u32[]{:S(2)}, u32[]{:S(2)}) async-start(bf16[4,8,3072]{2,1,0:T(8,128)(2,1)} %broadcast_in_dim.38), calls=%async_computation | async-start | bytes 393216 | tf_op jit(solution)/shard_map/all_to_all | solution.py:760
  228.0 10.9 %collective-permute-start.24 = (bf16[24,3072]{1,0:T(8,128)(2,1)}, bf16[24,3072]{1,0:T(8,128)(2,1)}, u32[]{:S(2)}, u32[]{:S(2)}) collective-permute-start(bf16[24,3072]{1,0:T(8,128)(2,1)} %get-tuple-element.219), channel_id=1, source_target_pairs={{0,8},{1,9},{2,10},{3,11},{4,12},{5,13},{6,14},{7,15},{8,16},{9,17... | collective-permute-start | bytes 442376 | tf_op jit(solution)/shard_map/ppermute | solution.py:742
  229.5 12.9 %collective-permute-start.25 = (bf16[24,3072]{1,0:T(8,128)(2,1)}, bf16[24,3072]{1,0:T(8,128)(2,1)}, u32[]{:S(2)}, u32[]{:S(2)}) collective-permute-start(bf16[24,3072]{1,0:T(8,128)(2,1)} %get-tuple-element.220), channel_id=1, source_target_pairs={{0,16},{1,17},{2,18},{3,19},{4,20},{5,21},{6,22},{7,23},{8,24},{9,... | collective-permute-start | bytes 442376 | tf_op jit(solution)/shard_map/ppermute | solution.py:742
  230.5 11.9 %collective-permute-start.26 = (bf16[24,3072]{1,0:T(8,128)(2,1)}, bf16[24,3072]{1,0:T(8,128)(2,1)}, u32[]{:S(2)}, u32[]{:S(2)}) collective-permute-start(bf16[24,3072]{1,0:T(8,128)(2,1)} %get-tuple-element.221), channel_id=1, source_target_pairs={{0,24},{1,25},{2,26},{3,27},{4,28},{5,29},{6,30},{7,31},{8,0},{9,1... | collective-permute-start | bytes 442376 | tf_op jit(solution)/shard_map/ppermute | solution.py:742
  (24 other events, 144.9 us)
Sparse Core Ops, SparseCore 0:
  11.5 92.4 all-gather.2

commit v6 on v5

--- a/solution.py
+++ b/solution.py
@@ -988,10 +988,7 @@
     bias_rows = heads * rels // columns
     extra = -(-(3 + bias_rows) // 8) * 8
     first_row = extra - bias_rows
-    small_top = jnp.concatenate(
-        [dup_bias.reshape(1, columns), dvec.reshape(2, columns), jnp.zeros((extra - 3, columns), f32)]
-    )
-    down_mine, (small_top,) = hold(down_mine, small_top)
+    down_mine, (grad_mixed,) = hold(down_mine, grad_mixed)
     down = [ffn_view(down_mine), ffn_view(down_recv)]
 
     step = Combine(grid, zs)
@@ -1003,7 +1000,12 @@
         step.write((zs, ys, up_rows, hidden), bf16, terms, stepped=0)
     sends = step.run("ffn_sum_core")
     down_sends, up_sends = sends[: ys - 1], sends[ys - 1 :]
-    grad_mixed, (down_sends, up_sends) = hold(grad_mixed, down_sends, up_sends)
+    grad_mixed, (down_sends, up_sends, dup_bias, dvec) = hold(
+        grad_mixed, down_sends, up_sends, dup_bias, dvec
+    )
+    small_top = jnp.concatenate(
+        [dup_bias.reshape(1, columns), dvec.reshape(2, columns), jnp.zeros((extra - 3, columns), f32)]
+    )
     down_new = grid.send(down_sends, "y")
     up_new = grid.send(up_sends, "x")
 

time: 254 us -> 254 us (level)
  transfers between devices with their start and end apart: 32 -> 32, of which waited for: 15 -> 15; matrix products, arithmetic and copies ran while one was open for 9% -> 8% of each run, Pallas kernels for 34% -> 34%
where the time goes in v6:
time: 254 us; the launch traced here: 252 us
  Pallas kernels  123 us (48%)
  waiting for transfers between devices  53.4 us (21%)
  starting transfers between devices  39.3 us (15%)
  between operations  14.5 us (6%)
  other arithmetic  12.2 us (5%)
  local copies, waits for them, and re-layouts  9.19 us (4%)
    ppermute x30, waiting for transfers between devices, shift(): return lax.ppermute(value, ('batch', 'wide'), pairs)  43.5 us
    ppermute x30, starting transfers between devices, shift(): return lax.ppermute(value, ('batch', 'wide'), pairs)  35.3 us
    pallas_call x8, Pallas kernels, run(): pl.pallas_call(kernel, grid_spec=pltpu.PrefetchScalarGridSpec(num_scalar_...  28.9 us
    pallas_call x1, Pallas kernels, feed_forward(): pl.pallas_call(ffn_kernel, grid_spec=pltpu.PrefetchScalarGridSpec(num_sca...  27.2 us
    pallas_call x1, Pallas kernels, attend_back(): pl.pallas_call(partial(attend_back_kernel, scale), grid_spec=pltpu.Prefet...  24.4 us
    pallas_call x1, Pallas kernels, attend(): pl.pallas_call(partial(attend_kernel, scale), grid=(pairs,), in_specs=[wh...  16.5 us
    all_gather x1, waiting for transfers between devices, per_device(): lax.all_gather(ffn_shard, ('wide', 'batch'), axis=0, tiled=False)  9.92 us
    pallas_call x1, Pallas kernels, token_gradient(): pl.pallas_call(token_gradient_kernel, grid=(parts,), in_specs=[pl.BlockSp...  6.43 us
  transfers between devices with their start and end apart: 32, of which 15 were waited for; matrix products, arithmetic and copies ran while one was open for 8% of the time, Pallas kernels for 34%

profile of v6, /device:TPU:0, one launch (start us, length us, event | category | flops | bytes accessed | tf_op | source)
XLA Modules:
  0.0 251.9 jit_solution(1732329168591536669)
XLA Ops:
  10.7 3.0 %collective-permute-start = (bf16[1,1,1,1,24,3072]{5,4,3,2,1,0:T(8,128)(2,1)}, bf16[1,1,1,1,24,3072]{5,4,3,2,1,0:T(8,128)(2,1)S(1)}, u32[]{:S(2)}, u32[]{:S(2)}) collective-permute-start(bf16[1,1,1,1,24,3072]{5,4,3,2,1,0:T(8,128)(2,1)} %bitcast.72), channel_id=1, source_target_pairs={{0,8},{1,9},{2,10},{3,11},{4,12},{5,13},{6,14},{7,15},{8,16},{9,17... | collective-permute-start | bytes 442376 | tf_op jit(solution)/shard_map/ppermute | solution.py:742
  20.8 5.5 %collective-permute-done.1 = bf16[1,1,1,1,24,3072]{5,4,3,2,1,0:T(8,128)(2,1)S(1)} collective-permute-done((bf16[1,1,1,1,24,3072]{5,4,3,2,1,0:T(8,128)(2,1)}, bf16[1,1,1,1,24,3072]{5,4,3,2,1,0:T(8,128)(2,1)S(1)}, u32[]{:S(2)}, u32[]{:S(2)}) %collective-permute-start.1) | collective-permute-done | bytes 147488 | tf_op jit(solution)/shard_map/ppermute | solution.py:742
  29.5 5.7 %collective-permute-done.3 = bf16[4,1,1,1,24,1536]{5,4,3,2,1,0:T(8,128)(2,1)S(1)} collective-permute-done((bf16[4,1,1,1,24,1536]{5,4,3,2,1,0:T(8,128)(2,1)S(1)}, bf16[4,1,1,1,24,1536]{5,4,3,2,1,0:T(8,128)(2,1)S(1)}, u32[]{:S(2)}, u32[]{:S(2)}) %collective-permute-start.3) | collective-permute-done | bytes 294944 | tf_op jit(solution)/shard_map/ppermute | solution.py:742
  44.7 5.4 %toeplitz.1.table_ref = f32[12,128,1024]{2,1,0:T(8,128)} custom-call(f32[6,2,1024]{2,1,0:T(2,128)} %reshape.149.bias_ref), custom_call_target="tpu_custom_call" | custom-call | flops 5000000000 | bytes 8000000 | tf_op jit(solution)/shard_map/toeplitz/pallas_call | solution.py:41
  50.7 9.2 %collective-permute-done.6 = bf16[4,2,1,1,24,1536]{5,4,3,2,1,0:T(8,128)(2,1)S(1)} collective-permute-done((bf16[4,2,1,1,24,1536]{5,4,3,2,1,0:T(8,128)(2,1)S(1)}, bf16[4,2,1,1,24,1536]{5,4,3,2,1,0:T(8,128)(2,1)S(1)}, u32[]{:S(2)}, u32[]{:S(2)}) %collective-permute-start.6) | collective-permute-done | bytes 589856 | tf_op jit(solution)/shard_map/ppermute | solution.py:742
  68.8 2.7 %pad_maximum_fusion.w_ref.wo_ref = bf16[768,3072]{1,0:T(8,128)(2,1)} fusion(bf16[768,1536]{1,0:T(8,128)(2,1)S(1)} %bitcast.66, bf16[768,1536]{1,0:T(8,128)(2,1)S(1)} %bitcast.65), kind=kLoop, calls=%fused_computation | loop fusion | flops 9437184 | bytes 9437184 | tf_op jit(solution)/shard_map/concatenate | solution.py:949
  71.5 16.5 %attend.1 = (bf16[512,768]{1,0:T(8,128)(2,1)}, f32[512,768]{1,0:T(8,128)}, f32[512,1536]{1,0:T(8,128)}, f32[512,1536]{1,0:T(8,128)}, bf16[512,768]{1,0:T(8,128)(2,1)}, /*index=5*/f32[512,768]{1,0:T(8,128)}) custom-call(bf16[512,768]{1,0:T(8,128)(2,1)} %tok_ref.1, bf16[768,3072]{1,0:T(8,128)(2,1)} %pad_maximum_fusion.w_ref.wo_ref, ...), custom_call_target="tpu_custom_call" | custom-call | tf_op jit(solution)/shard_map/attend/pallas_call | solution.py:131
  87.9 4.9 %first_norm.1 = (bf16[512,768]{1,0:T(8,128)(2,1)}, bf16[768,512]{1,0:T(8,128)(2,1)}, f32[512,768]{1,0:T(8,128)}, f32[512,1]{1,0:T(8,128)}) custom-call(bf16[512,768]{1,0:T(8,128)(2,1)} %tok_ref.1, bf16[512,768]{1,0:T(8,128)(2,1)} %get-tuple-element.141.mixed_ref, bf16[768,3072]{1,0:T(8,128)(2,1)} %pad_maximum_fusion.w_ref.wo_ref, f32[8,768]{1,0:T(8,128)} %stack.39.vec_ref), custom_call_target="tpu_custom_call" | custom-call | tf_op jit(solution)/shard_map/first_norm/pallas_call | solution.py:558
  94.1 9.9 %all-gather.3.cloned.1.call-done = bf16[6144,768]{1,0:T(8,128)(2,1)} async-done(((bf16[192,768]{1,0:T(8,128)(2,1)}), bf16[6144,768]{1,0:T(8,128)(2,1)}) %all-gather.3.cloned.1.call-update) | async-done | bytes 9437200 | tf_op jit(solution)/shard_map/all_gather | solution.py:950
  104.0 27.2 %feed_forward.1 = (bf16[512,768]{1,0:T(8,128)(2,1)}, f32[512,768]{1,0:T(8,128)}, bf16[2,8,96,768]{3,2,1,0:T(8,128)(2,1)}, bf16[2,8,96,768]{3,2,1,0:T(8,128)(2,1)...) custom-call(s32[1]{0:T(128)} %bitcast.place_ref, ...), custom_call_target="tpu_custom_call" | custom-call | tf_op jit(solution)/shard_map/feed_forward/pallas_call | solution.py:618
  131.9 5.9 %ffn_last.1 = (f32[512,768]{1,0:T(8,128)}, bf16[512,768]{1,0:T(8,128)(2,1)}, bf16[384,768]{1,0:T(8,128)(2,1)}, bf16[384,768]{1,0:T(8,128)(2,1)}, f32[8,768]{1,0:T(8,128)}) custom-call(s32[1]{0:T(128)} %bitcast.place_ref, f32[512,768]{1,0:T(8,128)} %get-tuple-element.155.acc_ref, f32[512,768]{1,0:T(8,128)} %get-tuple-element.149.xhat_ref, ...), custom_call_target="tpu_custom_call" | custom-call | tf_op jit(solution)/shard_map/ffn_last/pallas_call | solution.py:678
  139.6 5.3 %ffn_sum_core.1 = (bf16[2,4,96,768]{3,2,1,0:T(8,128)(2,1)}, bf16[4,2,96,768]{3,2,1,0:T(8,128)(2,1)}) custom-call(s32[4]{0:T(128)} %pad_add_fusion.vector_ref, bf16[2,4,2,96,768]{4,3,2,1,0:T(8,128)(2,1)} %bitcast.50, bf16[2,4,2,96,768]{4,3,2,1,0:T(8,128)(2,1)} %bitcast.23.refs_1_.refs_5_.refs_13_.refs_21_.refs_8_, bf16[2,4,2,96,768]{4,3,2,1,0:T(8,128)(2,1)} %bitcast.44, ...), custom_call_target="tpu_custom_call" | custom-call | tf_op jit(solution)/shard_map/ffn_sum_core/pallas_call | solution.py:841
  147.8 24.4 %attend_back.1 = (bf16[384,2304]{1,0:T(8,128)(2,1)}, bf16[384,2304]{1,0:T(8,128)(2,1)}, bf16[512,2304]{1,0:T(8,128)(2,1)}, f32[8,3072]{1,0:T(8,128)}) custom-call(s32[1]{0:T(128)} %bitcast.place_ref, bf16[768,512]{1,0:T(8,128)(2,1)} %bitcast.67, f32[12,128,1024]{2,1,0:T(8,128)} %toeplitz.1.table_ref, f32[4,512]{1,0:T(4,128)} %compare_select_fusion.mask_ref, ...), custom_call_target="tpu_custom_call" | custom-call | tf_op jit(solution)/shard_map/attend_back/pallas_call | solution.py:303
  175.1 3.9 %ffn_sum_plane.1 = (bf16[4,96,768]{2,1,0:T(8,128)(2,1)}, bf16[4,96,768]{2,1,0:T(8,128)(2,1)}) custom-call(s32[4]{0:T(128)} %pad_add_fusion.vector_ref, bf16[2,4,2,96,768]{4,3,2,1,0:T(8,128)(2,1)} %bitcast.51, bf16[2,4,2,96,768]{4,3,2,1,0:T(8,128)(2,1)} %bitcast.23.refs_1_.refs_5_.refs_13_.refs_21_.refs_8_, ...), custom_call_target="tpu_custom_call" | custom-call | tf_op jit(solution)/shard_map/ffn_sum_plane/pallas_call | solution.py:841
  187.4 4.0 %att_sum_core.1 = (bf16[4,24,3072]{2,1,0:T(8,128)(2,1)}, bf16[4,24,3072]{2,1,0:T(8,128)(2,1)}, bf16[4,24,3072]{2,1,0:T(8,128)(2,1)}) custom-call(s32[4]{0:T(128)} %pad_add_fusion.vector_ref, bf16[4,2,2,24,2304]{4,3,2,1,0:T(8,128)(2,1)} %bitcast.37, bf16[4,2,2,24,2304]{4,3,2,1,0:T(8,128)(2,1)} %bitcast.28.refs_1_.refs_5_.refs_9_.refs_4_.refs_11_.refs_18_, ...), custom_call_target="tpu_custom_call" | custom-call | tf_op jit(solution)/shard_map/att_sum_core/pallas_call | solution.py:841
  191.4 3.5 %collective-permute-done.13.refs_7_.refs_15_.refs_23_.refs_10_ = bf16[4,96,768]{2,1,0:T(8,128)(2,1)} collective-permute-done((bf16[4,96,768]{2,1,0:T(8,128)(2,1)}, bf16[4,96,768]{2,1,0:T(8,128)(2,1)}, u32[]{:S(2)}, u32[]{:S(2)}) %collective-permute-start.13) | collective-permute-done | bytes 589856 | tf_op jit(solution)/shard_map/ppermute | solution.py:742
  199.7 3.9 %ffn_sum_second.1 = (bf16[2,96,768]{2,1,0:T(8,128)(2,1)}, bf16[2,96,768]{2,1,0:T(8,128)(2,1)}, bf16[2,96,768]{2,1,0:T(8,128)(2,1)}) custom-call(s32[4]{0:T(128)} %pad_add_fusion.vector_ref, bf16[2,4,2,96,768]{4,3,2,1,0:T(8,128)(2,1)} %bitcast.46, bf16[2,4,2,96,768]{4,3,2,1,0:T(8,128)(2,1)} %bitcast.25.refs_3_.refs_4_.refs_1_.refs_9_.refs_17_, ...), custom_call_target="tpu_custom_call" | custom-call | tf_op jit(solution)/shard_map/ffn_sum_second/pallas_call | solution.py:841
  206.8 5.1 %collective-permute-done.21.refs_0_.refs_7_.refs_14_ = bf16[4,24,3072]{2,1,0:T(8,128)(2,1)} collective-permute-done((bf16[4,24,3072]{2,1,0:T(8,128)(2,1)}, bf16[4,24,3072]{2,1,0:T(8,128)(2,1)}, u32[]{:S(2)}, u32[]{:S(2)}) %collective-permute-start.21) | collective-permute-done | bytes 589856 | tf_op jit(solution)/shard_map/ppermute | solution.py:742
  213.8 4.0 %all-to-all-start = ((bf16[4,8,3072]{2,1,0:T(8,128)(2,1)}), bf16[4,8,3072]{2,1,0:T(8,128)(2,1)}, u32[]{:S(2)}, u32[]{:S(2)}) async-start(bf16[4,8,3072]{2,1,0:T(8,128)(2,1)} %broadcast_in_dim.38), calls=%async_computation | async-start | bytes 393216 | tf_op jit(solution)/shard_map/all_to_all | solution.py:760
  217.8 6.4 %token_gradient.1 = f32[512,768]{1,0:T(8,128)} custom-call(bf16[512,2304]{1,0:T(8,128)(2,1)} %get-tuple-element.212.d_ref, bf16[768,3072]{1,0:T(8,128)(2,1)} %pad_maximum_fusion.w_ref.wo_ref, f32[512,768]{1,0:T(8,128)} %get-tuple-element.213.before_ref), custom_call_target="tpu_custom_call" | custom-call | tf_op jit(solution)/shard_map/token_gradient/pallas_call | solution.py:872
  224.9 3.3 %att_sum_plane.1 = (bf16[24,3072]{1,0:T(8,128)(2,1)}, bf16[24,3072]{1,0:T(8,128)(2,1)}, bf16[24,3072]{1,0:T(8,128)(2,1)}) custom-call(s32[4]{0:T(128)} %pad_add_fusion.vector_ref, bf16[4,24,3072]{2,1,0:T(8,128)(2,1)} %collective-permute-done.21.refs_0_.refs_7_.refs_14_, bf16[4,24,3072]{2,1,0:T(8,128)(2,1)} %collective-permute-done.22.refs_1_.refs_8_.refs_15_, ...), custom_call_target="tpu_custom_call" | custom-call | tf_op jit(solution)/shard_map/att_sum_plane/pallas_call | solution.py:841
  233.0 3.2 %ffn_sum_last.1 = (f32[96,768]{1,0:T(8,128)}, f32[96,768]{1,0:T(8,128)}) custom-call(s32[4]{0:T(128)} %pad_add_fusion.vector_ref, bf16[2,96,768]{2,1,0:T(8,128)(2,1)} %collective-permute-done.27.refs_0_, bf16[2,96,768]{2,1,0:T(8,128)(2,1)} %collective-permute-done.28.refs_1_, bf16[2,96,768]{2,1,0:T(8,128)(2,1)} %collective-permute-done.29.refs_2_, ...), custom_call_target="tpu_custom_call" | custom-call | tf_op jit(solution)/shard_map/ffn_sum_last/pallas_call | solution.py:841
  236.2 2.8 %att_sum_own.1 = (f32[24,3072]{1,0:T(8,128)}, f32[3072]{0:T(1024)}, f32[768]{0:T(1024)}, f32[768]{0:T(1024)}, f32[768]{0:T(1024)}, /*index=5*/f32[768]{0:T(1024)}, f32[768]{0:T(1024)}, f32[12,1024]{1,0:T(8,128)}) custom-call(s32[4]{0:T(128)} %pad_add_fusion.vector_ref, bf16[4,24,3072]{2,1,0:T(8,128)(2,1)} %collective-permute-done.21.refs_0_.refs_7_.refs_14_, ...), custom_call_target="tpu_custom_call" | custom-call | tf_op jit(solution)/shard_map/att_sum_own/pallas_call | solution.py:841
  239.0 3.5 %collective-permute-done.25.refs_2_ = bf16[24,3072]{1,0:T(8,128)(2,1)} collective-permute-done((bf16[24,3072]{1,0:T(8,128)(2,1)}, bf16[24,3072]{1,0:T(8,128)(2,1)}, u32[]{:S(2)}, u32[]{:S(2)}) %collective-permute-start.25) | collective-permute-done | bytes 147488 | tf_op jit(solution)/shard_map/ppermute | solution.py:742
  (146 shorter events, 68.0 us)
Async XLA Ops:
  7.2 96.9 %all-gather.3.cloned.1.call-start = ((), (), s32[]{:S(2)}) async-start(), calls=%async_computation.1 | async-start | bytes 9732096 | tf_op jit(solution)/shard_map/all_gather | solution.py:950
  10.7 10.0 %collective-permute-start = (bf16[1,1,1,1,24,3072]{5,4,3,2,1,0:T(8,128)(2,1)}, bf16[1,1,1,1,24,3072]{5,4,3,2,1,0:T(8,128)(2,1)S(1)}, u32[]{:S(2)}, u32[]{:S(2)}) collective-permute-start(bf16[1,1,1,1,24,3072]{5,4,3,2,1,0:T(8,128)(2,1)} %bitcast.72), channel_id=1, source_target_pairs={{0,8},{1,9},{2,10},{3,11},{4,12},{5,13},{6,14},{7,15},{8,16},{9,17... | collective-permute-start | bytes 442376 | tf_op jit(solution)/shard_map/ppermute | solution.py:742
  13.7 12.5 %collective-permute-start.1 = (bf16[1,1,1,1,24,3072]{5,4,3,2,1,0:T(8,128)(2,1)}, bf16[1,1,1,1,24,3072]{5,4,3,2,1,0:T(8,128)(2,1)S(1)}, u32[]{:S(2)}, u32[]{:S(2)}) collective-permute-start(bf16[1,1,1,1,24,3072]{5,4,3,2,1,0:T(8,128)(2,1)} %bitcast.73), channel_id=1, source_target_pairs={{0,16},{1,17},{2,18},{3,19},{4,20},{5,21},{6,22},{7,23},{8,24},{9,... | collective-permute-start | bytes 442376 | tf_op jit(solution)/shard_map/ppermute | solution.py:742
  16.3 9.9 %collective-permute-start.2 = (bf16[1,1,1,1,24,3072]{5,4,3,2,1,0:T(8,128)(2,1)}, bf16[1,1,1,1,24,3072]{5,4,3,2,1,0:T(8,128)(2,1)S(1)}, u32[]{:S(2)}, u32[]{:S(2)}) collective-permute-start(bf16[1,1,1,1,24,3072]{5,4,3,2,1,0:T(8,128)(2,1)} %bitcast.74), channel_id=1, source_target_pairs={{0,24},{1,25},{2,26},{3,27},{4,28},{5,29},{6,30},{7,31},{8,0},{9,1... | collective-permute-start | bytes 442376 | tf_op jit(solution)/shard_map/ppermute | solution.py:742
  26.3 8.9 %collective-permute-start.3 = (bf16[4,1,1,1,24,1536]{5,4,3,2,1,0:T(8,128)(2,1)S(1)}, bf16[4,1,1,1,24,1536]{5,4,3,2,1,0:T(8,128)(2,1)S(1)}, u32[]{:S(2)}, u32[]{:S(2)}) collective-permute-start(bf16[4,1,1,1,24,1536]{5,4,3,2,1,0:T(8,128)(2,1)S(1)} %get-tuple-element.256), channel_id=1, source_target_pairs={{0,2},{1,3},{2,0},{3,1},{4,6},{5,7},{6,4},{7,5},{8,10},{9,11},{10,... | collective-permute-start | bytes 884744 | tf_op jit(solution)/shard_map/ppermute | solution.py:742
  37.4 22.5 %collective-permute-start.6 = (bf16[4,2,1,1,24,1536]{5,4,3,2,1,0:T(8,128)(2,1)S(1)}, bf16[4,2,1,1,24,1536]{5,4,3,2,1,0:T(8,128)(2,1)S(1)}, u32[]{:S(2)}, u32[]{:S(2)}) collective-permute-start(bf16[4,2,1,1,24,1536]{5,4,3,2,1,0:T(8,128)(2,1)S(1)} %pad_maximum_fusion.6), channel_id=1, source_target_pairs={{0,2},{1,3},{2,0},{3,1},{4,6},{5,7},{6,4},{7,5},{8,10},{9,11},{10,... | collective-permute-start | bytes 1769480 | tf_op jit(solution)/shard_map/ppermute | solution.py:742
  41.2 18.8 %collective-permute-start.5 = (bf16[4,1,2,1,24,1536]{5,4,3,2,1,0:T(8,128)(2,1)S(1)}, bf16[4,1,2,1,24,1536]{5,4,3,2,1,0:T(8,128)(2,1)}, u32[]{:S(2)}, u32[]{:S(2)}) collective-permute-start(bf16[4,1,2,1,24,1536]{5,4,3,2,1,0:T(8,128)(2,1)S(1)} %pad_maximum_fusion.5), channel_id=1, source_target_pairs={{0,4},{1,5},{2,6},{3,7},{4,0},{5,1},{6,2},{7,3},{8,12},{9,13},{10,... | collective-permute-start | bytes 1769480 | tf_op jit(solution)/shard_map/ppermute | solution.py:742
  144.9 28.4 %collective-permute-start.11 = (bf16[2,4,96,768]{3,2,1,0:T(8,128)(2,1)}, bf16[2,4,96,768]{3,2,1,0:T(8,128)(2,1)}, u32[]{:S(2)}, u32[]{:S(2)}) collective-permute-start(bf16[2,4,96,768]{3,2,1,0:T(8,128)(2,1)} %get-tuple-element.185), channel_id=1, source_target_pairs={{0,4},{1,5},{2,6},{3,7},{4,0},{5,1},{6,2},{7,3},{8,12},{9,13},{10,... | collective-permute-start | bytes 3538952 | tf_op jit(solution)/shard_map/ppermute | solution.py:742
  146.4 28.2 %collective-permute-start.12 = (bf16[4,2,96,768]{3,2,1,0:T(8,128)(2,1)}, bf16[4,2,96,768]{3,2,1,0:T(8,128)(2,1)}, u32[]{:S(2)}, u32[]{:S(2)}) collective-permute-start(bf16[4,2,96,768]{3,2,1,0:T(8,128)(2,1)} %get-tuple-element.186), channel_id=1, source_target_pairs={{0,2},{1,3},{2,0},{3,1},{4,6},{5,7},{6,4},{7,5},{8,10},{9,11},{10,... | collective-permute-start | bytes 3538952 | tf_op jit(solution)/shard_map/ppermute | solution.py:742
  174.5 10.5 %collective-permute-start.15 = (bf16[384,2304]{1,0:T(8,128)(2,1)}, bf16[384,2304]{1,0:T(8,128)(2,1)}, u32[]{:S(2)}, u32[]{:S(2)}) collective-permute-start(bf16[384,2304]{1,0:T(8,128)(2,1)} %get-tuple-element.193), channel_id=1, source_target_pairs={{0,1},{1,0},{2,3},{3,2},{4,5},{5,4},{6,7},{7,6},{8,9},{9,8},{10,11... | collective-permute-start | bytes 5308424 | tf_op jit(solution)/shard_map/ppermute | solution.py:742
  175.1 8.9 %collective-permute-start.16 = (bf16[384,768]{1,0:T(8,128)(2,1)}, bf16[384,768]{1,0:T(8,128)(2,1)}, u32[]{:S(2)}, u32[]{:S(2)}) collective-permute-start(bf16[384,768]{1,0:T(8,128)(2,1)} %get-tuple-element.195), channel_id=1, source_target_pairs={{0,1},{1,0},{2,3},{3,2},{4,5},{5,4},{6,7},{7,6},{8,9},{9,8},{10,11... | collective-permute-start | bytes 1769480 | tf_op jit(solution)/shard_map/ppermute | solution.py:742
  178.9 16.1 %collective-permute-start.13 = (bf16[4,96,768]{2,1,0:T(8,128)(2,1)}, bf16[4,96,768]{2,1,0:T(8,128)(2,1)}, u32[]{:S(2)}, u32[]{:S(2)}) collective-permute-start(bf16[4,96,768]{2,1,0:T(8,128)(2,1)} %get-tuple-element.189), channel_id=1, source_target_pairs={{0,2},{1,3},{2,0},{3,1},{4,6},{5,7},{6,4},{7,5},{8,10},{9,11},{10,... | collective-permute-start | bytes 1769480 | tf_op jit(solution)/shard_map/ppermute | solution.py:742
  179.5 15.8 %collective-permute-start.14 = (bf16[4,96,768]{2,1,0:T(8,128)(2,1)}, bf16[4,96,768]{2,1,0:T(8,128)(2,1)}, u32[]{:S(2)}, u32[]{:S(2)}) collective-permute-start(bf16[4,96,768]{2,1,0:T(8,128)(2,1)} %get-tuple-element.190), channel_id=1, source_target_pairs={{0,4},{1,5},{2,6},{3,7},{4,0},{5,1},{6,2},{7,3},{8,12},{9,13},{10,... | collective-permute-start | bytes 1769480 | tf_op jit(solution)/shard_map/ppermute | solution.py:742
  182.5 8.9 %collective-permute-start.18 = (bf16[8,3072]{1,0:T(8,128)(2,1)}, bf16[8,3072]{1,0:T(8,128)(2,1)}, u32[]{:S(2)}, u32[]{:S(2)}) collective-permute-start(bf16[8,3072]{1,0:T(8,128)(2,1)} %get-tuple-element.239), channel_id=1, source_target_pairs={{0,8},{1,9},{2,10},{3,11},{4,12},{5,13},{6,14},{7,15},{8,16},{9,17... | collective-permute-start | bytes 147464 | tf_op jit(solution)/shard_map/ppermute | solution.py:742
  195.3 16.6 %collective-permute-start.21 = (bf16[4,24,3072]{2,1,0:T(8,128)(2,1)}, bf16[4,24,3072]{2,1,0:T(8,128)(2,1)}, u32[]{:S(2)}, u32[]{:S(2)}) collective-permute-start(bf16[4,24,3072]{2,1,0:T(8,128)(2,1)} %get-tuple-element.200), channel_id=1, source_target_pairs={{0,2},{1,3},{2,0},{3,1},{4,6},{5,7},{6,4},{7,5},{8,10},{9,11},{10,... | collective-permute-start | bytes 1769480 | tf_op jit(solution)/shard_map/ppermute | solution.py:742
  196.7 27.4 %collective-permute-start.22 = (bf16[4,24,3072]{2,1,0:T(8,128)(2,1)}, bf16[4,24,3072]{2,1,0:T(8,128)(2,1)}, u32[]{:S(2)}, u32[]{:S(2)}) collective-permute-start(bf16[4,24,3072]{2,1,0:T(8,128)(2,1)} %get-tuple-element.201), channel_id=1, source_target_pairs={{0,4},{1,5},{2,6},{3,7},{4,0},{5,1},{6,2},{7,3},{8,12},{9,13},{10,... | collective-permute-start | bytes 1769480 | tf_op jit(solution)/shard_map/ppermute | solution.py:742
  197.3 27.6 %collective-permute-start.23 = (bf16[4,24,3072]{2,1,0:T(8,128)(2,1)}, bf16[4,24,3072]{2,1,0:T(8,128)(2,1)}, u32[]{:S(2)}, u32[]{:S(2)}) collective-permute-start(bf16[4,24,3072]{2,1,0:T(8,128)(2,1)} %get-tuple-element.202), channel_id=1, source_target_pairs={{0,6},{1,7},{2,4},{3,5},{4,2},{5,3},{6,0},{7,1},{8,14},{9,15},{10,... | collective-permute-start | bytes 1769480 | tf_op jit(solution)/shard_map/ppermute | solution.py:742
  204.3 26.3 %collective-permute-start.27 = (bf16[2,96,768]{2,1,0:T(8,128)(2,1)}, bf16[2,96,768]{2,1,0:T(8,128)(2,1)}, u32[]{:S(2)}, u32[]{:S(2)}) collective-permute-start(bf16[2,96,768]{2,1,0:T(8,128)(2,1)} %get-tuple-element.214), channel_id=1, source_target_pairs={{0,8},{1,9},{2,10},{3,11},{4,12},{5,13},{6,14},{7,15},{8,16},{9,17... | collective-permute-start | bytes 884744 | tf_op jit(solution)/shard_map/ppermute | solution.py:742
  205.8 27.2 %collective-permute-start.28 = (bf16[2,96,768]{2,1,0:T(8,128)(2,1)}, bf16[2,96,768]{2,1,0:T(8,128)(2,1)}, u32[]{:S(2)}, u32[]{:S(2)}) collective-permute-start(bf16[2,96,768]{2,1,0:T(8,128)(2,1)} %get-tuple-element.215), channel_id=1, source_target_pairs={{0,16},{1,17},{2,18},{3,19},{4,20},{5,21},{6,22},{7,23},{8,24},{9,... | collective-permute-start | bytes 884744 | tf_op jit(solution)/shard_map/ppermute | solution.py:742
  211.9 21.1 %collective-permute-start.29 = (bf16[2,96,768]{2,1,0:T(8,128)(2,1)}, bf16[2,96,768]{2,1,0:T(8,128)(2,1)}, u32[]{:S(2)}, u32[]{:S(2)}) collective-permute-start(bf16[2,96,768]{2,1,0:T(8,128)(2,1)} %get-tuple-element.216), channel_id=1, source_target_pairs={{0,24},{1,25},{2,26},{3,27},{4,28},{5,29},{6,30},{7,31},{8,0},{9,1... | collective-permute-start | bytes 884744 | tf_op jit(solution)/shard_map/ppermute | solution.py:742
  213.8 22.4 %all-to-all-start = ((bf16[4,8,3072]{2,1,0:T(8,128)(2,1)}), bf16[4,8,3072]{2,1,0:T(8,128)(2,1)}, u32[]{:S(2)}, u32[]{:S(2)}) async-start(bf16[4,8,3072]{2,1,0:T(8,128)(2,1)} %broadcast_in_dim.38), calls=%async_computation | async-start | bytes 393216 | tf_op jit(solution)/shard_map/all_to_all | solution.py:760
  228.1 10.8 %collective-permute-start.24 = (bf16[24,3072]{1,0:T(8,128)(2,1)}, bf16[24,3072]{1,0:T(8,128)(2,1)}, u32[]{:S(2)}, u32[]{:S(2)}) collective-permute-start(bf16[24,3072]{1,0:T(8,128)(2,1)} %get-tuple-element.223), channel_id=1, source_target_pairs={{0,8},{1,9},{2,10},{3,11},{4,12},{5,13},{6,14},{7,15},{8,16},{9,17... | collective-permute-start | bytes 442376 | tf_op jit(solution)/shard_map/ppermute | solution.py:742
  229.6 12.9 %collective-permute-start.25 = (bf16[24,3072]{1,0:T(8,128)(2,1)}, bf16[24,3072]{1,0:T(8,128)(2,1)}, u32[]{:S(2)}, u32[]{:S(2)}) collective-permute-start(bf16[24,3072]{1,0:T(8,128)(2,1)} %get-tuple-element.224), channel_id=1, source_target_pairs={{0,16},{1,17},{2,18},{3,19},{4,20},{5,21},{6,22},{7,23},{8,24},{9,... | collective-permute-start | bytes 442376 | tf_op jit(solution)/shard_map/ppermute | solution.py:742
  230.6 11.9 %collective-permute-start.26 = (bf16[24,3072]{1,0:T(8,128)(2,1)}, bf16[24,3072]{1,0:T(8,128)(2,1)}, u32[]{:S(2)}, u32[]{:S(2)}) collective-permute-start(bf16[24,3072]{1,0:T(8,128)(2,1)} %get-tuple-element.225), channel_id=1, source_target_pairs={{0,24},{1,25},{2,26},{3,27},{4,28},{5,29},{6,30},{7,31},{8,0},{9,1... | collective-permute-start | bytes 442376 | tf_op jit(solution)/shard_map/ppermute | solution.py:742
  (25 other events, 151.5 us)
Sparse Core Ops, SparseCore 0:
  11.5 92.4 all-gather.2
